TPU v7x, 32 devices: a whole 2x2x4 slice. The times are simulated.
32 devices in a mesh: boot: 4 (over z), tm: 8 (over y, x, core).
Axes of the slice: x: 2, y: 2, z: 4, core: 2. Of those that a mesh axis runs over, the one named last changes fastest.
Arguments:
- recording: bfloat16 [4096, 1024], P('tm'), may hold values from -60 to 60, as said below
- starts: int32 [4, 48], P('boot', 'tm'), may hold values from 0 to 448, as said below
- lengths: int32 [4, 48], P('boot', 'tm'), may hold values from 1 to 64, as said below
- support: int32 [4, 4096], P(None, 'boot'), may hold values 0 or 1
Outputs:
- averaged: float32 [32, 4096], P(None, 'boot')
- residual: float32 [32, 4096], P(None, 'tm')
Inputs may be any that keep to these rules, and one draw needn't show every extreme that they name: A shard's values are an autoregressive recording; its values stay within the range. Entry [b, j * 6 + k] starts block k of resample b on time shard j, counted from the shard's first sample; a block ends inside its shard. The 6 lengths of one resample on one time shard sum to at most 384.
All inputs are finite; a program needn't handle non-finite values. No bound on the sum of `support` on one device may be relied on, other than what follows from the above.
Results may differ from a plain program's by a relative error of at most 0.0043.
The roundings to bfloat16 on the way count: a program that leaves them out, or rounds other values in their place, can miss the bound.
Values may be sent and summed in bfloat16 or wider, within the bound.
No kernel may reach another device: no remote copies, remote signals or barrier semaphores. Data moves between devices by JAX's collectives and lax.ppermute only.
A program may use at most 64 MiB of HBM per device.

v0:
```python
import functools

import jax
import jax.numpy as jnp
from jax import lax
from jax.experimental import pallas as pl
from jax.experimental.pallas import tpu as pltpu
from jax.sharding import PartitionSpec as P


LAGS = 4
RESPONSE_COUNT = 32
NBLK = 6
CAP = 384
ITERS = 3
CHEB = 5

ridge_weight = 4.0
shrink_level = 0.75
epsilon = 1e-05

MARGIN = 128
HALO = 16
CHUNKS = 4


VMEM = pl.BlockSpec(memory_space=pltpu.VMEM)
HBM = pl.BlockSpec(memory_space=pltpu.HBM)
f32 = jnp.float32
bf16 = jnp.bfloat16


def swapped(block, axis, distance):
    devices = range(lax.axis_size(axis))
    return lax.ppermute(block, axis, [(i, i ^ distance) for i in devices])


def paired_sum(parts):
    while len(parts) > 1:
        parts = [parts[i] + parts[i + 1] for i in range(0, len(parts), 2)]
    return parts[0]


def chip_parts(block, step=2):
    reach = min(4, lax.axis_size("tm") // step)
    return [block] + [swapped(block, "tm", k * step) for k in range(1, reach)]


def chip_parts_sum(block):
    step = 2
    while step < lax.axis_size("tm"):
        parts = chip_parts(block, step)
        total = paired_sum([part.astype(f32) for part in parts])
        block = total.astype(block.dtype)
        step *= len(parts)
    return total


def rotated(values, shift, axis):
    return pltpu.roll(values, shift, axis)


def nt_dot(a, b):
    return lax.dot_general(a, b, (((1,), (1,)), ((), ())), preferred_element_type=f32)


def nn_dot(a, b):
    return jnp.dot(a, b, preferred_element_type=f32)


def split(values):
    high = values.astype(bf16)
    low = (values - high.astype(f32)).astype(bf16)
    return high, low


def gathered_lags(products, samples):
    rows = products.shape[0] // LAGS
    total = None
    for lag in range(LAGS):
        part = rotated(products[lag * rows : (lag + 1) * rows], 1 + lag, 1)
        total = part if total is None else total + part
    return total[:, :samples]


def spread_times_window(values, window):
    width = window.shape[0]
    lagged = jnp.concatenate(
        [rotated(values, width - 1 - lag, 1) for lag in range(LAGS)], axis=0
    )
    high, low = split(lagged)
    both = nn_dot(jnp.concatenate([high, low], axis=0), window)
    return both[: lagged.shape[0]] + both[lagged.shape[0] :]


def padded(values, width):
    rows, samples = values.shape
    return jnp.concatenate([values, jnp.zeros((rows, width - samples), f32)], axis=1)


def chebyshev(high, low, rhs, bound):
    center = ridge_weight + 0.5 * bound
    radius = 0.5 * bound
    sigma = center / radius
    answer = jnp.zeros_like(rhs)
    remain = rhs
    factor = 1.0 / sigma
    update = rhs / center
    for count in range(CHEB):
        answer = answer + update
        if count + 1 < CHEB:
            product = times_matrix(update, high, low)
            remain = remain - (ridge_weight * update + product)
            after = 1.0 / (2.0 * sigma - factor)
            update = after * factor * update + 2.0 * after / radius * remain
            factor = after
    return answer


def times_matrix(values, high, low):
    rows = values.shape[0]
    first, second = split(values)
    both = nn_dot(jnp.concatenate([first, second], axis=0), high)
    return both[:rows] + (both[rows:] + nn_dot(first, low))


def solving_matrix(weighted, bound):
    center = ridge_weight + 0.5 * bound
    radius = 0.5 * bound
    sigma = center / radius
    factors = [1.0 / sigma]
    for _ in range(CHEB - 1):
        factors.append(1.0 / (2.0 * sigma - factors[-1]))
    ratios = [None] * CHEB + [1.0]
    for k in reversed(range(CHEB)):
        ratios[k] = factors[k] * ratios[k + 1]
    g0, g1, g2, g3, g4, _ = ratios
    b4 = 2.0 * g0 / radius
    b3 = 4.0 * g1 / radius
    b2 = (4.0 * g2 + 2.0 * g0) / radius
    b1 = (4.0 * g3 + 4.0 * g1) / radius
    b0 = (2.0 * g4 + 2.0 * g2 + g0) / radius
    row = lax.broadcasted_iota(jnp.int32, weighted.shape, 0)
    column = lax.broadcasted_iota(jnp.int32, weighted.shape, 1)
    unit = jnp.where(row == column, 1.0, 0.0)
    t1 = unit - weighted * (1.0 / radius)
    high, low = split(t1)
    t2 = 2.0 * (nn_dot(high, high) + (nn_dot(low, high) + nn_dot(high, low))) - unit
    high, low = split(t2)
    first, second = split(b3 * t1 + b4 * t2)
    product = nn_dot(first, high) + (nn_dot(second, high) + nn_dot(first, low))
    return (b0 - b4) * unit + (b1 - b3) * t1 + b2 * t2 + 2.0 * product


def store_halves(core, values, state_ref, send_ref, keep_ref):
    state_ref[...] = values
    half = values.shape[0] // 2
    keep_ref[...] = state_ref[pl.ds(pl.multiple_of(core * half, half), half), :]
    send_ref[...] = state_ref[pl.ds(pl.multiple_of((1 - core) * half, half), half), :]


def uses_along(iota, starts_ref, lengths_ref):
    total = jnp.zeros(iota.shape, f32)
    for block in range(NBLK):
        begin = starts_ref[0, block]
        inside = (iota >= begin) & (iota < begin + lengths_ref[0, block])
        total = total + jnp.where(inside, 1.0, 0.0)
    return total


def place():
    index = lax.axis_index("tm")
    return lax.rem(index, 2), lax.div(index, 2), lax.axis_index("boot")


def power_kernel(
    starts_hbm,
    lengths_hbm,
    source_ref,
    recording_ref,
    packet_ref,
    along_ref,
    down_ref,
    starts_ref,
    lengths_ref,
    sems,
):
    samples, channels = source_ref.shape
    chunk = samples // CHUNKS
    plan = [
        pltpu.make_async_copy(starts_hbm, starts_ref, sems.at[CHUNKS]),
        pltpu.make_async_copy(lengths_hbm, lengths_ref, sems.at[CHUNKS + 1]),
    ]
    for copy in plan:
        copy.start()
    copies = []
    for k in range(CHUNKS):
        piece = pl.ds(k * chunk, chunk)
        copies.append(
            pltpu.make_async_copy(source_ref.at[piece], recording_ref.at[piece], sems.at[k])
        )
        copies[-1].start()
    for copy in plan:
        copy.wait()
    along_ref[...] = uses_along(
        lax.broadcasted_iota(jnp.int32, along_ref.shape, 1), starts_ref, lengths_ref
    )
    down_ref[...] = uses_along(
        lax.broadcasted_iota(jnp.int32, down_ref.shape, 0), starts_ref, lengths_ref
    )
    total = jnp.zeros((8, channels), f32)
    for k in range(CHUNKS):
        copies[k].wait()
        values = recording_ref[k * chunk : (k + 1) * chunk, :].astype(f32)
        total = total + jnp.sum((values * values).reshape(chunk // 8, 8, channels), axis=0)
    power = jnp.sum(total, axis=0, keepdims=True)
    last = recording_ref[samples - HALO :, :].astype(f32)[HALO - 8 :]
    row = lax.broadcasted_iota(jnp.int32, (8, channels), 0)
    packet_ref[...] = jnp.where(row < 8 - LAGS, power, last)


def merge_kernel(own_ref, other_ref, merged_ref):
    core, _, _ = place()
    own, other = own_ref[...], other_ref[...]
    row = lax.broadcasted_iota(jnp.int32, own.shape, 0)
    merged_ref[...] = jnp.where(row < 8 - LAGS, own + other, jnp.where(core == 1, own, other))


def preceding_rows(refs):
    if len(refs) == 1:
        return refs[0][...]
    core, chip, _ = place()
    other_ref, *chip_refs = refs
    rows = chip_refs[0][...]
    if len(chip_refs) == 3:
        rows = jnp.where(chip == 2, chip_refs[2][...], rows)
    rows = jnp.where(core == 1, other_ref[...], rows)
    return jnp.where(core + chip > 0, rows, 0.0)


def first_kernel(count, parts, halos, *refs):
    part_refs, refs = refs[:parts], refs[parts:]
    halo_refs, refs = refs[:halos], refs[halos:]
    (
        recording_ref,
        along_ref,
        down_ref,
        window_ref,
        high_ref,
        low_ref,
        bound_ref,
        answer_ref,
        state_ref,
        send_ref,
        keep_ref,
    ) = refs
    samples, channels = recording_ref.shape
    width = window_ref.shape[0]
    power = paired_sum([ref[:1, :] for ref in part_refs])
    scale = 1.0 / jnp.sqrt(power / count + epsilon)
    window_ref[:samples, :] = (recording_ref[...].astype(f32) * scale).astype(bf16)
    window_ref[samples : width - HALO, :] = jnp.zeros((width - HALO - samples, channels), bf16)
    row = lax.broadcasted_iota(jnp.int32, (8, channels), 0)
    tail = jnp.where(row >= 8 - LAGS, preceding_rows(halo_refs) * scale, 0.0)
    window_ref[width - HALO :, :] = jnp.concatenate(
        [jnp.zeros((HALO - 8, channels), f32), tail], axis=0
    ).astype(bf16)
    window = window_ref[...]

    along = along_ref[...]
    pairs = nt_dot(window, window)
    pairs = pairs + rotated(rotated(pairs, 1, 0), 1, 1)
    pairs = pairs + rotated(rotated(pairs, 2, 0), 2, 1)
    gram = rotated(rotated(pairs, 1, 0)[:samples], 1, 1)[:, :samples] * (1.0 / CAP)
    weighted = gram * down_ref[:, :1]
    squares = jnp.sum(weighted * gram, axis=0, keepdims=True) * along[:, :samples]
    bound = jnp.sqrt(jnp.sum(squares, axis=1, keepdims=True))
    bound_ref[...] = jnp.broadcast_to(bound, bound_ref.shape)
    high, low = split(weighted)
    high_ref[...] = high
    low_ref[...] = low

    answer = window_ref[:samples, :128].astype(f32).T[:RESPONSE_COUNT]
    answer_ref[...] = answer
    short = answer.astype(bf16)
    projected = (nn_dot(short, high) + nn_dot(short, low)) * (1.0 / CAP)
    weights = chebyshev(high, low, projected, bound).astype(bf16).astype(f32)
    kept = padded(answer * (1.0 / CAP) - weights, width) * along
    local = spread_times_window(kept, window) / ridge_weight
    core, _, _ = place()
    store_halves(core, local, state_ref, send_ref, keep_ref)


def side_kernel(
    window_ref, high_ref, low_ref, bound_ref, answer_ref, along_ref, cross_ref, first_ref, second_ref
):
    width = window_ref.shape[0]
    weighted = high_ref[...].astype(f32) + low_ref[...].astype(f32)
    first_ref[...], second_ref[...] = split(solving_matrix(weighted, bound_ref[:1, :1]))
    answer = padded(answer_ref[...], width) * along_ref[...]
    cross_ref[...] = spread_times_window(answer, window_ref[...]) * (1.0 / CAP)


def column_norms(mean):
    parts = mean.shape[0] // RESPONSE_COUNT
    cube = mean.reshape(parts, RESPONSE_COUNT, mean.shape[1])
    return cube, jnp.sqrt(jnp.sum(cube * cube, axis=1))


def shrunk(cube, norms, level):
    return cube * (jnp.maximum(norms - level, 0.0) / jnp.maximum(norms, level))[:, None, :]


def join_halves(core, own_ref, other_ref, full_ref):
    half = own_ref.shape[0]
    full_ref[pl.ds(pl.multiple_of(core * half, half), half), :] = own_ref[...]
    full_ref[pl.ds(pl.multiple_of((1 - core) * half, half), half), :] = other_ref[...]


def next_kernel(
    own_ref,
    other_ref,
    window_ref,
    first_ref,
    second_ref,
    cross_ref,
    along_ref,
    state_ref,
    later_ref,
    send_ref,
    keep_ref,
    mean_ref,
):
    core, _, _ = place()
    join_halves(core, own_ref, other_ref, mean_ref)
    cube, norms = column_norms(mean_ref[...])
    level = shrink_level * (jnp.sum(norms, keepdims=True) / norms.size)
    consensus = shrunk(cube, norms, level).reshape(mean_ref.shape)
    dual = state_ref[...] - consensus
    target = cross_ref[...] + ridge_weight * (consensus - dual)
    window = window_ref[...]
    samples = first_ref.shape[0]
    projected = gathered_lags(nt_dot(target.astype(bf16), window), samples) * (1.0 / CAP)
    weights = times_matrix(projected, first_ref[...], second_ref[...])
    kept = padded(weights.astype(bf16).astype(f32), window.shape[0]) * along_ref[...]
    local = (target - spread_times_window(kept, window)) / ridge_weight
    store_halves(core, local + dual, later_ref, send_ref, keep_ref)


def norm_kernel(shards, *refs):
    total_ref, *part_refs, mean_ref, sum_ref = refs
    change = paired_sum([ref[...].astype(f32) for ref in part_refs])
    mean = (total_ref[...] + change) / shards
    mean_ref[...] = mean
    _, norms = column_norms(mean)
    sum_ref[...] = jnp.broadcast_to(jnp.sum(norms, keepdims=True), sum_ref.shape)


def weigh_kernel(
    boots, mean_ref, own_ref, other_ref, support_ref, weighted_ref, tally_ref, blocks_ref
):
    core, chip, position = place()
    side = lax.rem(chip, 2)
    start = pl.multiple_of(side * RESPONSE_COUNT, RESPONSE_COUNT)
    cube, norms = column_norms(mean_ref[pl.ds(start, RESPONSE_COUNT), :])
    channels = cube.shape[2]
    level = shrink_level * ((own_ref[:1, :1] + other_ref[:1, :1]) / (LAGS * channels))
    for d in range(boots):
        blocks_ref[lax.bitwise_xor(position, d)] = support_ref[d * boots : (d + 1) * boots, :]
    each = channels // blocks_ref.shape[2]
    blocks = [blocks_ref.at[(core * 2 + side) * each + k] for k in range(each)]
    chosen = jnp.concatenate([b[pl.ds(position, 1), :] for b in blocks], axis=1)
    tally_ref[...] = jnp.concatenate(
        [jnp.sum(b[...], axis=0, keepdims=True) for b in blocks], axis=1
    )
    weighted = chosen[:, None, :] * shrunk(cube, norms, level)
    weighted_ref[...] = weighted.reshape(weighted_ref.shape).astype(bf16)


def average_kernel(*refs):
    *piece_refs, tally_ref, averaged_ref = refs
    added = paired_sum([ref[...].astype(f32) for ref in piece_refs])
    averaged_ref[...] = (added / jnp.maximum(tally_ref[...], 1.0)).astype(bf16)


def last_kernel(*refs):
    *lag_refs, window_ref, answer_ref, averaged_ref, residual_ref, full_ref = refs
    core, chip, position = place()
    mine = core * 2 + lax.rem(chip, 2)
    for step, ref in enumerate(lag_refs):
        lag = lax.bitwise_xor(mine, (step % 2) * 2 + step // 2)
        full_ref[pl.ds(pl.multiple_of(lag * RESPONSE_COUNT, RESPONSE_COUNT), RESPONSE_COUNT), :] = (
            ref[...]
        )
    samples = residual_ref.shape[1]
    forecast = gathered_lags(nt_dot(full_ref[...], window_ref[...]), samples)
    residual_ref[...] = answer_ref[...] - forecast
    channels = full_ref.shape[1]
    width = averaged_ref.shape[1]
    opening = position * width
    row = pl.multiple_of(lax.div(opening, channels) * RESPONSE_COUNT, RESPONSE_COUNT)
    if width == channels:
        block = full_ref[pl.ds(row, RESPONSE_COUNT), :]
    else:
        column = pl.multiple_of(lax.rem(opening, channels), width)
        block = full_ref[pl.ds(row, RESPONSE_COUNT), pl.ds(column, width)]
    averaged_ref[...] = block.astype(f32)


def shaped(shape, dtype=f32):
    return jax.ShapeDtypeStruct(shape, dtype)


def called(kernel, outs, ins, scratch=(), cost=None, room=32):
    return pl.pallas_call(
        kernel,
        cost_estimate=cost,
        out_shape=outs,
        in_specs=ins,
        out_specs=jax.tree.map(lambda _: VMEM, outs),
        scratch_shapes=scratch,
        compiler_params=pltpu.CompilerParams(vmem_limit_bytes=room * 1024 * 1024),
    )


def per_device(recording, starts, lengths, support):
    shards = lax.axis_size("tm")
    boots = lax.axis_size("boot")
    samples, channels = recording.shape
    width = samples + MARGIN
    rows = LAGS * RESPONSE_COUNT
    half = rows // 2
    half_shape = shaped((half, channels))
    full_shape = shaped((rows, channels))

    recording, packet, along, down = called(
        power_kernel,
        (
            shaped((samples, channels), bf16),
            shaped((8, channels)),
            shaped((1, width)),
            shaped((samples, 128)),
        ),
        [HBM] * 3,
        [
            pltpu.SMEM(starts.shape, jnp.int32),
            pltpu.SMEM(lengths.shape, jnp.int32),
            pltpu.SemaphoreType.DMA((CHUNKS + 2,)),
        ],
        room=32,
    )(*[pltpu.with_memory_space_constraint(a, pltpu.HBM) for a in (starts, lengths, recording)])
    other = swapped(packet, "tm", 1)
    merged = called(merge_kernel, shaped((8, channels)), [VMEM, VMEM])(packet, other)
    if shards <= 8:
        powers = chip_parts(merged)
        halos = [other] + powers[1:]
    else:
        powers = [chip_parts_sum(merged)]
        halos = [lax.ppermute(packet, "tm", [(i, i + 1) for i in range(shards - 1)])]

    square = shaped((samples, samples), bf16)
    window, high, low, bound, answer, state, send, keep = called(
        functools.partial(first_kernel, samples * shards, len(powers), len(halos)),
        (
            shaped((width, channels), bf16),
            square,
            square,
            shaped((8, 128)),
            shaped((RESPONSE_COUNT, samples)),
            full_shape,
            half_shape,
            half_shape,
        ),
        [VMEM] * (len(powers) + len(halos) + 3),
    )(*powers, *halos, recording, along, down)

    total = jnp.zeros((half, channels), f32)
    held = total
    support = support.astype(f32)
    reach = 1
    for count in range(1, ITERS):
        change = (keep + swapped(send, "tm", 1) - held).astype(bf16)
        change, support, window, high = lax.optimization_barrier((change, support, window, high))
        total = total + chip_parts_sum(change)
        held = held + change.astype(f32)
        mean = total / shards
        while reach < boots:
            support = jnp.concatenate([support, swapped(support, "boot", reach)], axis=0)
            reach *= 2
            if count + 1 < ITERS:
                break
        if count == 1:
            cross, first, second = called(
                side_kernel,
                (full_shape, square, square),
                [VMEM] * 6,
                cost=pl.CostEstimate(
                    flops=14 * samples**3, bytes_accessed=1 << 20, transcendentals=0
                ),
            )(window, high, low, bound, answer, along)
        mean, support = lax.optimization_barrier((mean, support))
        state, send, keep = called(
            next_kernel,
            (full_shape, half_shape, half_shape),
            [VMEM] * 8,
            [pltpu.VMEM((rows, channels), f32)],
        )(mean, swapped(mean, "tm", 1), window, first, second, cross, along, state)

    change = (keep + swapped(send, "tm", 1) - held).astype(bf16)
    parts = chip_parts(change) if shards <= 8 else [chip_parts_sum(change)]
    mean, summed = called(
        functools.partial(norm_kernel, shards),
        (half_shape, shaped((8, 128))),
        [VMEM] * (1 + len(parts)),
    )(total, *parts)
    lag_shape = shaped((RESPONSE_COUNT, channels), bf16)
    weighted, tally = called(
        functools.partial(weigh_kernel, boots),
        (lag_shape, shaped((1, channels))),
        [VMEM] * 4,
        [pltpu.VMEM((boots, boots, support.shape[1]), f32)],
    )(mean, summed, swapped(summed, "tm", 1), support)
    pieces = [weighted] + [swapped(weighted, "boot", d) for d in range(1, boots)]
    averaged = called(average_kernel, lag_shape, [VMEM] * (boots + 1))(*pieces, tally)
    return called(
        last_kernel,
        (
            shaped((RESPONSE_COUNT, LAGS * channels // boots)),
            shaped((RESPONSE_COUNT, samples)),
        ),
        [VMEM] * 6,
        [pltpu.VMEM((rows, channels), bf16)],
    )(averaged, *[swapped(averaged, "tm", d) for d in range(1, 4)], window, answer)


def solution(mesh):
    in_specs = (P("tm", None), P("boot", "tm"), P("boot", "tm"), P(None, "boot"))
    out_specs = (P(None, "boot"), P(None, "tm"))
    return jax.shard_map(
        per_device,
        mesh=mesh,
        in_specs=in_specs,
        out_specs=out_specs,
        check_vma=False,
    )
```

profile of v0, /device:TPU:0, one launch (start us, length us, event | category | flops | bytes accessed | tf_op | source)
XLA Modules:
  0.0 78.9 jit_solution(10770359834708485564)
XLA Ops:
  0.6 1.3 %shard_map.59 = (bf16[512,1024]{1,0:T(8,128)(2,1)S(1)}, f32[8,1024]{1,0:T(8,128)S(1)}, f32[1,640]{1,0:T(1,128)S(1)}, f32[512,128]{1,0:T(8,128)S(1)}) custom-call(s32[1,6]{1,0:T(1,128)} %starts_hbm.1, s32[1,6]{1,0:T(1,128)} %lengths_hbm.1, bf16[512,1024]{1,0:T(8,128)(2,1)} %source_ref.1), custom_call_target="tpu_custom_call" | custom-call | tf_op jit(solution)/shard_map/pallas_call | solution.py:436
  3.3 3.8 %collective-permute-start.3 = (f32[8,1024]{1,0:T(8,128)S(1)}, f32[8,1024]{1,0:T(8,128)S(1)}, u32[]{:S(2)}, u32[]{:S(2)}) collective-permute-start(f32[8,1024]{1,0:T(8,128)S(1)} %shard_map.60.refs_0_), channel_id=1, source_target_pairs={{0,6},{1,7},{2,4},{3,5},{4,2},{5,3},{6,0},{7,1},{8,14},{9,15},{10,... | collective-permute-start | bytes 98312 | tf_op jit(solution)/shard_map/ppermute | solution.py:35
  7.8 1.3 %collective-permute-done.3.refs_3_.refs_7_ = f32[8,1024]{1,0:T(8,128)S(1)} collective-permute-done((f32[8,1024]{1,0:T(8,128)S(1)}, f32[8,1024]{1,0:T(8,128)S(1)}, u32[]{:S(2)}, u32[]{:S(2)}) %collective-permute-start.3) | collective-permute-done | bytes 32800 | tf_op jit(solution)/shard_map/ppermute | solution.py:35
  9.1 2.0 %collective-permute-done.2.refs_2_.refs_6_ = f32[8,1024]{1,0:T(8,128)S(1)} collective-permute-done((f32[8,1024]{1,0:T(8,128)S(1)}, f32[8,1024]{1,0:T(8,128)S(1)}, u32[]{:S(2)}, u32[]{:S(2)}) %collective-permute-start.2) | collective-permute-done | bytes 32800 | tf_op jit(solution)/shard_map/ppermute | solution.py:35
  11.6 4.5 %shard_map.61 = (bf16[640,1024]{1,0:T(8,128)(2,1)S(1)}, bf16[512,512]{1,0:T(8,128)(2,1)S(1)}, bf16[512,512]{1,0:T(8,128)(2,1)S(1)}, f32[8,128]{1,0:T(8,128)S(1)}...) custom-call(f32[8,1024]{1,0:T(8,128)S(1)} %shard_map.60.refs_0_, ...), custom_call_target="tpu_custom_call" | custom-call | tf_op jit(solution)/shard_map/pallas_call | solution.py:462
  16.2 1.5 %collective-permute-done.4 = f32[64,1024]{1,0:T(8,128)S(1)} collective-permute-done((f32[64,1024]{1,0:T(8,128)S(1)}, f32[64,1024]{1,0:T(8,128)S(1)}, u32[]{:S(2)}, u32[]{:S(2)}) %collective-permute-start.4) | collective-permute-done | bytes 262176 | tf_op jit(solution)/shard_map/ppermute | solution.py:35
  17.8 1.6 %collective-permute-start.7 = (bf16[64,1024]{1,0:T(8,128)(2,1)S(1)}, bf16[64,1024]{1,0:T(8,128)(2,1)S(1)}, u32[]{:S(2)}, u32[]{:S(2)}) collective-permute-start(bf16[64,1024]{1,0:T(8,128)(2,1)S(1)} %add_convert_fusion), channel_id=1, source_target_pairs={{0,6},{1,7},{2,4},{3,5},{4,2},{5,3},{6,0},{7,1},{8,14},{9,15},{10,... | collective-permute-start | bytes 393224 | tf_op jit(solution)/shard_map/ppermute | solution.py:35
  19.4 1.9 %collective-permute-start.5 = (bf16[64,1024]{1,0:T(8,128)(2,1)S(1)}, bf16[64,1024]{1,0:T(8,128)(2,1)S(1)}, u32[]{:S(2)}, u32[]{:S(2)}) collective-permute-start(bf16[64,1024]{1,0:T(8,128)(2,1)S(1)} %add_convert_fusion), channel_id=1, source_target_pairs={{0,2},{1,3},{2,0},{3,1},{4,6},{5,7},{6,4},{7,5},{8,10},{9,11},{10,... | collective-permute-start | bytes 393224 | tf_op jit(solution)/shard_map/ppermute | solution.py:35
  21.3 1.6 %collective-permute-start.8 = (f32[4,1024]{1,0:T(4,128)S(1)}, f32[4,1024]{1,0:T(4,128)S(1)}, u32[]{:S(2)}, u32[]{:S(2)}) collective-permute-start(f32[4,1024]{1,0:T(4,128)S(1)} %convert_element_type.39), channel_id=1, source_target_pairs={{0,8},{8,0},{16,24},{24,16},{1,9},{9,1},{17,25},{25,17},{2,10},{10... | collective-permute-start | bytes 49160 | tf_op jit(solution)/shard_map/ppermute | solution.py:35
  22.9 2.2 %collective-permute-done.8 = f32[4,1024]{1,0:T(4,128)S(1)} collective-permute-done((f32[4,1024]{1,0:T(4,128)S(1)}, f32[4,1024]{1,0:T(4,128)S(1)}, u32[]{:S(2)}, u32[]{:S(2)}) %collective-permute-start.8) | collective-permute-done | bytes 16416 | tf_op jit(solution)/shard_map/ppermute | solution.py:35
  25.1 2.0 %collective-permute-done.6 = bf16[64,1024]{1,0:T(8,128)(2,1)S(1)} collective-permute-done((bf16[64,1024]{1,0:T(8,128)(2,1)S(1)}, bf16[64,1024]{1,0:T(8,128)(2,1)S(1)}, u32[]{:S(2)}, u32[]{:S(2)}) %collective-permute-start.6) | collective-permute-done | bytes 131104 | tf_op jit(solution)/shard_map/ppermute | solution.py:35
  27.3 2.8 %shard_map.62 = (f32[128,1024]{1,0:T(8,128)S(1)}, bf16[512,512]{1,0:T(8,128)(2,1)S(1)}, bf16[512,512]{1,0:T(8,128)(2,1)S(1)}) custom-call(bf16[640,1024]{1,0:T(8,128)(2,1)S(1)} %get-tuple-element.63.window_ref.refs_4_, bf16[512,512]{1,0:T(8,128)(2,1)S(1)} %get-tuple-element.49.high_ref, bf16[512,512]{1,0:T(8,128)(2,1)S(1)} %get-tuple-element.50.low_ref, ...), custom_call_target="tpu_custom_call" | custom-call | flops 1879048192 | bytes 1048576 | tf_op jit(solution)/shard_map/pallas_call | solution.py:493
  30.1 2.0 %shard_map.63 = (f32[128,1024]{1,0:T(8,128)S(1)}, f32[64,1024]{1,0:T(8,128)S(1)}, f32[64,1024]{1,0:T(8,128)S(1)}) custom-call(f32[64,1024]{1,0:T(8,128)S(1)} %broadcast_multiply_fusion.1.own_ref, f32[64,1024]{1,0:T(8,128)S(1)} %collective-permute-done.9.other_ref, bf16[640,1024]{1,0:T(8,128)(2,1)S(1)} %get-tuple-element.63.window_ref.refs_4_, ...), custom_call_target="tpu_custom_call" | custom-call | tf_op jit(solution)/shard_map/pallas_call | solution.py:502
  33.9 2.7 %collective-permute-start.14 = (f32[8,1024]{1,0:T(8,128)S(1)}, f32[8,1024]{1,0:T(8,128)S(1)}, u32[]{:S(2)}, u32[]{:S(2)}) collective-permute-start(f32[8,1024]{1,0:T(8,128)S(1)} %pad_maximum_fusion.1), channel_id=1, source_target_pairs={{0,16},{8,24},{16,0},{24,8},{1,17},{9,25},{17,1},{25,9},{2,18},{10... | collective-permute-start | bytes 98312 | tf_op jit(solution)/shard_map/ppermute | solution.py:35
  36.6 1.4 %collective-permute-start.13 = (bf16[64,1024]{1,0:T(8,128)(2,1)S(1)}, bf16[64,1024]{1,0:T(8,128)(2,1)S(1)}, u32[]{:S(2)}, u32[]{:S(2)}) collective-permute-start(bf16[64,1024]{1,0:T(8,128)(2,1)S(1)} %fusion.3), channel_id=1, source_target_pairs={{0,6},{1,7},{2,4},{3,5},{4,2},{5,3},{6,0},{7,1},{8,14},{9,15},{10,... | collective-permute-start | bytes 393224 | tf_op jit(solution)/shard_map/ppermute | solution.py:35
  38.5 1.5 %collective-permute-start.11 = (bf16[64,1024]{1,0:T(8,128)(2,1)S(1)}, bf16[64,1024]{1,0:T(8,128)(2,1)S(1)}, u32[]{:S(2)}, u32[]{:S(2)}) collective-permute-start(bf16[64,1024]{1,0:T(8,128)(2,1)S(1)} %fusion.3), channel_id=1, source_target_pairs={{0,2},{1,3},{2,0},{3,1},{4,6},{5,7},{6,4},{7,5},{8,10},{9,11},{10,... | collective-permute-start | bytes 393224 | tf_op jit(solution)/shard_map/ppermute | solution.py:35
  40.1 3.8 %collective-permute-done.13 = bf16[64,1024]{1,0:T(8,128)(2,1)S(1)} collective-permute-done((bf16[64,1024]{1,0:T(8,128)(2,1)S(1)}, bf16[64,1024]{1,0:T(8,128)(2,1)S(1)}, u32[]{:S(2)}, u32[]{:S(2)}) %collective-permute-start.13) | collective-permute-done | bytes 131104 | tf_op jit(solution)/shard_map/ppermute | solution.py:35
  43.9 1.9 %collective-permute-done.12 = bf16[64,1024]{1,0:T(8,128)(2,1)S(1)} collective-permute-done((bf16[64,1024]{1,0:T(8,128)(2,1)S(1)}, bf16[64,1024]{1,0:T(8,128)(2,1)S(1)}, u32[]{:S(2)}, u32[]{:S(2)}) %collective-permute-start.12) | collective-permute-done | bytes 131104 | tf_op jit(solution)/shard_map/ppermute | solution.py:35
  46.0 1.5 %collective-permute-done.15.other_ref = f32[64,1024]{1,0:T(8,128)S(1)} collective-permute-done((f32[64,1024]{1,0:T(8,128)S(1)}, f32[64,1024]{1,0:T(8,128)S(1)}, u32[]{:S(2)}, u32[]{:S(2)}) %collective-permute-start.15) | collective-permute-done | bytes 262176 | tf_op jit(solution)/shard_map/ppermute | solution.py:35
  47.6 2.8 %shard_map.64 = (f32[128,1024]{1,0:T(8,128)}, f32[64,1024]{1,0:T(8,128)S(1)}, f32[64,1024]{1,0:T(8,128)S(1)}) custom-call(f32[64,1024]{1,0:T(8,128)S(1)} %get-tuple-element.62.own_ref, f32[64,1024]{1,0:T(8,128)S(1)} %collective-permute-done.15.other_ref, bf16[640,1024]{1,0:T(8,128)(2,1)S(1)} %get-tuple-element.63.window_ref.refs_4_, ...), custom_call_target="tpu_custom_call" | custom-call | tf_op jit(solution)/shard_map/pallas_call | solution.py:502
  50.5 1.4 %collective-permute-done.16 = f32[64,1024]{1,0:T(8,128)S(1)} collective-permute-done((f32[64,1024]{1,0:T(8,128)S(1)}, f32[64,1024]{1,0:T(8,128)S(1)}, u32[]{:S(2)}, u32[]{:S(2)}) %collective-permute-start.16) | collective-permute-done | bytes 262176 | tf_op jit(solution)/shard_map/ppermute | solution.py:35
  51.9 1.4 %collective-permute-start.19 = (bf16[64,1024]{1,0:T(8,128)(2,1)S(1)}, bf16[64,1024]{1,0:T(8,128)(2,1)S(1)}, u32[]{:S(2)}, u32[]{:S(2)}) collective-permute-start(bf16[64,1024]{1,0:T(8,128)(2,1)S(1)} %fusion.5.refs_1_), channel_id=1, source_target_pairs={{0,6},{1,7},{2,4},{3,5},{4,2},{5,3},{6,0},{7,1},{8,14},{9,15},{10,... | collective-permute-start | bytes 393224 | tf_op jit(solution)/shard_map/ppermute | solution.py:35
  54.0 1.5 %collective-permute-start.17 = (bf16[64,1024]{1,0:T(8,128)(2,1)S(1)}, bf16[64,1024]{1,0:T(8,128)(2,1)S(1)}, u32[]{:S(2)}, u32[]{:S(2)}) collective-permute-start(bf16[64,1024]{1,0:T(8,128)(2,1)S(1)} %fusion.5.refs_1_), channel_id=1, source_target_pairs={{0,2},{1,3},{2,0},{3,1},{4,6},{5,7},{6,4},{7,5},{8,10},{9,11},{10,... | collective-permute-start | bytes 393224 | tf_op jit(solution)/shard_map/ppermute | solution.py:35
  55.5 3.8 %collective-permute-done.19.refs_4_ = bf16[64,1024]{1,0:T(8,128)(2,1)S(1)} collective-permute-done((bf16[64,1024]{1,0:T(8,128)(2,1)S(1)}, bf16[64,1024]{1,0:T(8,128)(2,1)S(1)}, u32[]{:S(2)}, u32[]{:S(2)}) %collective-permute-start.19) | collective-permute-done | bytes 131104 | tf_op jit(solution)/shard_map/ppermute | solution.py:35
  59.3 2.0 %collective-permute-done.18.refs_3_ = bf16[64,1024]{1,0:T(8,128)(2,1)S(1)} collective-permute-done((bf16[64,1024]{1,0:T(8,128)(2,1)S(1)}, bf16[64,1024]{1,0:T(8,128)(2,1)S(1)}, u32[]{:S(2)}, u32[]{:S(2)}) %collective-permute-start.18) | collective-permute-done | bytes 131104 | tf_op jit(solution)/shard_map/ppermute | solution.py:35
  62.9 1.4 %collective-permute-start.23 = (bf16[32,1024]{1,0:T(8,128)(2,1)S(1)}, bf16[32,1024]{1,0:T(8,128)(2,1)S(1)}, u32[]{:S(2)}, u32[]{:S(2)}) collective-permute-start(bf16[32,1024]{1,0:T(8,128)(2,1)S(1)} %get-tuple-element.70.refs_0_), channel_id=1, source_target_pairs={{0,24},{8,16},{16,8},{24,0},{1,25},{9,17},{17,9},{25,1},{2,26},{10... | collective-permute-start | bytes 196616 | tf_op jit(solution)/shard_map/ppermute | solution.py:35
  64.4 1.7 %collective-permute-start.22 = (bf16[32,1024]{1,0:T(8,128)(2,1)S(1)}, bf16[32,1024]{1,0:T(8,128)(2,1)S(1)}, u32[]{:S(2)}, u32[]{:S(2)}) collective-permute-start(bf16[32,1024]{1,0:T(8,128)(2,1)S(1)} %get-tuple-element.70.refs_0_), channel_id=1, source_target_pairs={{0,16},{8,24},{16,0},{24,8},{1,17},{9,25},{17,1},{25,9},{2,18},{10... | collective-permute-start | bytes 196616 | tf_op jit(solution)/shard_map/ppermute | solution.py:35
  66.0 1.3 %collective-permute-start.21 = (bf16[32,1024]{1,0:T(8,128)(2,1)S(1)}, bf16[32,1024]{1,0:T(8,128)(2,1)S(1)}, u32[]{:S(2)}, u32[]{:S(2)}) collective-permute-start(bf16[32,1024]{1,0:T(8,128)(2,1)S(1)} %get-tuple-element.70.refs_0_), channel_id=1, source_target_pairs={{0,8},{8,0},{16,24},{24,16},{1,9},{9,1},{17,25},{25,17},{2,10},{10... | collective-permute-start | bytes 196616 | tf_op jit(solution)/shard_map/ppermute | solution.py:35
  67.4 2.4 %collective-permute-done.23.refs_3_ = bf16[32,1024]{1,0:T(8,128)(2,1)S(1)} collective-permute-done((bf16[32,1024]{1,0:T(8,128)(2,1)S(1)}, bf16[32,1024]{1,0:T(8,128)(2,1)S(1)}, u32[]{:S(2)}, u32[]{:S(2)}) %collective-permute-start.23) | collective-permute-done | bytes 65568 | tf_op jit(solution)/shard_map/ppermute | solution.py:35
  69.8 2.7 %collective-permute-done.22.refs_2_ = bf16[32,1024]{1,0:T(8,128)(2,1)S(1)} collective-permute-done((bf16[32,1024]{1,0:T(8,128)(2,1)S(1)}, bf16[32,1024]{1,0:T(8,128)(2,1)S(1)}, u32[]{:S(2)}, u32[]{:S(2)}) %collective-permute-start.22) | collective-permute-done | bytes 65568 | tf_op jit(solution)/shard_map/ppermute | solution.py:35
  74.4 2.5 %collective-permute-done.26.refs_3_ = bf16[32,1024]{1,0:T(8,128)(2,1)S(1)} collective-permute-done((bf16[32,1024]{1,0:T(8,128)(2,1)S(1)}, bf16[32,1024]{1,0:T(8,128)(2,1)S(1)}, u32[]{:S(2)}, u32[]{:S(2)}) %collective-permute-start.26) | collective-permute-done | bytes 65568 | tf_op jit(solution)/shard_map/ppermute | solution.py:35
  77.6 1.3 %shard_map.68 = (f32[32,1024]{1,0:T(8,128)}, f32[32,512]{1,0:T(8,128)}) custom-call(bf16[32,1024]{1,0:T(8,128)(2,1)S(1)} %shard_map.67.refs_0_, bf16[32,1024]{1,0:T(8,128)(2,1)S(1)} %collective-permute-done.24.refs_1_, bf16[32,1024]{1,0:T(8,128)(2,1)S(1)} %collective-permute-done.25.refs_2_, bf16[32,1024]{1,0:T(8,128)(2,1)S(1)} %collective-permute-done.26.refs_3_, ...), custom_call_target="tpu_custom_call" | custom-call | tf_op jit(solution)/shard_map/pallas_call | solution.py:525
  (42 shorter events, 10.8 us)
Async XLA Ops:
  0.6 15.6 %copy-start = (s32[4,1024]{1,0:T(4,128)S(1)}, s32[4,1024]{1,0:T(4,128)}, u32[]{:S(2)}) copy-start(s32[4,1024]{1,0:T(4,128)} %param.7) | copy-start | bytes 49156
  1.9 1.4 %collective-permute-start = (f32[8,1024]{1,0:T(8,128)S(1)}, f32[8,1024]{1,0:T(8,128)S(1)}, u32[]{:S(2)}, u32[]{:S(2)}) collective-permute-start(f32[8,1024]{1,0:T(8,128)S(1)} %get-tuple-element.37.own_ref), channel_id=1, source_target_pairs={{0,1},{1,0},{2,3},{3,2},{4,5},{5,4},{6,7},{7,6},{8,9},{9,8},{10,11... | collective-permute-start | bytes 98312 | tf_op jit(solution)/shard_map/ppermute | solution.py:35
  3.3 5.7 %collective-permute-start.3 = (f32[8,1024]{1,0:T(8,128)S(1)}, f32[8,1024]{1,0:T(8,128)S(1)}, u32[]{:S(2)}, u32[]{:S(2)}) collective-permute-start(f32[8,1024]{1,0:T(8,128)S(1)} %shard_map.60.refs_0_), channel_id=1, source_target_pairs={{0,6},{1,7},{2,4},{3,5},{4,2},{5,3},{6,0},{7,1},{8,14},{9,15},{10,... | collective-permute-start | bytes 98312 | tf_op jit(solution)/shard_map/ppermute | solution.py:35
  7.2 3.9 %collective-permute-start.2 = (f32[8,1024]{1,0:T(8,128)S(1)}, f32[8,1024]{1,0:T(8,128)S(1)}, u32[]{:S(2)}, u32[]{:S(2)}) collective-permute-start(f32[8,1024]{1,0:T(8,128)S(1)} %shard_map.60.refs_0_), channel_id=1, source_target_pairs={{0,4},{1,5},{2,6},{3,7},{4,0},{5,1},{6,2},{7,3},{8,12},{9,13},{10,... | collective-permute-start | bytes 98312 | tf_op jit(solution)/shard_map/ppermute | solution.py:35
  7.7 3.9 %collective-permute-start.1 = (f32[8,1024]{1,0:T(8,128)S(1)}, f32[8,1024]{1,0:T(8,128)S(1)}, u32[]{:S(2)}, u32[]{:S(2)}) collective-permute-start(f32[8,1024]{1,0:T(8,128)S(1)} %shard_map.60.refs_0_), channel_id=1, source_target_pairs={{0,2},{1,3},{2,0},{3,1},{4,6},{5,7},{6,4},{7,5},{8,10},{9,11},{10,... | collective-permute-start | bytes 98312 | tf_op jit(solution)/shard_map/ppermute | solution.py:35
  16.1 1.6 %collective-permute-start.4 = (f32[64,1024]{1,0:T(8,128)S(1)}, f32[64,1024]{1,0:T(8,128)S(1)}, u32[]{:S(2)}, u32[]{:S(2)}) collective-permute-start(f32[64,1024]{1,0:T(8,128)S(1)} %get-tuple-element.42), channel_id=1, source_target_pairs={{0,1},{1,0},{2,3},{3,2},{4,5},{5,4},{6,7},{7,6},{8,9},{9,8},{10,11... | collective-permute-start | bytes 786440 | tf_op jit(solution)/shard_map/ppermute | solution.py:35
  17.8 7.4 %collective-permute-start.7 = (bf16[64,1024]{1,0:T(8,128)(2,1)S(1)}, bf16[64,1024]{1,0:T(8,128)(2,1)S(1)}, u32[]{:S(2)}, u32[]{:S(2)}) collective-permute-start(bf16[64,1024]{1,0:T(8,128)(2,1)S(1)} %add_convert_fusion), channel_id=1, source_target_pairs={{0,6},{1,7},{2,4},{3,5},{4,2},{5,3},{6,0},{7,1},{8,14},{9,15},{10,... | collective-permute-start | bytes 393224 | tf_op jit(solution)/shard_map/ppermute | solution.py:35
  19.3 7.8 %collective-permute-start.6 = (bf16[64,1024]{1,0:T(8,128)(2,1)S(1)}, bf16[64,1024]{1,0:T(8,128)(2,1)S(1)}, u32[]{:S(2)}, u32[]{:S(2)}) collective-permute-start(bf16[64,1024]{1,0:T(8,128)(2,1)S(1)} %add_convert_fusion), channel_id=1, source_target_pairs={{0,4},{1,5},{2,6},{3,7},{4,0},{5,1},{6,2},{7,3},{8,12},{9,13},{10,... | collective-permute-start | bytes 393224 | tf_op jit(solution)/shard_map/ppermute | solution.py:35
  19.4 7.8 %collective-permute-start.5 = (bf16[64,1024]{1,0:T(8,128)(2,1)S(1)}, bf16[64,1024]{1,0:T(8,128)(2,1)S(1)}, u32[]{:S(2)}, u32[]{:S(2)}) collective-permute-start(bf16[64,1024]{1,0:T(8,128)(2,1)S(1)} %add_convert_fusion), channel_id=1, source_target_pairs={{0,2},{1,3},{2,0},{3,1},{4,6},{5,7},{6,4},{7,5},{8,10},{9,11},{10,... | collective-permute-start | bytes 393224 | tf_op jit(solution)/shard_map/ppermute | solution.py:35
  21.3 3.7 %collective-permute-start.8 = (f32[4,1024]{1,0:T(4,128)S(1)}, f32[4,1024]{1,0:T(4,128)S(1)}, u32[]{:S(2)}, u32[]{:S(2)}) collective-permute-start(f32[4,1024]{1,0:T(4,128)S(1)} %convert_element_type.39), channel_id=1, source_target_pairs={{0,8},{8,0},{16,24},{24,16},{1,9},{9,1},{17,25},{25,17},{2,10},{10... | collective-permute-start | bytes 49160 | tf_op jit(solution)/shard_map/ppermute | solution.py:35
  27.3 2.9 %collective-permute-start.9 = (f32[64,1024]{1,0:T(8,128)S(1)}, f32[64,1024]{1,0:T(8,128)S(1)}, u32[]{:S(2)}, u32[]{:S(2)}) collective-permute-start(f32[64,1024]{1,0:T(8,128)S(1)} %broadcast_multiply_fusion.1.own_ref), channel_id=1, source_target_pairs={{0,1},{1,0},{2,3},{3,2},{4,5},{5,4},{6,7},{7,6},{8,9},{9,8},{10,11... | collective-permute-start | bytes 786440 | tf_op jit(solution)/shard_map/ppermute | solution.py:35
  32.1 1.7 %collective-permute-start.10 = (f32[64,1024]{1,0:T(8,128)S(1)}, f32[64,1024]{1,0:T(8,128)S(1)}, u32[]{:S(2)}, u32[]{:S(2)}) collective-permute-start(f32[64,1024]{1,0:T(8,128)S(1)} %get-tuple-element.58), channel_id=1, source_target_pairs={{0,1},{1,0},{2,3},{3,2},{4,5},{5,4},{6,7},{7,6},{8,9},{9,8},{10,11... | collective-permute-start | bytes 786440 | tf_op jit(solution)/shard_map/ppermute | solution.py:35
  33.9 6.2 %collective-permute-start.14 = (f32[8,1024]{1,0:T(8,128)S(1)}, f32[8,1024]{1,0:T(8,128)S(1)}, u32[]{:S(2)}, u32[]{:S(2)}) collective-permute-start(f32[8,1024]{1,0:T(8,128)S(1)} %pad_maximum_fusion.1), channel_id=1, source_target_pairs={{0,16},{8,24},{16,0},{24,8},{1,17},{9,25},{17,1},{25,9},{2,18},{10... | collective-permute-start | bytes 98312 | tf_op jit(solution)/shard_map/ppermute | solution.py:35
  36.6 7.3 %collective-permute-start.13 = (bf16[64,1024]{1,0:T(8,128)(2,1)S(1)}, bf16[64,1024]{1,0:T(8,128)(2,1)S(1)}, u32[]{:S(2)}, u32[]{:S(2)}) collective-permute-start(bf16[64,1024]{1,0:T(8,128)(2,1)S(1)} %fusion.3), channel_id=1, source_target_pairs={{0,6},{1,7},{2,4},{3,5},{4,2},{5,3},{6,0},{7,1},{8,14},{9,15},{10,... | collective-permute-start | bytes 393224 | tf_op jit(solution)/shard_map/ppermute | solution.py:35
  37.9 7.8 %collective-permute-start.12 = (bf16[64,1024]{1,0:T(8,128)(2,1)S(1)}, bf16[64,1024]{1,0:T(8,128)(2,1)S(1)}, u32[]{:S(2)}, u32[]{:S(2)}) collective-permute-start(bf16[64,1024]{1,0:T(8,128)(2,1)S(1)} %fusion.3), channel_id=1, source_target_pairs={{0,4},{1,5},{2,6},{3,7},{4,0},{5,1},{6,2},{7,3},{8,12},{9,13},{10,... | collective-permute-start | bytes 393224 | tf_op jit(solution)/shard_map/ppermute | solution.py:35
  38.5 7.3 %collective-permute-start.11 = (bf16[64,1024]{1,0:T(8,128)(2,1)S(1)}, bf16[64,1024]{1,0:T(8,128)(2,1)S(1)}, u32[]{:S(2)}, u32[]{:S(2)}) collective-permute-start(bf16[64,1024]{1,0:T(8,128)(2,1)S(1)} %fusion.3), channel_id=1, source_target_pairs={{0,2},{1,3},{2,0},{3,1},{4,6},{5,7},{6,4},{7,5},{8,10},{9,11},{10,... | collective-permute-start | bytes 393224 | tf_op jit(solution)/shard_map/ppermute | solution.py:35
  46.0 1.6 %collective-permute-start.15 = (f32[64,1024]{1,0:T(8,128)S(1)}, f32[64,1024]{1,0:T(8,128)S(1)}, u32[]{:S(2)}, u32[]{:S(2)}) collective-permute-start(f32[64,1024]{1,0:T(8,128)S(1)} %get-tuple-element.62.own_ref), channel_id=1, source_target_pairs={{0,1},{1,0},{2,3},{3,2},{4,5},{5,4},{6,7},{7,6},{8,9},{9,8},{10,11... | collective-permute-start | bytes 786440 | tf_op jit(solution)/shard_map/ppermute | solution.py:35
  50.3 1.5 %collective-permute-start.16 = (f32[64,1024]{1,0:T(8,128)S(1)}, f32[64,1024]{1,0:T(8,128)S(1)}, u32[]{:S(2)}, u32[]{:S(2)}) collective-permute-start(f32[64,1024]{1,0:T(8,128)S(1)} %get-tuple-element.66), channel_id=1, source_target_pairs={{0,1},{1,0},{2,3},{3,2},{4,5},{5,4},{6,7},{7,6},{8,9},{9,8},{10,11... | collective-permute-start | bytes 786440 | tf_op jit(solution)/shard_map/ppermute | solution.py:35
  51.9 7.4 %collective-permute-start.19 = (bf16[64,1024]{1,0:T(8,128)(2,1)S(1)}, bf16[64,1024]{1,0:T(8,128)(2,1)S(1)}, u32[]{:S(2)}, u32[]{:S(2)}) collective-permute-start(bf16[64,1024]{1,0:T(8,128)(2,1)S(1)} %fusion.5.refs_1_), channel_id=1, source_target_pairs={{0,6},{1,7},{2,4},{3,5},{4,2},{5,3},{6,0},{7,1},{8,14},{9,15},{10,... | collective-permute-start | bytes 393224 | tf_op jit(solution)/shard_map/ppermute | solution.py:35
  53.4 7.9 %collective-permute-start.18 = (bf16[64,1024]{1,0:T(8,128)(2,1)S(1)}, bf16[64,1024]{1,0:T(8,128)(2,1)S(1)}, u32[]{:S(2)}, u32[]{:S(2)}) collective-permute-start(bf16[64,1024]{1,0:T(8,128)(2,1)S(1)} %fusion.5.refs_1_), channel_id=1, source_target_pairs={{0,4},{1,5},{2,6},{3,7},{4,0},{5,1},{6,2},{7,3},{8,12},{9,13},{10,... | collective-permute-start | bytes 393224 | tf_op jit(solution)/shard_map/ppermute | solution.py:35
  54.0 7.3 %collective-permute-start.17 = (bf16[64,1024]{1,0:T(8,128)(2,1)S(1)}, bf16[64,1024]{1,0:T(8,128)(2,1)S(1)}, u32[]{:S(2)}, u32[]{:S(2)}) collective-permute-start(bf16[64,1024]{1,0:T(8,128)(2,1)S(1)} %fusion.5.refs_1_), channel_id=1, source_target_pairs={{0,2},{1,3},{2,0},{3,1},{4,6},{5,7},{6,4},{7,5},{8,10},{9,11},{10,... | collective-permute-start | bytes 393224 | tf_op jit(solution)/shard_map/ppermute | solution.py:35
  61.6 1.2 %collective-permute-start.20 = (f32[8,128]{1,0:T(8,128)S(1)}, f32[8,128]{1,0:T(8,128)S(1)}, u32[]{:S(2)}, u32[]{:S(2)}) collective-permute-start(f32[8,128]{1,0:T(8,128)S(1)} %get-tuple-element.68.own_ref), channel_id=1, source_target_pairs={{0,1},{1,0},{2,3},{3,2},{4,5},{5,4},{6,7},{7,6},{8,9},{9,8},{10,11... | collective-permute-start | bytes 12296 | tf_op jit(solution)/shard_map/ppermute | solution.py:35
  62.9 6.9 %collective-permute-start.23 = (bf16[32,1024]{1,0:T(8,128)(2,1)S(1)}, bf16[32,1024]{1,0:T(8,128)(2,1)S(1)}, u32[]{:S(2)}, u32[]{:S(2)}) collective-permute-start(bf16[32,1024]{1,0:T(8,128)(2,1)S(1)} %get-tuple-element.70.refs_0_), channel_id=1, source_target_pairs={{0,24},{8,16},{16,8},{24,0},{1,25},{9,17},{17,9},{25,1},{2,26},{10... | collective-permute-start | bytes 196616 | tf_op jit(solution)/shard_map/ppermute | solution.py:35
  64.4 8.1 %collective-permute-start.22 = (bf16[32,1024]{1,0:T(8,128)(2,1)S(1)}, bf16[32,1024]{1,0:T(8,128)(2,1)S(1)}, u32[]{:S(2)}, u32[]{:S(2)}) collective-permute-start(bf16[32,1024]{1,0:T(8,128)(2,1)S(1)} %get-tuple-element.70.refs_0_), channel_id=1, source_target_pairs={{0,16},{8,24},{16,0},{24,8},{1,17},{9,25},{17,1},{25,9},{2,18},{10... | collective-permute-start | bytes 196616 | tf_op jit(solution)/shard_map/ppermute | solution.py:35
  66.0 6.4 %collective-permute-start.21 = (bf16[32,1024]{1,0:T(8,128)(2,1)S(1)}, bf16[32,1024]{1,0:T(8,128)(2,1)S(1)}, u32[]{:S(2)}, u32[]{:S(2)}) collective-permute-start(bf16[32,1024]{1,0:T(8,128)(2,1)S(1)} %get-tuple-element.70.refs_0_), channel_id=1, source_target_pairs={{0,8},{8,0},{16,24},{24,16},{1,9},{9,1},{17,25},{25,17},{2,10},{10... | collective-permute-start | bytes 196616 | tf_op jit(solution)/shard_map/ppermute | solution.py:35
  72.5 4.4 %collective-permute-start.26 = (bf16[32,1024]{1,0:T(8,128)(2,1)S(1)}, bf16[32,1024]{1,0:T(8,128)(2,1)S(1)}, u32[]{:S(2)}, u32[]{:S(2)}) collective-permute-start(bf16[32,1024]{1,0:T(8,128)(2,1)S(1)} %shard_map.67.refs_0_), channel_id=1, source_target_pairs={{0,3},{1,2},{2,1},{3,0},{4,7},{5,6},{6,5},{7,4},{8,11},{9,10},{10,... | collective-permute-start | bytes 196616 | tf_op jit(solution)/shard_map/ppermute | solution.py:35
  72.6 5.0 %collective-permute-start.25 = (bf16[32,1024]{1,0:T(8,128)(2,1)S(1)}, bf16[32,1024]{1,0:T(8,128)(2,1)S(1)}, u32[]{:S(2)}, u32[]{:S(2)}) collective-permute-start(bf16[32,1024]{1,0:T(8,128)(2,1)S(1)} %shard_map.67.refs_0_), channel_id=1, source_target_pairs={{0,2},{1,3},{2,0},{3,1},{4,6},{5,7},{6,4},{7,5},{8,10},{9,11},{10,... | collective-permute-start | bytes 196616 | tf_op jit(solution)/shard_map/ppermute | solution.py:35
  73.6 4.0 %collective-permute-start.24 = (bf16[32,1024]{1,0:T(8,128)(2,1)S(1)}, bf16[32,1024]{1,0:T(8,128)(2,1)S(1)}, u32[]{:S(2)}, u32[]{:S(2)}) collective-permute-start(bf16[32,1024]{1,0:T(8,128)(2,1)S(1)} %shard_map.67.refs_0_), channel_id=1, source_target_pairs={{0,1},{1,0},{2,3},{3,2},{4,5},{5,4},{6,7},{7,6},{8,9},{9,8},{10,11... | collective-permute-start | bytes 196616 | tf_op jit(solution)/shard_map/ppermute | solution.py:35
where the time goes:
time: 79 us; the launch traced here: 78.9 us
  waiting for transfers between devices  35.4 us (45%)
  starting transfers between devices  27.3 us (35%)
  Pallas kernels  15.1 us (19%)
    ppermute x27, waiting for transfers between devices, swapped(): return lax.ppermute(block, axis, [(i, i ^ distance) for i in devices])  35.4 us
    ppermute x27, starting transfers between devices, swapped(): return lax.ppermute(block, axis, [(i, i ^ distance) for i in devices])  27.3 us
    pallas_call x2, Pallas kernels, per_device(): called(next_kernel, (full_shape, half_shape, half_shape), [VMEM] * 8, [pl...  4.79 us
    pallas_call x1, Pallas kernels, per_device(): called(functools.partial(first_kernel, samples * shards, len(powers), len...  4.53 us
    pallas_call x1, Pallas kernels, per_device(): called(side_kernel, (full_shape, square, square), [VMEM] * 6, cost=pl.Cos...  2.77 us
  transfers between devices with their start and end apart: 27, of which 20 were waited for; matrix products, arithmetic and copies ran while one was open for 0% of the time, Pallas kernels for 4%

commit v1 on v0

--- a/solution.py
+++ b/solution.py
@@ -238,6 +238,31 @@
     return jnp.where(core + chip > 0, rows, 0.0)
 
 
+def moved_lanes(blocks, shift):
+    turned = [rotated(block, shift, 1) for block in blocks]
+    lane = lax.broadcasted_iota(jnp.int32, turned[0].shape, 1)
+    return [jnp.where(lane < shift, turned[k - 1], turned[k]) for k in range(len(turned))]
+
+
+def lagged_gram(window_ref, pairs_ref, sums_ref):
+    width = window_ref.shape[0]
+    count, rows, lanes = pairs_ref.shape
+    samples = rows - HALO
+    left = jnp.concatenate([window_ref[width - HALO :, :], window_ref[:samples, :]], axis=0)
+    pairs = nt_dot(left, window_ref[...])
+    for k in range(count):
+        pairs_ref[k] = pairs[:, k * lanes : (k + 1) * lanes]
+    body = rows - 8
+    earlier = moved_lanes([pairs_ref[k, 7 : 7 + body, :] for k in range(count)], 1)
+    for k in range(count):
+        sums_ref[k, 8:, :] = pairs_ref[k, 8:, :] + earlier[k]
+    first = moved_lanes([sums_ref[k, HALO - 1 : rows - 1, :] for k in range(count)], 1)
+    later = moved_lanes([sums_ref[k, HALO - 3 : rows - 3, :] for k in range(count)], 3)
+    return jnp.concatenate(
+        [first[k] + later[k] for k in range(samples // lanes)], axis=1
+    )
+
+
 def first_kernel(count, parts, halos, *refs):
     part_refs, refs = refs[:parts], refs[parts:]
     halo_refs, refs = refs[:halos], refs[halos:]
@@ -253,6 +278,8 @@
         state_ref,
         send_ref,
         keep_ref,
+        pairs_ref,
+        sums_ref,
     ) = refs
     samples, channels = recording_ref.shape
     width = window_ref.shape[0]
@@ -268,10 +295,7 @@
     window = window_ref[...]
 
     along = along_ref[...]
-    pairs = nt_dot(window, window)
-    pairs = pairs + rotated(rotated(pairs, 1, 0), 1, 1)
-    pairs = pairs + rotated(rotated(pairs, 2, 0), 2, 1)
-    gram = rotated(rotated(pairs, 1, 0)[:samples], 1, 1)[:, :samples] * (1.0 / CAP)
+    gram = lagged_gram(window_ref, pairs_ref, sums_ref) * (1.0 / CAP)
     weighted = gram * down_ref[:, :1]
     squares = jnp.sum(weighted * gram, axis=0, keepdims=True) * along[:, :samples]
     bound = jnp.sqrt(jnp.sum(squares, axis=1, keepdims=True))
@@ -326,11 +350,11 @@
     cross_ref,
     along_ref,
     state_ref,
-    later_ref,
     send_ref,
     keep_ref,
-    mean_ref,
+    *state_refs,
 ):
+    later_ref, mean_ref = state_refs if len(state_refs) == 2 else state_refs * 2
     core, _, _ = place()
     join_halves(core, own_ref, other_ref, mean_ref)
     cube, norms = column_norms(mean_ref[...])
@@ -347,64 +371,60 @@
     store_halves(core, local + dual, later_ref, send_ref, keep_ref)
 
 
-def norm_kernel(shards, *refs):
-    total_ref, *part_refs, mean_ref, sum_ref = refs
-    change = paired_sum([ref[...].astype(f32) for ref in part_refs])
-    mean = (total_ref[...] + change) / shards
-    mean_ref[...] = mean
-    _, norms = column_norms(mean)
-    sum_ref[...] = jnp.broadcast_to(jnp.sum(norms, keepdims=True), sum_ref.shape)
-
-
-def weigh_kernel(
-    boots, mean_ref, own_ref, other_ref, support_ref, weighted_ref, tally_ref, blocks_ref
-):
-    core, chip, position = place()
-    side = lax.rem(chip, 2)
-    start = pl.multiple_of(side * RESPONSE_COUNT, RESPONSE_COUNT)
-    cube, norms = column_norms(mean_ref[pl.ds(start, RESPONSE_COUNT), :])
-    channels = cube.shape[2]
-    level = shrink_level * ((own_ref[:1, :1] + other_ref[:1, :1]) / (LAGS * channels))
+def part_kernel(boots, own_ref, other_ref, window_ref, support_ref, *refs):
+    piece_refs, (tally_ref, full_ref, blocks_ref) = refs[:boots], refs[boots:]
+    core, _, position = place()
+    join_halves(core, own_ref, other_ref, full_ref)
+    cube, norms = column_norms(full_ref[...])
+    level = shrink_level * (jnp.sum(norms, keepdims=True) / norms.size)
     for d in range(boots):
         blocks_ref[lax.bitwise_xor(position, d)] = support_ref[d * boots : (d + 1) * boots, :]
-    each = channels // blocks_ref.shape[2]
-    blocks = [blocks_ref.at[(core * 2 + side) * each + k] for k in range(each)]
-    chosen = jnp.concatenate([b[pl.ds(position, 1), :] for b in blocks], axis=1)
-    tally_ref[...] = jnp.concatenate(
-        [jnp.sum(b[...], axis=0, keepdims=True) for b in blocks], axis=1
-    )
-    weighted = chosen[:, None, :] * shrunk(cube, norms, level)
-    weighted_ref[...] = weighted.reshape(weighted_ref.shape).astype(bf16)
+    channels = full_ref.shape[1]
+    width = blocks_ref.shape[2]
+    each = channels // width
+    chosen, tally = [], []
+    for lag in range(LAGS):
+        blocks = [blocks_ref.at[lag * each + k] for k in range(each)]
+        chosen.append(jnp.concatenate([b[pl.ds(position, 1), :] for b in blocks], axis=1))
+        tally.append(
+            jnp.concatenate([jnp.sum(b[...], axis=0, keepdims=True) for b in blocks], axis=1)
+        )
+    chosen = jnp.concatenate(chosen, axis=0)[:, None, :]
+    tally = jnp.maximum(jnp.concatenate(tally, axis=0), 1.0)[:, None, :]
+    tally_ref[...] = jnp.sum(blocks_ref[position], axis=0, keepdims=True)
+    weighted = chosen * shrunk(cube, norms, level)
+    full_ref[...] = weighted.reshape(full_ref.shape)
+    share = (weighted / tally).reshape(full_ref.shape).astype(bf16)
+    half = RESPONSE_COUNT // 2
+    samples = (piece_refs[0].shape[1] - width) // 2
+    forecast = gathered_lags(nt_dot(share, window_ref[...]), samples).astype(bf16)
+    for d in range(boots):
+        opening = lax.bitwise_xor(position, d) * width
+        row = lax.div(opening, channels) * RESPONSE_COUNT + core * half
+        rows = pl.ds(pl.multiple_of(row, half), half)
+        if width == channels:
+            block = full_ref[rows, :]
+        else:
+            column = pl.multiple_of(lax.rem(opening, channels), width)
+            block = full_ref[rows, pl.ds(column, width)]
+        piece_refs[d][:, :width] = block.astype(bf16)
+        piece_refs[d][:, width : width + samples] = forecast[:half]
+        piece_refs[d][:, width + samples :] = forecast[half:]
 
 
 def average_kernel(*refs):
-    *piece_refs, tally_ref, averaged_ref = refs
+    *piece_refs, tally_ref, answer_ref, averaged_ref, residual_ref = refs
+    half, width = averaged_ref.shape
+    samples = residual_ref.shape[1]
     added = paired_sum([ref[...].astype(f32) for ref in piece_refs])
-    averaged_ref[...] = (added / jnp.maximum(tally_ref[...], 1.0)).astype(bf16)
-
-
-def last_kernel(*refs):
-    *lag_refs, window_ref, answer_ref, averaged_ref, residual_ref, full_ref = refs
-    core, chip, position = place()
-    mine = core * 2 + lax.rem(chip, 2)
-    for step, ref in enumerate(lag_refs):
-        lag = lax.bitwise_xor(mine, (step % 2) * 2 + step // 2)
-        full_ref[pl.ds(pl.multiple_of(lag * RESPONSE_COUNT, RESPONSE_COUNT), RESPONSE_COUNT), :] = (
-            ref[...]
-        )
-    samples = residual_ref.shape[1]
-    forecast = gathered_lags(nt_dot(full_ref[...], window_ref[...]), samples)
-    residual_ref[...] = answer_ref[...] - forecast
-    channels = full_ref.shape[1]
-    width = averaged_ref.shape[1]
-    opening = position * width
-    row = pl.multiple_of(lax.div(opening, channels) * RESPONSE_COUNT, RESPONSE_COUNT)
-    if width == channels:
-        block = full_ref[pl.ds(row, RESPONSE_COUNT), :]
-    else:
-        column = pl.multiple_of(lax.rem(opening, channels), width)
-        block = full_ref[pl.ds(row, RESPONSE_COUNT), pl.ds(column, width)]
-    averaged_ref[...] = block.astype(f32)
+    averaged_ref[...] = added[:, :width] / jnp.maximum(tally_ref[...], 1.0)
+    residual_ref[:half, :] = answer_ref[:half, :] - added[:, width : width + samples]
+    residual_ref[half:, :] = answer_ref[half:, :] - added[:, width + samples :]
+
+
+def last_kernel(own_ref, other_ref, averaged_ref):
+    core, _, _ = place()
+    join_halves(core, own_ref, other_ref, averaged_ref)
 
 
 def shaped(shape, dtype=f32):
@@ -472,18 +492,24 @@
             half_shape,
         ),
         [VMEM] * (len(powers) + len(halos) + 3),
+        [pltpu.VMEM((width // 128, samples + HALO, 128), f32)] * 2,
     )(*powers, *halos, recording, along, down)
 
     total = jnp.zeros((half, channels), f32)
     held = total
     support = support.astype(f32)
     reach = 1
-    for count in range(1, ITERS):
+    for count in range(1, ITERS + 1):
         change = (keep + swapped(send, "tm", 1) - held).astype(bf16)
-        change, support, window, high = lax.optimization_barrier((change, support, window, high))
+        if count < ITERS:
+            change, support, window, high = lax.optimization_barrier(
+                (change, support, window, high)
+            )
         total = total + chip_parts_sum(change)
         held = held + change.astype(f32)
         mean = total / shards
+        if count == ITERS:
+            break
         while reach < boots:
             support = jnp.concatenate([support, swapped(support, "boot", reach)], axis=0)
             reach *= 2
@@ -499,38 +525,33 @@
                 ),
             )(window, high, low, bound, answer, along)
         mean, support = lax.optimization_barrier((mean, support))
-        state, send, keep = called(
+        going = count + 1 < ITERS
+        send, keep, *states = called(
             next_kernel,
-            (full_shape, half_shape, half_shape),
+            (half_shape, half_shape) + (full_shape,) * going,
             [VMEM] * 8,
             [pltpu.VMEM((rows, channels), f32)],
         )(mean, swapped(mean, "tm", 1), window, first, second, cross, along, state)
-
-    change = (keep + swapped(send, "tm", 1) - held).astype(bf16)
-    parts = chip_parts(change) if shards <= 8 else [chip_parts_sum(change)]
-    mean, summed = called(
-        functools.partial(norm_kernel, shards),
-        (half_shape, shaped((8, 128))),
-        [VMEM] * (1 + len(parts)),
-    )(total, *parts)
-    lag_shape = shaped((RESPONSE_COUNT, channels), bf16)
-    weighted, tally = called(
-        functools.partial(weigh_kernel, boots),
-        (lag_shape, shaped((1, channels))),
+        state = states[0] if going else None
+
+    features = LAGS * channels // boots
+    piece = shaped((RESPONSE_COUNT // 2, features + 2 * samples), bf16)
+    *pieces, tally = called(
+        functools.partial(part_kernel, boots),
+        (piece,) * boots + (shaped((1, features)),),
         [VMEM] * 4,
-        [pltpu.VMEM((boots, boots, support.shape[1]), f32)],
-    )(mean, summed, swapped(summed, "tm", 1), support)
-    pieces = [weighted] + [swapped(weighted, "boot", d) for d in range(1, boots)]
-    averaged = called(average_kernel, lag_shape, [VMEM] * (boots + 1))(*pieces, tally)
-    return called(
-        last_kernel,
-        (
-            shaped((RESPONSE_COUNT, LAGS * channels // boots)),
-            shaped((RESPONSE_COUNT, samples)),
-        ),
-        [VMEM] * 6,
-        [pltpu.VMEM((rows, channels), bf16)],
-    )(averaged, *[swapped(averaged, "tm", d) for d in range(1, 4)], window, answer)
+        [pltpu.VMEM((rows, channels), f32), pltpu.VMEM((boots, boots, features), f32)],
+    )(mean, swapped(mean, "tm", 1), window, support)
+    pieces = pieces[:1] + [swapped(pieces[d], "boot", d) for d in range(1, boots)]
+    averaged, residual = called(
+        average_kernel,
+        (shaped((RESPONSE_COUNT // 2, features)), shaped((RESPONSE_COUNT, samples))),
+        [VMEM] * (boots + 2),
+    )(*pieces, tally, answer)
+    averaged = called(last_kernel, shaped((RESPONSE_COUNT, features)), [VMEM] * 2)(
+        averaged, swapped(averaged, "tm", 1)
+    )
+    return averaged, residual
 
 
 def solution(mesh):

time: 79 us -> 74.7 us (0.946)
  starting transfers between devices: 27.3 us -> 25.4 us
  waiting for transfers between devices: 35.4 us -> 33.8 us
  Pallas kernels: 15.1 us -> 14.2 us
    ppermute x27 -> x25, starting transfers between devices: 27.3 us -> 25.4 us  [swapped(): return lax.ppermute(block, axis, [(i, i ^ distance) for i in devices])]
    ppermute x27 -> x25, waiting for transfers between devices: 35.4 us -> 33.8 us  [swapped(): return lax.ppermute(block, axis, [(i, i ^ distance) for i in devices])]
    pallas_call x6 -> x5, Pallas kernels: 6.5 us -> 6.24 us  [the longest x2 4.03 us: per_device(): called(next_kernel, (half_shape, half_shape) + (full_shape,) * going, [VM...]
  transfers between devices with their start and end apart: 27 -> 25, of which waited for: 20 -> 18; matrix products, arithmetic and copies ran while one was open for 0% -> 0% of each run, Pallas kernels for 4% -> 4%
where the time goes in v1:
time: 74.7 us; the launch traced here: 74.6 us
  waiting for transfers between devices  33.8 us (45%)
  starting transfers between devices  25.4 us (34%)
  Pallas kernels  14.2 us (19%)
  between operations  0.77 us (1%)
    ppermute x25, waiting for transfers between devices, swapped(): return lax.ppermute(block, axis, [(i, i ^ distance) for i in devices])  33.8 us
    ppermute x25, starting transfers between devices, swapped(): return lax.ppermute(block, axis, [(i, i ^ distance) for i in devices])  25.4 us
    pallas_call x2, Pallas kernels, per_device(): called(next_kernel, (half_shape, half_shape) + (full_shape,) * going, [VM...  4.03 us
    pallas_call x1, Pallas kernels, per_device(): called(functools.partial(first_kernel, samples * shards, len(powers), len...  3.93 us
    pallas_call x1, Pallas kernels, per_device(): called(side_kernel, (full_shape, square, square), [VMEM] * 6, cost=pl.Cos...  2.77 us
  transfers between devices with their start and end apart: 25, of which 18 were waited for; matrix products, arithmetic and copies ran while one was open for 0% of the time, Pallas kernels for 4%

profile of v1, /device:TPU:0, one launch (start us, length us, event | category | flops | bytes accessed | tf_op | source)
XLA Modules:
  0.0 74.6 jit_solution(12006860658496775915)
XLA Ops:
  0.6 1.3 %shard_map.59 = (bf16[512,1024]{1,0:T(8,128)(2,1)S(1)}, f32[8,1024]{1,0:T(8,128)S(1)}, f32[1,640]{1,0:T(1,128)S(1)}, f32[512,128]{1,0:T(8,128)S(1)}) custom-call(s32[1,6]{1,0:T(1,128)} %starts_hbm.1, s32[1,6]{1,0:T(1,128)} %lengths_hbm.1, bf16[512,1024]{1,0:T(8,128)(2,1)} %source_ref.1), custom_call_target="tpu_custom_call" | custom-call | tf_op jit(solution)/shard_map/pallas_call | solution.py:456
  3.4 3.8 %collective-permute-start.3 = (f32[8,1024]{1,0:T(8,128)S(1)}, f32[8,1024]{1,0:T(8,128)S(1)}, u32[]{:S(2)}, u32[]{:S(2)}) collective-permute-start(f32[8,1024]{1,0:T(8,128)S(1)} %shard_map.60.refs_0_), channel_id=1, source_target_pairs={{0,6},{1,7},{2,4},{3,5},{4,2},{5,3},{6,0},{7,1},{8,14},{9,15},{10,... | collective-permute-start | bytes 98312 | tf_op jit(solution)/shard_map/ppermute | solution.py:35
  7.8 1.3 %collective-permute-done.3.refs_3_.refs_7_ = f32[8,1024]{1,0:T(8,128)S(1)} collective-permute-done((f32[8,1024]{1,0:T(8,128)S(1)}, f32[8,1024]{1,0:T(8,128)S(1)}, u32[]{:S(2)}, u32[]{:S(2)}) %collective-permute-start.3) | collective-permute-done | bytes 32800 | tf_op jit(solution)/shard_map/ppermute | solution.py:35
  9.1 2.0 %collective-permute-done.2.refs_2_.refs_6_ = f32[8,1024]{1,0:T(8,128)S(1)} collective-permute-done((f32[8,1024]{1,0:T(8,128)S(1)}, f32[8,1024]{1,0:T(8,128)S(1)}, u32[]{:S(2)}, u32[]{:S(2)}) %collective-permute-start.2) | collective-permute-done | bytes 32800 | tf_op jit(solution)/shard_map/ppermute | solution.py:35
  11.6 3.9 %shard_map.61 = (bf16[640,1024]{1,0:T(8,128)(2,1)S(1)}, bf16[512,512]{1,0:T(8,128)(2,1)S(1)}, bf16[512,512]{1,0:T(8,128)(2,1)S(1)}, f32[8,128]{1,0:T(8,128)S(1)}...) custom-call(f32[8,1024]{1,0:T(8,128)S(1)} %shard_map.60.refs_0_, ...), custom_call_target="tpu_custom_call" | custom-call | tf_op jit(solution)/shard_map/pallas_call | solution.py:482
  15.7 1.5 %collective-permute-done.4 = f32[64,1024]{1,0:T(8,128)S(1)} collective-permute-done((f32[64,1024]{1,0:T(8,128)S(1)}, f32[64,1024]{1,0:T(8,128)S(1)}, u32[]{:S(2)}, u32[]{:S(2)}) %collective-permute-start.4) | collective-permute-done | bytes 262176 | tf_op jit(solution)/shard_map/ppermute | solution.py:35
  17.2 1.6 %collective-permute-start.7 = (bf16[64,1024]{1,0:T(8,128)(2,1)S(1)}, bf16[64,1024]{1,0:T(8,128)(2,1)S(1)}, u32[]{:S(2)}, u32[]{:S(2)}) collective-permute-start(bf16[64,1024]{1,0:T(8,128)(2,1)S(1)} %add_convert_fusion), channel_id=1, source_target_pairs={{0,6},{1,7},{2,4},{3,5},{4,2},{5,3},{6,0},{7,1},{8,14},{9,15},{10,... | collective-permute-start | bytes 393224 | tf_op jit(solution)/shard_map/ppermute | solution.py:35
  18.8 1.9 %collective-permute-start.5 = (bf16[64,1024]{1,0:T(8,128)(2,1)S(1)}, bf16[64,1024]{1,0:T(8,128)(2,1)S(1)}, u32[]{:S(2)}, u32[]{:S(2)}) collective-permute-start(bf16[64,1024]{1,0:T(8,128)(2,1)S(1)} %add_convert_fusion), channel_id=1, source_target_pairs={{0,2},{1,3},{2,0},{3,1},{4,6},{5,7},{6,4},{7,5},{8,10},{9,11},{10,... | collective-permute-start | bytes 393224 | tf_op jit(solution)/shard_map/ppermute | solution.py:35
  20.7 1.6 %collective-permute-start.8 = (f32[4,1024]{1,0:T(4,128)S(1)}, f32[4,1024]{1,0:T(4,128)S(1)}, u32[]{:S(2)}, u32[]{:S(2)}) collective-permute-start(f32[4,1024]{1,0:T(4,128)S(1)} %convert_element_type.51), channel_id=1, source_target_pairs={{0,8},{8,0},{16,24},{24,16},{1,9},{9,1},{17,25},{25,17},{2,10},{10... | collective-permute-start | bytes 49160 | tf_op jit(solution)/shard_map/ppermute | solution.py:35
  22.3 2.2 %collective-permute-done.8 = f32[4,1024]{1,0:T(4,128)S(1)} collective-permute-done((f32[4,1024]{1,0:T(4,128)S(1)}, f32[4,1024]{1,0:T(4,128)S(1)}, u32[]{:S(2)}, u32[]{:S(2)}) %collective-permute-start.8) | collective-permute-done | bytes 16416 | tf_op jit(solution)/shard_map/ppermute | solution.py:35
  24.5 2.0 %collective-permute-done.6 = bf16[64,1024]{1,0:T(8,128)(2,1)S(1)} collective-permute-done((bf16[64,1024]{1,0:T(8,128)(2,1)S(1)}, bf16[64,1024]{1,0:T(8,128)(2,1)S(1)}, u32[]{:S(2)}, u32[]{:S(2)}) %collective-permute-start.6) | collective-permute-done | bytes 131104 | tf_op jit(solution)/shard_map/ppermute | solution.py:35
  26.8 2.8 %shard_map.62 = (f32[128,1024]{1,0:T(8,128)S(1)}, bf16[512,512]{1,0:T(8,128)(2,1)S(1)}, bf16[512,512]{1,0:T(8,128)(2,1)S(1)}) custom-call(bf16[640,1024]{1,0:T(8,128)(2,1)S(1)} %get-tuple-element.66.window_ref, bf16[512,512]{1,0:T(8,128)(2,1)S(1)} %get-tuple-element.52.high_ref, bf16[512,512]{1,0:T(8,128)(2,1)S(1)} %get-tuple-element.53.low_ref, ...), custom_call_target="tpu_custom_call" | custom-call | flops 1879048192 | bytes 1048576 | tf_op jit(solution)/shard_map/pallas_call | solution.py:519
  29.5 2.0 %shard_map.63 = (f32[64,1024]{1,0:T(8,128)S(1)}, f32[64,1024]{1,0:T(8,128)S(1)}, f32[128,1024]{1,0:T(8,128)S(1)}) custom-call(f32[64,1024]{1,0:T(8,128)S(1)} %broadcast_multiply_fusion.1.own_ref, f32[64,1024]{1,0:T(8,128)S(1)} %collective-permute-done.9.other_ref, bf16[640,1024]{1,0:T(8,128)(2,1)S(1)} %get-tuple-element.66.window_ref, ...), custom_call_target="tpu_custom_call" | custom-call | tf_op jit(solution)/shard_map/pallas_call | solution.py:529
  32.1 1.2 %collective-permute-done.10 = f32[64,1024]{1,0:T(8,128)S(1)} collective-permute-done((f32[64,1024]{1,0:T(8,128)S(1)}, f32[64,1024]{1,0:T(8,128)S(1)}, u32[]{:S(2)}, u32[]{:S(2)}) %collective-permute-start.10) | collective-permute-done | bytes 262176 | tf_op jit(solution)/shard_map/ppermute | solution.py:35
  33.3 2.6 %collective-permute-start.14 = (f32[8,1024]{1,0:T(8,128)S(1)}, f32[8,1024]{1,0:T(8,128)S(1)}, u32[]{:S(2)}, u32[]{:S(2)}) collective-permute-start(f32[8,1024]{1,0:T(8,128)S(1)} %pad_maximum_fusion.1), channel_id=1, source_target_pairs={{0,16},{8,24},{16,0},{24,8},{1,17},{9,25},{17,1},{25,9},{2,18},{10... | collective-permute-start | bytes 98312 | tf_op jit(solution)/shard_map/ppermute | solution.py:35
  36.0 1.4 %collective-permute-start.13 = (bf16[64,1024]{1,0:T(8,128)(2,1)S(1)}, bf16[64,1024]{1,0:T(8,128)(2,1)S(1)}, u32[]{:S(2)}, u32[]{:S(2)}) collective-permute-start(bf16[64,1024]{1,0:T(8,128)(2,1)S(1)} %fusion.3), channel_id=1, source_target_pairs={{0,6},{1,7},{2,4},{3,5},{4,2},{5,3},{6,0},{7,1},{8,14},{9,15},{10,... | collective-permute-start | bytes 393224 | tf_op jit(solution)/shard_map/ppermute | solution.py:35
  37.9 1.5 %collective-permute-start.11 = (bf16[64,1024]{1,0:T(8,128)(2,1)S(1)}, bf16[64,1024]{1,0:T(8,128)(2,1)S(1)}, u32[]{:S(2)}, u32[]{:S(2)}) collective-permute-start(bf16[64,1024]{1,0:T(8,128)(2,1)S(1)} %fusion.3), channel_id=1, source_target_pairs={{0,2},{1,3},{2,0},{3,1},{4,6},{5,7},{6,4},{7,5},{8,10},{9,11},{10,... | collective-permute-start | bytes 393224 | tf_op jit(solution)/shard_map/ppermute | solution.py:35
  39.5 3.8 %collective-permute-done.13 = bf16[64,1024]{1,0:T(8,128)(2,1)S(1)} collective-permute-done((bf16[64,1024]{1,0:T(8,128)(2,1)S(1)}, bf16[64,1024]{1,0:T(8,128)(2,1)S(1)}, u32[]{:S(2)}, u32[]{:S(2)}) %collective-permute-start.13) | collective-permute-done | bytes 131104 | tf_op jit(solution)/shard_map/ppermute | solution.py:35
  43.3 1.9 %collective-permute-done.12 = bf16[64,1024]{1,0:T(8,128)(2,1)S(1)} collective-permute-done((bf16[64,1024]{1,0:T(8,128)(2,1)S(1)}, bf16[64,1024]{1,0:T(8,128)(2,1)S(1)}, u32[]{:S(2)}, u32[]{:S(2)}) %collective-permute-start.12) | collective-permute-done | bytes 131104 | tf_op jit(solution)/shard_map/ppermute | solution.py:35
  45.4 1.5 %collective-permute-done.15.other_ref = f32[64,1024]{1,0:T(8,128)S(1)} collective-permute-done((f32[64,1024]{1,0:T(8,128)S(1)}, f32[64,1024]{1,0:T(8,128)S(1)}, u32[]{:S(2)}, u32[]{:S(2)}) %collective-permute-start.15) | collective-permute-done | bytes 262176 | tf_op jit(solution)/shard_map/ppermute | solution.py:35
  46.9 2.0 %shard_map.64 = (f32[64,1024]{1,0:T(8,128)S(1)}, f32[64,1024]{1,0:T(8,128)S(1)}) custom-call(f32[64,1024]{1,0:T(8,128)S(1)} %get-tuple-element.65.own_ref, f32[64,1024]{1,0:T(8,128)S(1)} %collective-permute-done.15.other_ref, bf16[640,1024]{1,0:T(8,128)(2,1)S(1)} %get-tuple-element.66.window_ref, bf16[512,512]{1,0:T(8,128)(2,1)S(1)} %get-tuple-element.56.first_ref, ...), custom_call_target="tpu_custom_call" | custom-call | tf_op jit(solution)/shard_map/pallas_call | solution.py:529
  49.2 1.4 %collective-permute-done.16 = f32[64,1024]{1,0:T(8,128)S(1)} collective-permute-done((f32[64,1024]{1,0:T(8,128)S(1)}, f32[64,1024]{1,0:T(8,128)S(1)}, u32[]{:S(2)}, u32[]{:S(2)}) %collective-permute-start.16) | collective-permute-done | bytes 262176 | tf_op jit(solution)/shard_map/ppermute | solution.py:35
  50.6 1.4 %collective-permute-start.19 = (bf16[64,1024]{1,0:T(8,128)(2,1)S(1)}, bf16[64,1024]{1,0:T(8,128)(2,1)S(1)}, u32[]{:S(2)}, u32[]{:S(2)}) collective-permute-start(bf16[64,1024]{1,0:T(8,128)(2,1)S(1)} %fusion.5), channel_id=1, source_target_pairs={{0,6},{1,7},{2,4},{3,5},{4,2},{5,3},{6,0},{7,1},{8,14},{9,15},{10,... | collective-permute-start | bytes 393224 | tf_op jit(solution)/shard_map/ppermute | solution.py:35
  52.7 1.5 %collective-permute-start.17 = (bf16[64,1024]{1,0:T(8,128)(2,1)S(1)}, bf16[64,1024]{1,0:T(8,128)(2,1)S(1)}, u32[]{:S(2)}, u32[]{:S(2)}) collective-permute-start(bf16[64,1024]{1,0:T(8,128)(2,1)S(1)} %fusion.5), channel_id=1, source_target_pairs={{0,2},{1,3},{2,0},{3,1},{4,6},{5,7},{6,4},{7,5},{8,10},{9,11},{10,... | collective-permute-start | bytes 393224 | tf_op jit(solution)/shard_map/ppermute | solution.py:35
  54.2 3.8 %collective-permute-done.19 = bf16[64,1024]{1,0:T(8,128)(2,1)S(1)} collective-permute-done((bf16[64,1024]{1,0:T(8,128)(2,1)S(1)}, bf16[64,1024]{1,0:T(8,128)(2,1)S(1)}, u32[]{:S(2)}, u32[]{:S(2)}) %collective-permute-start.19) | collective-permute-done | bytes 131104 | tf_op jit(solution)/shard_map/ppermute | solution.py:35
  58.0 1.9 %collective-permute-done.18 = bf16[64,1024]{1,0:T(8,128)(2,1)S(1)} collective-permute-done((bf16[64,1024]{1,0:T(8,128)(2,1)S(1)}, bf16[64,1024]{1,0:T(8,128)(2,1)S(1)}, u32[]{:S(2)}, u32[]{:S(2)}) %collective-permute-start.18) | collective-permute-done | bytes 131104 | tf_op jit(solution)/shard_map/ppermute | solution.py:35
  60.1 1.5 %collective-permute-done.20.other_ref = f32[64,1024]{1,0:T(8,128)S(1)} collective-permute-done((f32[64,1024]{1,0:T(8,128)S(1)}, f32[64,1024]{1,0:T(8,128)S(1)}, u32[]{:S(2)}, u32[]{:S(2)}) %collective-permute-start.20) | collective-permute-done | bytes 262176 | tf_op jit(solution)/shard_map/ppermute | solution.py:35
  61.6 0.9 %shard_map.65 = (bf16[16,2048]{1,0:T(8,128)(2,1)S(1)}, bf16[16,2048]{1,0:T(8,128)(2,1)S(1)}, bf16[16,2048]{1,0:T(8,128)(2,1)S(1)}, bf16[16,2048]{1,0:T(8,128)(2,1)S(1)}, f32[1,1024]{1,0:T(1,128)S(1)}) custom-call(f32[64,1024]{1,0:T(8,128)S(1)} %add_multiply_fusion.own_ref, f32[64,1024]{1,0:T(8,128)S(1)} %collective-permute-done.20.other_ref, ...), custom_call_target="tpu_custom_call" | custom-call | tf_op jit(solution)/shard_map/pallas_call | solution.py:539
  62.5 1.6 %collective-permute-start.21 = (bf16[16,2048]{1,0:T(8,128)(2,1)S(1)}, bf16[16,2048]{1,0:T(8,128)(2,1)S(1)}, u32[]{:S(2)}, u32[]{:S(2)}) collective-permute-start(bf16[16,2048]{1,0:T(8,128)(2,1)S(1)} %get-tuple-element.72), channel_id=1, source_target_pairs={{0,8},{8,0},{16,24},{24,16},{1,9},{9,1},{17,25},{25,17},{2,10},{10... | collective-permute-start | bytes 196616 | tf_op jit(solution)/shard_map/ppermute | solution.py:35
  64.5 2.5 %collective-permute-start.23 = (bf16[16,2048]{1,0:T(8,128)(2,1)S(1)}, bf16[16,2048]{1,0:T(8,128)(2,1)S(1)}, u32[]{:S(2)}, u32[]{:S(2)}) collective-permute-start(bf16[16,2048]{1,0:T(8,128)(2,1)S(1)} %get-tuple-element.74), channel_id=1, source_target_pairs={{0,24},{8,16},{16,8},{24,0},{1,25},{9,17},{17,9},{25,1},{2,26},{10... | collective-permute-start | bytes 196616 | tf_op jit(solution)/shard_map/ppermute | solution.py:35
  67.0 5.0 %collective-permute-done.22.refs_2_ = bf16[16,2048]{1,0:T(8,128)(2,1)S(1)} collective-permute-done((bf16[16,2048]{1,0:T(8,128)(2,1)S(1)}, bf16[16,2048]{1,0:T(8,128)(2,1)S(1)}, u32[]{:S(2)}, u32[]{:S(2)}) %collective-permute-start.22) | collective-permute-done | bytes 65568 | tf_op jit(solution)/shard_map/ppermute | solution.py:35
  72.7 1.3 %collective-permute-done.24.other_ref = f32[16,1024]{1,0:T(8,128)S(1)} collective-permute-done((f32[16,1024]{1,0:T(8,128)S(1)}, f32[16,1024]{1,0:T(8,128)S(1)}, u32[]{:S(2)}, u32[]{:S(2)}) %collective-permute-start.24) | collective-permute-done | bytes 65568 | tf_op jit(solution)/shard_map/ppermute | solution.py:35
  (38 shorter events, 7.2 us)
Async XLA Ops:
  0.6 15.0 %copy-start = (s32[4,1024]{1,0:T(4,128)S(1)}, s32[4,1024]{1,0:T(4,128)}, u32[]{:S(2)}) copy-start(s32[4,1024]{1,0:T(4,128)} %param.7) | copy-start | bytes 49156
  1.9 1.4 %collective-permute-start = (f32[8,1024]{1,0:T(8,128)S(1)}, f32[8,1024]{1,0:T(8,128)S(1)}, u32[]{:S(2)}, u32[]{:S(2)}) collective-permute-start(f32[8,1024]{1,0:T(8,128)S(1)} %get-tuple-element.40.own_ref), channel_id=1, source_target_pairs={{0,1},{1,0},{2,3},{3,2},{4,5},{5,4},{6,7},{7,6},{8,9},{9,8},{10,11... | collective-permute-start | bytes 98312 | tf_op jit(solution)/shard_map/ppermute | solution.py:35
  3.4 5.7 %collective-permute-start.3 = (f32[8,1024]{1,0:T(8,128)S(1)}, f32[8,1024]{1,0:T(8,128)S(1)}, u32[]{:S(2)}, u32[]{:S(2)}) collective-permute-start(f32[8,1024]{1,0:T(8,128)S(1)} %shard_map.60.refs_0_), channel_id=1, source_target_pairs={{0,6},{1,7},{2,4},{3,5},{4,2},{5,3},{6,0},{7,1},{8,14},{9,15},{10,... | collective-permute-start | bytes 98312 | tf_op jit(solution)/shard_map/ppermute | solution.py:35
  7.2 3.9 %collective-permute-start.2 = (f32[8,1024]{1,0:T(8,128)S(1)}, f32[8,1024]{1,0:T(8,128)S(1)}, u32[]{:S(2)}, u32[]{:S(2)}) collective-permute-start(f32[8,1024]{1,0:T(8,128)S(1)} %shard_map.60.refs_0_), channel_id=1, source_target_pairs={{0,4},{1,5},{2,6},{3,7},{4,0},{5,1},{6,2},{7,3},{8,12},{9,13},{10,... | collective-permute-start | bytes 98312 | tf_op jit(solution)/shard_map/ppermute | solution.py:35
  7.7 3.9 %collective-permute-start.1 = (f32[8,1024]{1,0:T(8,128)S(1)}, f32[8,1024]{1,0:T(8,128)S(1)}, u32[]{:S(2)}, u32[]{:S(2)}) collective-permute-start(f32[8,1024]{1,0:T(8,128)S(1)} %shard_map.60.refs_0_), channel_id=1, source_target_pairs={{0,2},{1,3},{2,0},{3,1},{4,6},{5,7},{6,4},{7,5},{8,10},{9,11},{10,... | collective-permute-start | bytes 98312 | tf_op jit(solution)/shard_map/ppermute | solution.py:35
  15.6 1.6 %collective-permute-start.4 = (f32[64,1024]{1,0:T(8,128)S(1)}, f32[64,1024]{1,0:T(8,128)S(1)}, u32[]{:S(2)}, u32[]{:S(2)}) collective-permute-start(f32[64,1024]{1,0:T(8,128)S(1)} %get-tuple-element.45), channel_id=1, source_target_pairs={{0,1},{1,0},{2,3},{3,2},{4,5},{5,4},{6,7},{7,6},{8,9},{9,8},{10,11... | collective-permute-start | bytes 786440 | tf_op jit(solution)/shard_map/ppermute | solution.py:35
  17.2 7.4 %collective-permute-start.7 = (bf16[64,1024]{1,0:T(8,128)(2,1)S(1)}, bf16[64,1024]{1,0:T(8,128)(2,1)S(1)}, u32[]{:S(2)}, u32[]{:S(2)}) collective-permute-start(bf16[64,1024]{1,0:T(8,128)(2,1)S(1)} %add_convert_fusion), channel_id=1, source_target_pairs={{0,6},{1,7},{2,4},{3,5},{4,2},{5,3},{6,0},{7,1},{8,14},{9,15},{10,... | collective-permute-start | bytes 393224 | tf_op jit(solution)/shard_map/ppermute | solution.py:35
  18.7 7.8 %collective-permute-start.6 = (bf16[64,1024]{1,0:T(8,128)(2,1)S(1)}, bf16[64,1024]{1,0:T(8,128)(2,1)S(1)}, u32[]{:S(2)}, u32[]{:S(2)}) collective-permute-start(bf16[64,1024]{1,0:T(8,128)(2,1)S(1)} %add_convert_fusion), channel_id=1, source_target_pairs={{0,4},{1,5},{2,6},{3,7},{4,0},{5,1},{6,2},{7,3},{8,12},{9,13},{10,... | collective-permute-start | bytes 393224 | tf_op jit(solution)/shard_map/ppermute | solution.py:35
  18.8 7.8 %collective-permute-start.5 = (bf16[64,1024]{1,0:T(8,128)(2,1)S(1)}, bf16[64,1024]{1,0:T(8,128)(2,1)S(1)}, u32[]{:S(2)}, u32[]{:S(2)}) collective-permute-start(bf16[64,1024]{1,0:T(8,128)(2,1)S(1)} %add_convert_fusion), channel_id=1, source_target_pairs={{0,2},{1,3},{2,0},{3,1},{4,6},{5,7},{6,4},{7,5},{8,10},{9,11},{10,... | collective-permute-start | bytes 393224 | tf_op jit(solution)/shard_map/ppermute | solution.py:35
  20.7 3.7 %collective-permute-start.8 = (f32[4,1024]{1,0:T(4,128)S(1)}, f32[4,1024]{1,0:T(4,128)S(1)}, u32[]{:S(2)}, u32[]{:S(2)}) collective-permute-start(f32[4,1024]{1,0:T(4,128)S(1)} %convert_element_type.51), channel_id=1, source_target_pairs={{0,8},{8,0},{16,24},{24,16},{1,9},{9,1},{17,25},{25,17},{2,10},{10... | collective-permute-start | bytes 49160 | tf_op jit(solution)/shard_map/ppermute | solution.py:35
  26.7 2.9 %collective-permute-start.9 = (f32[64,1024]{1,0:T(8,128)S(1)}, f32[64,1024]{1,0:T(8,128)S(1)}, u32[]{:S(2)}, u32[]{:S(2)}) collective-permute-start(f32[64,1024]{1,0:T(8,128)S(1)} %broadcast_multiply_fusion.1.own_ref), channel_id=1, source_target_pairs={{0,1},{1,0},{2,3},{3,2},{4,5},{5,4},{6,7},{7,6},{8,9},{9,8},{10,11... | collective-permute-start | bytes 786440 | tf_op jit(solution)/shard_map/ppermute | solution.py:35
  31.6 1.7 %collective-permute-start.10 = (f32[64,1024]{1,0:T(8,128)S(1)}, f32[64,1024]{1,0:T(8,128)S(1)}, u32[]{:S(2)}, u32[]{:S(2)}) collective-permute-start(f32[64,1024]{1,0:T(8,128)S(1)} %get-tuple-element.61), channel_id=1, source_target_pairs={{0,1},{1,0},{2,3},{3,2},{4,5},{5,4},{6,7},{7,6},{8,9},{9,8},{10,11... | collective-permute-start | bytes 786440 | tf_op jit(solution)/shard_map/ppermute | solution.py:35
  33.3 6.1 %collective-permute-start.14 = (f32[8,1024]{1,0:T(8,128)S(1)}, f32[8,1024]{1,0:T(8,128)S(1)}, u32[]{:S(2)}, u32[]{:S(2)}) collective-permute-start(f32[8,1024]{1,0:T(8,128)S(1)} %pad_maximum_fusion.1), channel_id=1, source_target_pairs={{0,16},{8,24},{16,0},{24,8},{1,17},{9,25},{17,1},{25,9},{2,18},{10... | collective-permute-start | bytes 98312 | tf_op jit(solution)/shard_map/ppermute | solution.py:35
  36.0 7.3 %collective-permute-start.13 = (bf16[64,1024]{1,0:T(8,128)(2,1)S(1)}, bf16[64,1024]{1,0:T(8,128)(2,1)S(1)}, u32[]{:S(2)}, u32[]{:S(2)}) collective-permute-start(bf16[64,1024]{1,0:T(8,128)(2,1)S(1)} %fusion.3), channel_id=1, source_target_pairs={{0,6},{1,7},{2,4},{3,5},{4,2},{5,3},{6,0},{7,1},{8,14},{9,15},{10,... | collective-permute-start | bytes 393224 | tf_op jit(solution)/shard_map/ppermute | solution.py:35
  37.3 7.8 %collective-permute-start.12 = (bf16[64,1024]{1,0:T(8,128)(2,1)S(1)}, bf16[64,1024]{1,0:T(8,128)(2,1)S(1)}, u32[]{:S(2)}, u32[]{:S(2)}) collective-permute-start(bf16[64,1024]{1,0:T(8,128)(2,1)S(1)} %fusion.3), channel_id=1, source_target_pairs={{0,4},{1,5},{2,6},{3,7},{4,0},{5,1},{6,2},{7,3},{8,12},{9,13},{10,... | collective-permute-start | bytes 393224 | tf_op jit(solution)/shard_map/ppermute | solution.py:35
  37.9 7.2 %collective-permute-start.11 = (bf16[64,1024]{1,0:T(8,128)(2,1)S(1)}, bf16[64,1024]{1,0:T(8,128)(2,1)S(1)}, u32[]{:S(2)}, u32[]{:S(2)}) collective-permute-start(bf16[64,1024]{1,0:T(8,128)(2,1)S(1)} %fusion.3), channel_id=1, source_target_pairs={{0,2},{1,3},{2,0},{3,1},{4,6},{5,7},{6,4},{7,5},{8,10},{9,11},{10,... | collective-permute-start | bytes 393224 | tf_op jit(solution)/shard_map/ppermute | solution.py:35
  45.3 1.6 %collective-permute-start.15 = (f32[64,1024]{1,0:T(8,128)S(1)}, f32[64,1024]{1,0:T(8,128)S(1)}, u32[]{:S(2)}, u32[]{:S(2)}) collective-permute-start(f32[64,1024]{1,0:T(8,128)S(1)} %get-tuple-element.65.own_ref), channel_id=1, source_target_pairs={{0,1},{1,0},{2,3},{3,2},{4,5},{5,4},{6,7},{7,6},{8,9},{9,8},{10,11... | collective-permute-start | bytes 786440 | tf_op jit(solution)/shard_map/ppermute | solution.py:35
  49.0 1.6 %collective-permute-start.16 = (f32[64,1024]{1,0:T(8,128)S(1)}, f32[64,1024]{1,0:T(8,128)S(1)}, u32[]{:S(2)}, u32[]{:S(2)}) collective-permute-start(f32[64,1024]{1,0:T(8,128)S(1)} %get-tuple-element.69), channel_id=1, source_target_pairs={{0,1},{1,0},{2,3},{3,2},{4,5},{5,4},{6,7},{7,6},{8,9},{9,8},{10,11... | collective-permute-start | bytes 786440 | tf_op jit(solution)/shard_map/ppermute | solution.py:35
  50.6 7.4 %collective-permute-start.19 = (bf16[64,1024]{1,0:T(8,128)(2,1)S(1)}, bf16[64,1024]{1,0:T(8,128)(2,1)S(1)}, u32[]{:S(2)}, u32[]{:S(2)}) collective-permute-start(bf16[64,1024]{1,0:T(8,128)(2,1)S(1)} %fusion.5), channel_id=1, source_target_pairs={{0,6},{1,7},{2,4},{3,5},{4,2},{5,3},{6,0},{7,1},{8,14},{9,15},{10,... | collective-permute-start | bytes 393224 | tf_op jit(solution)/shard_map/ppermute | solution.py:35
  52.1 7.9 %collective-permute-start.18 = (bf16[64,1024]{1,0:T(8,128)(2,1)S(1)}, bf16[64,1024]{1,0:T(8,128)(2,1)S(1)}, u32[]{:S(2)}, u32[]{:S(2)}) collective-permute-start(bf16[64,1024]{1,0:T(8,128)(2,1)S(1)} %fusion.5), channel_id=1, source_target_pairs={{0,4},{1,5},{2,6},{3,7},{4,0},{5,1},{6,2},{7,3},{8,12},{9,13},{10,... | collective-permute-start | bytes 393224 | tf_op jit(solution)/shard_map/ppermute | solution.py:35
  52.7 7.3 %collective-permute-start.17 = (bf16[64,1024]{1,0:T(8,128)(2,1)S(1)}, bf16[64,1024]{1,0:T(8,128)(2,1)S(1)}, u32[]{:S(2)}, u32[]{:S(2)}) collective-permute-start(bf16[64,1024]{1,0:T(8,128)(2,1)S(1)} %fusion.5), channel_id=1, source_target_pairs={{0,2},{1,3},{2,0},{3,1},{4,6},{5,7},{6,4},{7,5},{8,10},{9,11},{10,... | collective-permute-start | bytes 393224 | tf_op jit(solution)/shard_map/ppermute | solution.py:35
  60.0 1.6 %collective-permute-start.20 = (f32[64,1024]{1,0:T(8,128)S(1)}, f32[64,1024]{1,0:T(8,128)S(1)}, u32[]{:S(2)}, u32[]{:S(2)}) collective-permute-start(f32[64,1024]{1,0:T(8,128)S(1)} %add_multiply_fusion.own_ref), channel_id=1, source_target_pairs={{0,1},{1,0},{2,3},{3,2},{4,5},{5,4},{6,7},{7,6},{8,9},{9,8},{10,11... | collective-permute-start | bytes 786440 | tf_op jit(solution)/shard_map/ppermute | solution.py:35
  62.5 4.5 %collective-permute-start.21 = (bf16[16,2048]{1,0:T(8,128)(2,1)S(1)}, bf16[16,2048]{1,0:T(8,128)(2,1)S(1)}, u32[]{:S(2)}, u32[]{:S(2)}) collective-permute-start(bf16[16,2048]{1,0:T(8,128)(2,1)S(1)} %get-tuple-element.72), channel_id=1, source_target_pairs={{0,8},{8,0},{16,24},{24,16},{1,9},{9,1},{17,25},{25,17},{2,10},{10... | collective-permute-start | bytes 196616 | tf_op jit(solution)/shard_map/ppermute | solution.py:35
  64.2 7.8 %collective-permute-start.22 = (bf16[16,2048]{1,0:T(8,128)(2,1)S(1)}, bf16[16,2048]{1,0:T(8,128)(2,1)S(1)}, u32[]{:S(2)}, u32[]{:S(2)}) collective-permute-start(bf16[16,2048]{1,0:T(8,128)(2,1)S(1)} %get-tuple-element.73), channel_id=1, source_target_pairs={{0,16},{8,24},{16,0},{24,8},{1,17},{9,25},{17,1},{25,9},{2,18},{10... | collective-permute-start | bytes 196616 | tf_op jit(solution)/shard_map/ppermute | solution.py:35
  64.5 7.5 %collective-permute-start.23 = (bf16[16,2048]{1,0:T(8,128)(2,1)S(1)}, bf16[16,2048]{1,0:T(8,128)(2,1)S(1)}, u32[]{:S(2)}, u32[]{:S(2)}) collective-permute-start(bf16[16,2048]{1,0:T(8,128)(2,1)S(1)} %get-tuple-element.74), channel_id=1, source_target_pairs={{0,24},{8,16},{16,8},{24,0},{1,25},{9,17},{17,9},{25,1},{2,26},{10... | collective-permute-start | bytes 196616 | tf_op jit(solution)/shard_map/ppermute | solution.py:35
  72.7 1.3 %collective-permute-start.24 = (f32[16,1024]{1,0:T(8,128)S(1)}, f32[16,1024]{1,0:T(8,128)S(1)}, u32[]{:S(2)}, u32[]{:S(2)}) collective-permute-start(f32[16,1024]{1,0:T(8,128)S(1)} %get-tuple-element.76.own_ref), channel_id=1, source_target_pairs={{0,1},{1,0},{2,3},{3,2},{4,5},{5,4},{6,7},{7,6},{8,9},{9,8},{10,11... | collective-permute-start | bytes 196616 | tf_op jit(solution)/shard_map/ppermute | solution.py:35

commit v2 on v1

--- a/solution.py
+++ b/solution.py
@@ -21,7 +21,7 @@
 
 MARGIN = 128
 HALO = 16
-CHUNKS = 4
+CHUNKS = 8
 
 
 VMEM = pl.BlockSpec(memory_space=pltpu.VMEM)
@@ -223,7 +223,13 @@
     core, _, _ = place()
     own, other = own_ref[...], other_ref[...]
     row = lax.broadcasted_iota(jnp.int32, own.shape, 0)
-    merged_ref[...] = jnp.where(row < 8 - LAGS, own + other, jnp.where(core == 1, own, other))
+    power = own + other
+    first = power.astype(merged_ref.dtype).astype(f32)
+    second = (power - first).astype(merged_ref.dtype).astype(f32)
+    pieces = jnp.where(row == 0, first, jnp.where(row == 1, second, power - first - second))
+    last = jnp.where(core == 1, own, other)
+    packet = jnp.where(row < 3, pieces, jnp.where(row < 8 - LAGS, 0.0, last))
+    merged_ref[...] = packet.astype(merged_ref.dtype)
 
 
 def preceding_rows(refs):
@@ -231,9 +237,9 @@
         return refs[0][...]
     core, chip, _ = place()
     other_ref, *chip_refs = refs
-    rows = chip_refs[0][...]
+    rows = chip_refs[0][...].astype(f32)
     if len(chip_refs) == 3:
-        rows = jnp.where(chip == 2, chip_refs[2][...], rows)
+        rows = jnp.where(chip == 2, chip_refs[2][...].astype(f32), rows)
     rows = jnp.where(core == 1, other_ref[...], rows)
     return jnp.where(core + chip > 0, rows, 0.0)
 
@@ -283,7 +289,8 @@
     ) = refs
     samples, channels = recording_ref.shape
     width = window_ref.shape[0]
-    power = paired_sum([ref[:1, :] for ref in part_refs])
+    packets = [ref[...].astype(f32) for ref in part_refs]
+    power = paired_sum([packet[:1] + packet[1:2] + packet[2:3] for packet in packets])
     scale = 1.0 / jnp.sqrt(power / count + epsilon)
     window_ref[:samples, :] = (recording_ref[...].astype(f32) * scale).astype(bf16)
     window_ref[samples : width - HALO, :] = jnp.zeros((width - HALO - samples, channels), bf16)
@@ -413,13 +420,20 @@
 
 
 def average_kernel(*refs):
-    *piece_refs, tally_ref, answer_ref, averaged_ref, residual_ref = refs
-    half, width = averaged_ref.shape
-    samples = residual_ref.shape[1]
-    added = paired_sum([ref[...].astype(f32) for ref in piece_refs])
-    averaged_ref[...] = added[:, :width] / jnp.maximum(tally_ref[...], 1.0)
-    residual_ref[:half, :] = answer_ref[:half, :] - added[:, width : width + samples]
-    residual_ref[half:, :] = answer_ref[half:, :] - added[:, width + samples :]
+    *piece_refs, tally_ref, averaged_ref = refs
+    width = averaged_ref.shape[1]
+    added = paired_sum([ref[:, :width].astype(f32) for ref in piece_refs])
+    averaged_ref[...] = added / jnp.maximum(tally_ref[...], 1.0)
+
+
+def residual_kernel(*refs):
+    *piece_refs, answer_ref, residual_ref = refs
+    half = answer_ref.shape[0] // 2
+    samples = answer_ref.shape[1]
+    start = piece_refs[0].shape[1] - 2 * samples
+    added = paired_sum([ref[:, start:].astype(f32) for ref in piece_refs])
+    residual_ref[:half, :] = answer_ref[:half, :] - added[:, :samples]
+    residual_ref[half:, :] = answer_ref[half:, :] - added[:, samples:]
 
 
 def last_kernel(own_ref, other_ref, averaged_ref):
@@ -470,8 +484,11 @@
         room=32,
     )(*[pltpu.with_memory_space_constraint(a, pltpu.HBM) for a in (starts, lengths, recording)])
     other = swapped(packet, "tm", 1)
-    merged = called(merge_kernel, shaped((8, channels)), [VMEM, VMEM])(packet, other)
-    if shards <= 8:
+    direct = shards <= 8
+    merged = called(
+        merge_kernel, shaped((8, channels), bf16 if direct else f32), [VMEM, VMEM]
+    )(packet, other)
+    if direct:
         powers = chip_parts(merged)
         halos = [other] + powers[1:]
     else:
@@ -543,11 +560,12 @@
         [pltpu.VMEM((rows, channels), f32), pltpu.VMEM((boots, boots, features), f32)],
     )(mean, swapped(mean, "tm", 1), window, support)
     pieces = pieces[:1] + [swapped(pieces[d], "boot", d) for d in range(1, boots)]
-    averaged, residual = called(
-        average_kernel,
-        (shaped((RESPONSE_COUNT // 2, features)), shaped((RESPONSE_COUNT, samples))),
-        [VMEM] * (boots + 2),
-    )(*pieces, tally, answer)
+    averaged = called(
+        average_kernel, shaped((RESPONSE_COUNT // 2, features)), [VMEM] * (boots + 1)
+    )(*pieces, tally)
+    residual = called(
+        residual_kernel, shaped((RESPONSE_COUNT, samples)), [VMEM] * (boots + 1)
+    )(*pieces, answer)
     averaged = called(last_kernel, shaped((RESPONSE_COUNT, features)), [VMEM] * 2)(
         averaged, swapped(averaged, "tm", 1)
     )

time: 74.7 us -> 74.2 us (level)
  waiting for transfers between devices: 33.8 us -> 32.9 us
    ppermute x25, waiting for transfers between devices: 33.8 us -> 32.9 us  [swapped(): return lax.ppermute(block, axis, [(i, i ^ distance) for i in devices])]
  transfers between devices with their start and end apart: 25 -> 25, of which waited for: 18 -> 18; matrix products, arithmetic and copies ran while one was open for 0% -> 0% of each run, Pallas kernels for 4% -> 5%
where the time goes in v2:
time: 74.2 us; the launch traced here: 74 us
  waiting for transfers between devices  32.9 us (44%)
  starting transfers between devices  25.4 us (34%)
  Pallas kernels  14.4 us (19%)
  between operations  0.78 us (1%)
    ppermute x25, waiting for transfers between devices, swapped(): return lax.ppermute(block, axis, [(i, i ^ distance) for i in devices])  32.9 us
    ppermute x25, starting transfers between devices, swapped(): return lax.ppermute(block, axis, [(i, i ^ distance) for i in devices])  25.4 us
    pallas_call x2, Pallas kernels, per_device(): called(next_kernel, (half_shape, half_shape) + (full_shape,) * going, [VM...  4.03 us
    pallas_call x1, Pallas kernels, per_device(): called(functools.partial(first_kernel, samples * shards, len(powers), len...  3.96 us
    pallas_call x1, Pallas kernels, per_device(): called(side_kernel, (full_shape, square, square), [VMEM] * 6, cost=pl.Cos...  2.77 us
  transfers between devices with their start and end apart: 25, of which 18 were waited for; matrix products, arithmetic and copies ran while one was open for 0% of the time, Pallas kernels for 5%

profile of v2, /device:TPU:0, one launch (start us, length us, event | category | flops | bytes accessed | tf_op | source)
XLA Modules:
  0.0 74.0 jit_solution(8415338091837392964)
XLA Ops:
  0.6 1.4 %shard_map.59 = (bf16[512,1024]{1,0:T(8,128)(2,1)S(1)}, f32[8,1024]{1,0:T(8,128)S(1)}, f32[1,640]{1,0:T(1,128)S(1)}, f32[512,128]{1,0:T(8,128)S(1)}) custom-call(s32[1,6]{1,0:T(1,128)} %starts_hbm.1, s32[1,6]{1,0:T(1,128)} %lengths_hbm.1, bf16[512,1024]{1,0:T(8,128)(2,1)} %source_ref.1), custom_call_target="tpu_custom_call" | custom-call | tf_op jit(solution)/shard_map/pallas_call | solution.py:470
  2.6 0.9 %collective-permute-done.other_ref.refs_4_ = f32[8,1024]{1,0:T(8,128)S(1)} collective-permute-done((f32[8,1024]{1,0:T(8,128)S(1)}, f32[8,1024]{1,0:T(8,128)S(1)}, u32[]{:S(2)}, u32[]{:S(2)}) %collective-permute-start) | collective-permute-done | bytes 32800 | tf_op jit(solution)/shard_map/ppermute | solution.py:35
  3.5 3.8 %collective-permute-start.3 = (bf16[8,1024]{1,0:T(8,128)(2,1)S(1)}, bf16[8,1024]{1,0:T(8,128)(2,1)S(1)}, u32[]{:S(2)}, u32[]{:S(2)}) collective-permute-start(bf16[8,1024]{1,0:T(8,128)(2,1)S(1)} %shard_map.60.refs_0_), channel_id=1, source_target_pairs={{0,6},{1,7},{2,4},{3,5},{4,2},{5,3},{6,0},{7,1},{8,14},{9,15},{10,... | collective-permute-start | bytes 49160 | tf_op jit(solution)/shard_map/ppermute | solution.py:35
  8.0 1.1 %collective-permute-done.3.refs_3_.refs_7_ = bf16[8,1024]{1,0:T(8,128)(2,1)S(1)} collective-permute-done((bf16[8,1024]{1,0:T(8,128)(2,1)S(1)}, bf16[8,1024]{1,0:T(8,128)(2,1)S(1)}, u32[]{:S(2)}, u32[]{:S(2)}) %collective-permute-start.3) | collective-permute-done | bytes 16416 | tf_op jit(solution)/shard_map/ppermute | solution.py:35
  9.0 2.0 %collective-permute-done.2.refs_2_.refs_6_ = bf16[8,1024]{1,0:T(8,128)(2,1)S(1)} collective-permute-done((bf16[8,1024]{1,0:T(8,128)(2,1)S(1)}, bf16[8,1024]{1,0:T(8,128)(2,1)S(1)}, u32[]{:S(2)}, u32[]{:S(2)}) %collective-permute-start.2) | collective-permute-done | bytes 16416 | tf_op jit(solution)/shard_map/ppermute | solution.py:35
  11.6 4.0 %shard_map.61 = (bf16[640,1024]{1,0:T(8,128)(2,1)S(1)}, bf16[512,512]{1,0:T(8,128)(2,1)S(1)}, bf16[512,512]{1,0:T(8,128)(2,1)S(1)}, f32[8,128]{1,0:T(8,128)S(1)}...) custom-call(bf16[8,1024]{1,0:T(8,128)(2,1)S(1)} %shard_map.60.refs_0_, ...), custom_call_target="tpu_custom_call" | custom-call | tf_op jit(solution)/shard_map/pallas_call | solution.py:499
  15.6 1.5 %collective-permute-done.4 = f32[64,1024]{1,0:T(8,128)S(1)} collective-permute-done((f32[64,1024]{1,0:T(8,128)S(1)}, f32[64,1024]{1,0:T(8,128)S(1)}, u32[]{:S(2)}, u32[]{:S(2)}) %collective-permute-start.4) | collective-permute-done | bytes 262176 | tf_op jit(solution)/shard_map/ppermute | solution.py:35
  17.2 1.6 %collective-permute-start.7 = (bf16[64,1024]{1,0:T(8,128)(2,1)S(1)}, bf16[64,1024]{1,0:T(8,128)(2,1)S(1)}, u32[]{:S(2)}, u32[]{:S(2)}) collective-permute-start(bf16[64,1024]{1,0:T(8,128)(2,1)S(1)} %add_convert_fusion), channel_id=1, source_target_pairs={{0,6},{1,7},{2,4},{3,5},{4,2},{5,3},{6,0},{7,1},{8,14},{9,15},{10,... | collective-permute-start | bytes 393224 | tf_op jit(solution)/shard_map/ppermute | solution.py:35
  18.8 1.9 %collective-permute-start.5 = (bf16[64,1024]{1,0:T(8,128)(2,1)S(1)}, bf16[64,1024]{1,0:T(8,128)(2,1)S(1)}, u32[]{:S(2)}, u32[]{:S(2)}) collective-permute-start(bf16[64,1024]{1,0:T(8,128)(2,1)S(1)} %add_convert_fusion), channel_id=1, source_target_pairs={{0,2},{1,3},{2,0},{3,1},{4,6},{5,7},{6,4},{7,5},{8,10},{9,11},{10,... | collective-permute-start | bytes 393224 | tf_op jit(solution)/shard_map/ppermute | solution.py:35
  20.7 1.6 %collective-permute-start.8 = (f32[4,1024]{1,0:T(4,128)S(1)}, f32[4,1024]{1,0:T(4,128)S(1)}, u32[]{:S(2)}, u32[]{:S(2)}) collective-permute-start(f32[4,1024]{1,0:T(4,128)S(1)} %convert_element_type.51), channel_id=1, source_target_pairs={{0,8},{8,0},{16,24},{24,16},{1,9},{9,1},{17,25},{25,17},{2,10},{10... | collective-permute-start | bytes 49160 | tf_op jit(solution)/shard_map/ppermute | solution.py:35
  22.3 2.2 %collective-permute-done.8 = f32[4,1024]{1,0:T(4,128)S(1)} collective-permute-done((f32[4,1024]{1,0:T(4,128)S(1)}, f32[4,1024]{1,0:T(4,128)S(1)}, u32[]{:S(2)}, u32[]{:S(2)}) %collective-permute-start.8) | collective-permute-done | bytes 16416 | tf_op jit(solution)/shard_map/ppermute | solution.py:35
  24.5 2.0 %collective-permute-done.6 = bf16[64,1024]{1,0:T(8,128)(2,1)S(1)} collective-permute-done((bf16[64,1024]{1,0:T(8,128)(2,1)S(1)}, bf16[64,1024]{1,0:T(8,128)(2,1)S(1)}, u32[]{:S(2)}, u32[]{:S(2)}) %collective-permute-start.6) | collective-permute-done | bytes 131104 | tf_op jit(solution)/shard_map/ppermute | solution.py:35
  26.7 2.8 %shard_map.62 = (f32[128,1024]{1,0:T(8,128)S(1)}, bf16[512,512]{1,0:T(8,128)(2,1)S(1)}, bf16[512,512]{1,0:T(8,128)(2,1)S(1)}) custom-call(bf16[640,1024]{1,0:T(8,128)(2,1)S(1)} %get-tuple-element.64.window_ref, bf16[512,512]{1,0:T(8,128)(2,1)S(1)} %get-tuple-element.50.high_ref, bf16[512,512]{1,0:T(8,128)(2,1)S(1)} %get-tuple-element.51.low_ref, ...), custom_call_target="tpu_custom_call" | custom-call | flops 1879048192 | bytes 1048576 | tf_op jit(solution)/shard_map/pallas_call | solution.py:536
  29.5 2.0 %shard_map.63 = (f32[64,1024]{1,0:T(8,128)S(1)}, f32[64,1024]{1,0:T(8,128)S(1)}, f32[128,1024]{1,0:T(8,128)S(1)}) custom-call(f32[64,1024]{1,0:T(8,128)S(1)} %broadcast_multiply_fusion.1.own_ref, f32[64,1024]{1,0:T(8,128)S(1)} %collective-permute-done.9.other_ref, bf16[640,1024]{1,0:T(8,128)(2,1)S(1)} %get-tuple-element.64.window_ref, ...), custom_call_target="tpu_custom_call" | custom-call | tf_op jit(solution)/shard_map/pallas_call | solution.py:546
  32.1 1.2 %collective-permute-done.10 = f32[64,1024]{1,0:T(8,128)S(1)} collective-permute-done((f32[64,1024]{1,0:T(8,128)S(1)}, f32[64,1024]{1,0:T(8,128)S(1)}, u32[]{:S(2)}, u32[]{:S(2)}) %collective-permute-start.10) | collective-permute-done | bytes 262176 | tf_op jit(solution)/shard_map/ppermute | solution.py:35
  33.3 2.6 %collective-permute-start.14 = (f32[8,1024]{1,0:T(8,128)S(1)}, f32[8,1024]{1,0:T(8,128)S(1)}, u32[]{:S(2)}, u32[]{:S(2)}) collective-permute-start(f32[8,1024]{1,0:T(8,128)S(1)} %pad_maximum_fusion.1), channel_id=1, source_target_pairs={{0,16},{8,24},{16,0},{24,8},{1,17},{9,25},{17,1},{25,9},{2,18},{10... | collective-permute-start | bytes 98312 | tf_op jit(solution)/shard_map/ppermute | solution.py:35
  36.0 1.4 %collective-permute-start.13 = (bf16[64,1024]{1,0:T(8,128)(2,1)S(1)}, bf16[64,1024]{1,0:T(8,128)(2,1)S(1)}, u32[]{:S(2)}, u32[]{:S(2)}) collective-permute-start(bf16[64,1024]{1,0:T(8,128)(2,1)S(1)} %fusion.3), channel_id=1, source_target_pairs={{0,6},{1,7},{2,4},{3,5},{4,2},{5,3},{6,0},{7,1},{8,14},{9,15},{10,... | collective-permute-start | bytes 393224 | tf_op jit(solution)/shard_map/ppermute | solution.py:35
  37.9 1.5 %collective-permute-start.11 = (bf16[64,1024]{1,0:T(8,128)(2,1)S(1)}, bf16[64,1024]{1,0:T(8,128)(2,1)S(1)}, u32[]{:S(2)}, u32[]{:S(2)}) collective-permute-start(bf16[64,1024]{1,0:T(8,128)(2,1)S(1)} %fusion.3), channel_id=1, source_target_pairs={{0,2},{1,3},{2,0},{3,1},{4,6},{5,7},{6,4},{7,5},{8,10},{9,11},{10,... | collective-permute-start | bytes 393224 | tf_op jit(solution)/shard_map/ppermute | solution.py:35
  39.5 3.8 %collective-permute-done.13 = bf16[64,1024]{1,0:T(8,128)(2,1)S(1)} collective-permute-done((bf16[64,1024]{1,0:T(8,128)(2,1)S(1)}, bf16[64,1024]{1,0:T(8,128)(2,1)S(1)}, u32[]{:S(2)}, u32[]{:S(2)}) %collective-permute-start.13) | collective-permute-done | bytes 131104 | tf_op jit(solution)/shard_map/ppermute | solution.py:35
  43.3 1.9 %collective-permute-done.12 = bf16[64,1024]{1,0:T(8,128)(2,1)S(1)} collective-permute-done((bf16[64,1024]{1,0:T(8,128)(2,1)S(1)}, bf16[64,1024]{1,0:T(8,128)(2,1)S(1)}, u32[]{:S(2)}, u32[]{:S(2)}) %collective-permute-start.12) | collective-permute-done | bytes 131104 | tf_op jit(solution)/shard_map/ppermute | solution.py:35
  45.4 1.5 %collective-permute-done.15.other_ref = f32[64,1024]{1,0:T(8,128)S(1)} collective-permute-done((f32[64,1024]{1,0:T(8,128)S(1)}, f32[64,1024]{1,0:T(8,128)S(1)}, u32[]{:S(2)}, u32[]{:S(2)}) %collective-permute-start.15) | collective-permute-done | bytes 262176 | tf_op jit(solution)/shard_map/ppermute | solution.py:35
  46.9 2.0 %shard_map.64 = (f32[64,1024]{1,0:T(8,128)S(1)}, f32[64,1024]{1,0:T(8,128)S(1)}) custom-call(f32[64,1024]{1,0:T(8,128)S(1)} %get-tuple-element.63.own_ref, f32[64,1024]{1,0:T(8,128)S(1)} %collective-permute-done.15.other_ref, bf16[640,1024]{1,0:T(8,128)(2,1)S(1)} %get-tuple-element.64.window_ref, bf16[512,512]{1,0:T(8,128)(2,1)S(1)} %get-tuple-element.54.first_ref, ...), custom_call_target="tpu_custom_call" | custom-call | tf_op jit(solution)/shard_map/pallas_call | solution.py:546
  49.2 1.4 %collective-permute-done.16 = f32[64,1024]{1,0:T(8,128)S(1)} collective-permute-done((f32[64,1024]{1,0:T(8,128)S(1)}, f32[64,1024]{1,0:T(8,128)S(1)}, u32[]{:S(2)}, u32[]{:S(2)}) %collective-permute-start.16) | collective-permute-done | bytes 262176 | tf_op jit(solution)/shard_map/ppermute | solution.py:35
  50.6 1.4 %collective-permute-start.19 = (bf16[64,1024]{1,0:T(8,128)(2,1)S(1)}, bf16[64,1024]{1,0:T(8,128)(2,1)S(1)}, u32[]{:S(2)}, u32[]{:S(2)}) collective-permute-start(bf16[64,1024]{1,0:T(8,128)(2,1)S(1)} %fusion.5), channel_id=1, source_target_pairs={{0,6},{1,7},{2,4},{3,5},{4,2},{5,3},{6,0},{7,1},{8,14},{9,15},{10,... | collective-permute-start | bytes 393224 | tf_op jit(solution)/shard_map/ppermute | solution.py:35
  52.7 1.5 %collective-permute-start.17 = (bf16[64,1024]{1,0:T(8,128)(2,1)S(1)}, bf16[64,1024]{1,0:T(8,128)(2,1)S(1)}, u32[]{:S(2)}, u32[]{:S(2)}) collective-permute-start(bf16[64,1024]{1,0:T(8,128)(2,1)S(1)} %fusion.5), channel_id=1, source_target_pairs={{0,2},{1,3},{2,0},{3,1},{4,6},{5,7},{6,4},{7,5},{8,10},{9,11},{10,... | collective-permute-start | bytes 393224 | tf_op jit(solution)/shard_map/ppermute | solution.py:35
  54.2 3.8 %collective-permute-done.19 = bf16[64,1024]{1,0:T(8,128)(2,1)S(1)} collective-permute-done((bf16[64,1024]{1,0:T(8,128)(2,1)S(1)}, bf16[64,1024]{1,0:T(8,128)(2,1)S(1)}, u32[]{:S(2)}, u32[]{:S(2)}) %collective-permute-start.19) | collective-permute-done | bytes 131104 | tf_op jit(solution)/shard_map/ppermute | solution.py:35
  58.0 1.9 %collective-permute-done.18 = bf16[64,1024]{1,0:T(8,128)(2,1)S(1)} collective-permute-done((bf16[64,1024]{1,0:T(8,128)(2,1)S(1)}, bf16[64,1024]{1,0:T(8,128)(2,1)S(1)}, u32[]{:S(2)}, u32[]{:S(2)}) %collective-permute-start.18) | collective-permute-done | bytes 131104 | tf_op jit(solution)/shard_map/ppermute | solution.py:35
  60.1 1.5 %collective-permute-done.20.other_ref = f32[64,1024]{1,0:T(8,128)S(1)} collective-permute-done((f32[64,1024]{1,0:T(8,128)S(1)}, f32[64,1024]{1,0:T(8,128)S(1)}, u32[]{:S(2)}, u32[]{:S(2)}) %collective-permute-start.20) | collective-permute-done | bytes 262176 | tf_op jit(solution)/shard_map/ppermute | solution.py:35
  61.6 0.9 %shard_map.65 = (bf16[16,2048]{1,0:T(8,128)(2,1)S(1)}, bf16[16,2048]{1,0:T(8,128)(2,1)S(1)}, bf16[16,2048]{1,0:T(8,128)(2,1)S(1)}, bf16[16,2048]{1,0:T(8,128)(2,1)S(1)}, f32[1,1024]{1,0:T(1,128)S(1)}) custom-call(f32[64,1024]{1,0:T(8,128)S(1)} %add_multiply_fusion.own_ref, f32[64,1024]{1,0:T(8,128)S(1)} %collective-permute-done.20.other_ref, ...), custom_call_target="tpu_custom_call" | custom-call | tf_op jit(solution)/shard_map/pallas_call | solution.py:556
  62.5 1.6 %collective-permute-start.21 = (bf16[16,2048]{1,0:T(8,128)(2,1)S(1)}, bf16[16,2048]{1,0:T(8,128)(2,1)S(1)}, u32[]{:S(2)}, u32[]{:S(2)}) collective-permute-start(bf16[16,2048]{1,0:T(8,128)(2,1)S(1)} %get-tuple-element.70), channel_id=1, source_target_pairs={{0,8},{8,0},{16,24},{24,16},{1,9},{9,1},{17,25},{25,17},{2,10},{10... | collective-permute-start | bytes 196616 | tf_op jit(solution)/shard_map/ppermute | solution.py:35
  64.5 2.5 %collective-permute-start.23 = (bf16[16,2048]{1,0:T(8,128)(2,1)S(1)}, bf16[16,2048]{1,0:T(8,128)(2,1)S(1)}, u32[]{:S(2)}, u32[]{:S(2)}) collective-permute-start(bf16[16,2048]{1,0:T(8,128)(2,1)S(1)} %get-tuple-element.72), channel_id=1, source_target_pairs={{0,24},{8,16},{16,8},{24,0},{1,25},{9,17},{17,9},{25,1},{2,26},{10... | collective-permute-start | bytes 196616 | tf_op jit(solution)/shard_map/ppermute | solution.py:35
  67.0 5.0 %collective-permute-done.22.refs_2_ = bf16[16,2048]{1,0:T(8,128)(2,1)S(1)} collective-permute-done((bf16[16,2048]{1,0:T(8,128)(2,1)S(1)}, bf16[16,2048]{1,0:T(8,128)(2,1)S(1)}, u32[]{:S(2)}, u32[]{:S(2)}) %collective-permute-start.22) | collective-permute-done | bytes 65568 | tf_op jit(solution)/shard_map/ppermute | solution.py:35
  (39 shorter events, 7.1 us)
Async XLA Ops:
  0.6 15.0 %copy-start = (s32[4,1024]{1,0:T(4,128)S(1)}, s32[4,1024]{1,0:T(4,128)}, u32[]{:S(2)}) copy-start(s32[4,1024]{1,0:T(4,128)} %param.7) | copy-start | bytes 49156
  2.0 1.4 %collective-permute-start = (f32[8,1024]{1,0:T(8,128)S(1)}, f32[8,1024]{1,0:T(8,128)S(1)}, u32[]{:S(2)}, u32[]{:S(2)}) collective-permute-start(f32[8,1024]{1,0:T(8,128)S(1)} %get-tuple-element.38.own_ref), channel_id=1, source_target_pairs={{0,1},{1,0},{2,3},{3,2},{4,5},{5,4},{6,7},{7,6},{8,9},{9,8},{10,11... | collective-permute-start | bytes 98312 | tf_op jit(solution)/shard_map/ppermute | solution.py:35
  3.5 5.6 %collective-permute-start.3 = (bf16[8,1024]{1,0:T(8,128)(2,1)S(1)}, bf16[8,1024]{1,0:T(8,128)(2,1)S(1)}, u32[]{:S(2)}, u32[]{:S(2)}) collective-permute-start(bf16[8,1024]{1,0:T(8,128)(2,1)S(1)} %shard_map.60.refs_0_), channel_id=1, source_target_pairs={{0,6},{1,7},{2,4},{3,5},{4,2},{5,3},{6,0},{7,1},{8,14},{9,15},{10,... | collective-permute-start | bytes 49160 | tf_op jit(solution)/shard_map/ppermute | solution.py:35
  7.3 3.7 %collective-permute-start.2 = (bf16[8,1024]{1,0:T(8,128)(2,1)S(1)}, bf16[8,1024]{1,0:T(8,128)(2,1)S(1)}, u32[]{:S(2)}, u32[]{:S(2)}) collective-permute-start(bf16[8,1024]{1,0:T(8,128)(2,1)S(1)} %shard_map.60.refs_0_), channel_id=1, source_target_pairs={{0,4},{1,5},{2,6},{3,7},{4,0},{5,1},{6,2},{7,3},{8,12},{9,13},{10,... | collective-permute-start | bytes 49160 | tf_op jit(solution)/shard_map/ppermute | solution.py:35
  7.8 3.7 %collective-permute-start.1 = (bf16[8,1024]{1,0:T(8,128)(2,1)S(1)}, bf16[8,1024]{1,0:T(8,128)(2,1)S(1)}, u32[]{:S(2)}, u32[]{:S(2)}) collective-permute-start(bf16[8,1024]{1,0:T(8,128)(2,1)S(1)} %shard_map.60.refs_0_), channel_id=1, source_target_pairs={{0,2},{1,3},{2,0},{3,1},{4,6},{5,7},{6,4},{7,5},{8,10},{9,11},{10,... | collective-permute-start | bytes 49160 | tf_op jit(solution)/shard_map/ppermute | solution.py:35
  15.5 1.6 %collective-permute-start.4 = (f32[64,1024]{1,0:T(8,128)S(1)}, f32[64,1024]{1,0:T(8,128)S(1)}, u32[]{:S(2)}, u32[]{:S(2)}) collective-permute-start(f32[64,1024]{1,0:T(8,128)S(1)} %get-tuple-element.43), channel_id=1, source_target_pairs={{0,1},{1,0},{2,3},{3,2},{4,5},{5,4},{6,7},{7,6},{8,9},{9,8},{10,11... | collective-permute-start | bytes 786440 | tf_op jit(solution)/shard_map/ppermute | solution.py:35
  17.2 7.4 %collective-permute-start.7 = (bf16[64,1024]{1,0:T(8,128)(2,1)S(1)}, bf16[64,1024]{1,0:T(8,128)(2,1)S(1)}, u32[]{:S(2)}, u32[]{:S(2)}) collective-permute-start(bf16[64,1024]{1,0:T(8,128)(2,1)S(1)} %add_convert_fusion), channel_id=1, source_target_pairs={{0,6},{1,7},{2,4},{3,5},{4,2},{5,3},{6,0},{7,1},{8,14},{9,15},{10,... | collective-permute-start | bytes 393224 | tf_op jit(solution)/shard_map/ppermute | solution.py:35
  18.7 7.8 %collective-permute-start.6 = (bf16[64,1024]{1,0:T(8,128)(2,1)S(1)}, bf16[64,1024]{1,0:T(8,128)(2,1)S(1)}, u32[]{:S(2)}, u32[]{:S(2)}) collective-permute-start(bf16[64,1024]{1,0:T(8,128)(2,1)S(1)} %add_convert_fusion), channel_id=1, source_target_pairs={{0,4},{1,5},{2,6},{3,7},{4,0},{5,1},{6,2},{7,3},{8,12},{9,13},{10,... | collective-permute-start | bytes 393224 | tf_op jit(solution)/shard_map/ppermute | solution.py:35
  18.8 7.8 %collective-permute-start.5 = (bf16[64,1024]{1,0:T(8,128)(2,1)S(1)}, bf16[64,1024]{1,0:T(8,128)(2,1)S(1)}, u32[]{:S(2)}, u32[]{:S(2)}) collective-permute-start(bf16[64,1024]{1,0:T(8,128)(2,1)S(1)} %add_convert_fusion), channel_id=1, source_target_pairs={{0,2},{1,3},{2,0},{3,1},{4,6},{5,7},{6,4},{7,5},{8,10},{9,11},{10,... | collective-permute-start | bytes 393224 | tf_op jit(solution)/shard_map/ppermute | solution.py:35
  20.7 3.7 %collective-permute-start.8 = (f32[4,1024]{1,0:T(4,128)S(1)}, f32[4,1024]{1,0:T(4,128)S(1)}, u32[]{:S(2)}, u32[]{:S(2)}) collective-permute-start(f32[4,1024]{1,0:T(4,128)S(1)} %convert_element_type.51), channel_id=1, source_target_pairs={{0,8},{8,0},{16,24},{24,16},{1,9},{9,1},{17,25},{25,17},{2,10},{10... | collective-permute-start | bytes 49160 | tf_op jit(solution)/shard_map/ppermute | solution.py:35
  26.7 2.9 %collective-permute-start.9 = (f32[64,1024]{1,0:T(8,128)S(1)}, f32[64,1024]{1,0:T(8,128)S(1)}, u32[]{:S(2)}, u32[]{:S(2)}) collective-permute-start(f32[64,1024]{1,0:T(8,128)S(1)} %broadcast_multiply_fusion.1.own_ref), channel_id=1, source_target_pairs={{0,1},{1,0},{2,3},{3,2},{4,5},{5,4},{6,7},{7,6},{8,9},{9,8},{10,11... | collective-permute-start | bytes 786440 | tf_op jit(solution)/shard_map/ppermute | solution.py:35
  31.5 1.7 %collective-permute-start.10 = (f32[64,1024]{1,0:T(8,128)S(1)}, f32[64,1024]{1,0:T(8,128)S(1)}, u32[]{:S(2)}, u32[]{:S(2)}) collective-permute-start(f32[64,1024]{1,0:T(8,128)S(1)} %get-tuple-element.59), channel_id=1, source_target_pairs={{0,1},{1,0},{2,3},{3,2},{4,5},{5,4},{6,7},{7,6},{8,9},{9,8},{10,11... | collective-permute-start | bytes 786440 | tf_op jit(solution)/shard_map/ppermute | solution.py:35
  33.3 6.1 %collective-permute-start.14 = (f32[8,1024]{1,0:T(8,128)S(1)}, f32[8,1024]{1,0:T(8,128)S(1)}, u32[]{:S(2)}, u32[]{:S(2)}) collective-permute-start(f32[8,1024]{1,0:T(8,128)S(1)} %pad_maximum_fusion.1), channel_id=1, source_target_pairs={{0,16},{8,24},{16,0},{24,8},{1,17},{9,25},{17,1},{25,9},{2,18},{10... | collective-permute-start | bytes 98312 | tf_op jit(solution)/shard_map/ppermute | solution.py:35
  36.0 7.3 %collective-permute-start.13 = (bf16[64,1024]{1,0:T(8,128)(2,1)S(1)}, bf16[64,1024]{1,0:T(8,128)(2,1)S(1)}, u32[]{:S(2)}, u32[]{:S(2)}) collective-permute-start(bf16[64,1024]{1,0:T(8,128)(2,1)S(1)} %fusion.3), channel_id=1, source_target_pairs={{0,6},{1,7},{2,4},{3,5},{4,2},{5,3},{6,0},{7,1},{8,14},{9,15},{10,... | collective-permute-start | bytes 393224 | tf_op jit(solution)/shard_map/ppermute | solution.py:35
  37.3 7.8 %collective-permute-start.12 = (bf16[64,1024]{1,0:T(8,128)(2,1)S(1)}, bf16[64,1024]{1,0:T(8,128)(2,1)S(1)}, u32[]{:S(2)}, u32[]{:S(2)}) collective-permute-start(bf16[64,1024]{1,0:T(8,128)(2,1)S(1)} %fusion.3), channel_id=1, source_target_pairs={{0,4},{1,5},{2,6},{3,7},{4,0},{5,1},{6,2},{7,3},{8,12},{9,13},{10,... | collective-permute-start | bytes 393224 | tf_op jit(solution)/shard_map/ppermute | solution.py:35
  37.9 7.2 %collective-permute-start.11 = (bf16[64,1024]{1,0:T(8,128)(2,1)S(1)}, bf16[64,1024]{1,0:T(8,128)(2,1)S(1)}, u32[]{:S(2)}, u32[]{:S(2)}) collective-permute-start(bf16[64,1024]{1,0:T(8,128)(2,1)S(1)} %fusion.3), channel_id=1, source_target_pairs={{0,2},{1,3},{2,0},{3,1},{4,6},{5,7},{6,4},{7,5},{8,10},{9,11},{10,... | collective-permute-start | bytes 393224 | tf_op jit(solution)/shard_map/ppermute | solution.py:35
  45.3 1.6 %collective-permute-start.15 = (f32[64,1024]{1,0:T(8,128)S(1)}, f32[64,1024]{1,0:T(8,128)S(1)}, u32[]{:S(2)}, u32[]{:S(2)}) collective-permute-start(f32[64,1024]{1,0:T(8,128)S(1)} %get-tuple-element.63.own_ref), channel_id=1, source_target_pairs={{0,1},{1,0},{2,3},{3,2},{4,5},{5,4},{6,7},{7,6},{8,9},{9,8},{10,11... | collective-permute-start | bytes 786440 | tf_op jit(solution)/shard_map/ppermute | solution.py:35
  49.0 1.6 %collective-permute-start.16 = (f32[64,1024]{1,0:T(8,128)S(1)}, f32[64,1024]{1,0:T(8,128)S(1)}, u32[]{:S(2)}, u32[]{:S(2)}) collective-permute-start(f32[64,1024]{1,0:T(8,128)S(1)} %get-tuple-element.67), channel_id=1, source_target_pairs={{0,1},{1,0},{2,3},{3,2},{4,5},{5,4},{6,7},{7,6},{8,9},{9,8},{10,11... | collective-permute-start | bytes 786440 | tf_op jit(solution)/shard_map/ppermute | solution.py:35
  50.6 7.4 %collective-permute-start.19 = (bf16[64,1024]{1,0:T(8,128)(2,1)S(1)}, bf16[64,1024]{1,0:T(8,128)(2,1)S(1)}, u32[]{:S(2)}, u32[]{:S(2)}) collective-permute-start(bf16[64,1024]{1,0:T(8,128)(2,1)S(1)} %fusion.5), channel_id=1, source_target_pairs={{0,6},{1,7},{2,4},{3,5},{4,2},{5,3},{6,0},{7,1},{8,14},{9,15},{10,... | collective-permute-start | bytes 393224 | tf_op jit(solution)/shard_map/ppermute | solution.py:35
  52.1 7.9 %collective-permute-start.18 = (bf16[64,1024]{1,0:T(8,128)(2,1)S(1)}, bf16[64,1024]{1,0:T(8,128)(2,1)S(1)}, u32[]{:S(2)}, u32[]{:S(2)}) collective-permute-start(bf16[64,1024]{1,0:T(8,128)(2,1)S(1)} %fusion.5), channel_id=1, source_target_pairs={{0,4},{1,5},{2,6},{3,7},{4,0},{5,1},{6,2},{7,3},{8,12},{9,13},{10,... | collective-permute-start | bytes 393224 | tf_op jit(solution)/shard_map/ppermute | solution.py:35
  52.7 7.3 %collective-permute-start.17 = (bf16[64,1024]{1,0:T(8,128)(2,1)S(1)}, bf16[64,1024]{1,0:T(8,128)(2,1)S(1)}, u32[]{:S(2)}, u32[]{:S(2)}) collective-permute-start(bf16[64,1024]{1,0:T(8,128)(2,1)S(1)} %fusion.5), channel_id=1, source_target_pairs={{0,2},{1,3},{2,0},{3,1},{4,6},{5,7},{6,4},{7,5},{8,10},{9,11},{10,... | collective-permute-start | bytes 393224 | tf_op jit(solution)/shard_map/ppermute | solution.py:35
  60.0 1.6 %collective-permute-start.20 = (f32[64,1024]{1,0:T(8,128)S(1)}, f32[64,1024]{1,0:T(8,128)S(1)}, u32[]{:S(2)}, u32[]{:S(2)}) collective-permute-start(f32[64,1024]{1,0:T(8,128)S(1)} %add_multiply_fusion.own_ref), channel_id=1, source_target_pairs={{0,1},{1,0},{2,3},{3,2},{4,5},{5,4},{6,7},{7,6},{8,9},{9,8},{10,11... | collective-permute-start | bytes 786440 | tf_op jit(solution)/shard_map/ppermute | solution.py:35
  62.5 4.5 %collective-permute-start.21 = (bf16[16,2048]{1,0:T(8,128)(2,1)S(1)}, bf16[16,2048]{1,0:T(8,128)(2,1)S(1)}, u32[]{:S(2)}, u32[]{:S(2)}) collective-permute-start(bf16[16,2048]{1,0:T(8,128)(2,1)S(1)} %get-tuple-element.70), channel_id=1, source_target_pairs={{0,8},{8,0},{16,24},{24,16},{1,9},{9,1},{17,25},{25,17},{2,10},{10... | collective-permute-start | bytes 196616 | tf_op jit(solution)/shard_map/ppermute | solution.py:35
  64.2 7.8 %collective-permute-start.22 = (bf16[16,2048]{1,0:T(8,128)(2,1)S(1)}, bf16[16,2048]{1,0:T(8,128)(2,1)S(1)}, u32[]{:S(2)}, u32[]{:S(2)}) collective-permute-start(bf16[16,2048]{1,0:T(8,128)(2,1)S(1)} %get-tuple-element.71), channel_id=1, source_target_pairs={{0,16},{8,24},{16,0},{24,8},{1,17},{9,25},{17,1},{25,9},{2,18},{10... | collective-permute-start | bytes 196616 | tf_op jit(solution)/shard_map/ppermute | solution.py:35
  64.5 7.5 %collective-permute-start.23 = (bf16[16,2048]{1,0:T(8,128)(2,1)S(1)}, bf16[16,2048]{1,0:T(8,128)(2,1)S(1)}, u32[]{:S(2)}, u32[]{:S(2)}) collective-permute-start(bf16[16,2048]{1,0:T(8,128)(2,1)S(1)} %get-tuple-element.72), channel_id=1, source_target_pairs={{0,24},{8,16},{16,8},{24,0},{1,25},{9,17},{17,9},{25,1},{2,26},{10... | collective-permute-start | bytes 196616 | tf_op jit(solution)/shard_map/ppermute | solution.py:35
  72.0 1.3 %collective-permute-start.24 = (f32[16,1024]{1,0:T(8,128)S(1)}, f32[16,1024]{1,0:T(8,128)S(1)}, u32[]{:S(2)}, u32[]{:S(2)}) collective-permute-start(f32[16,1024]{1,0:T(8,128)S(1)} %shard_map.66.own_ref), channel_id=1, source_target_pairs={{0,1},{1,0},{2,3},{3,2},{4,5},{5,4},{6,7},{7,6},{8,9},{9,8},{10,11... | collective-permute-start | bytes 196616 | tf_op jit(solution)/shard_map/ppermute | solution.py:35

commit v3 on v2

--- a/solution.py
+++ b/solution.py
@@ -21,7 +21,7 @@
 
 MARGIN = 128
 HALO = 16
-CHUNKS = 8
+CHUNKS = 4
 
 
 VMEM = pl.BlockSpec(memory_space=pltpu.VMEM)
@@ -255,9 +255,11 @@
     count, rows, lanes = pairs_ref.shape
     samples = rows - HALO
     left = jnp.concatenate([window_ref[width - HALO :, :], window_ref[:samples, :]], axis=0)
-    pairs = nt_dot(left, window_ref[...])
-    for k in range(count):
-        pairs_ref[k] = pairs[:, k * lanes : (k + 1) * lanes]
+    for k in [count - 1] + list(range(0, count - 1, 2)):
+        wide = 1 if k == count - 1 else 2
+        pairs = nt_dot(left, window_ref[k * lanes : (k + wide) * lanes, :])
+        for i in range(wide):
+            pairs_ref[k + i] = pairs[:, i * lanes : (i + 1) * lanes]
     body = rows - 8
     earlier = moved_lanes([pairs_ref[k, 7 : 7 + body, :] for k in range(count)], 1)
     for k in range(count):
@@ -323,9 +325,19 @@
 
 
 def side_kernel(
-    window_ref, high_ref, low_ref, bound_ref, answer_ref, along_ref, cross_ref, first_ref, second_ref
+    window_ref,
+    high_ref,
+    low_ref,
+    bound_ref,
+    answer_ref,
+    along_ref,
+    cross_ref,
+    first_ref,
+    second_ref,
+    turned_ref,
 ):
     width = window_ref.shape[0]
+    turned_ref[...] = window_ref[...].T
     weighted = high_ref[...].astype(f32) + low_ref[...].astype(f32)
     first_ref[...], second_ref[...] = split(solving_matrix(weighted, bound_ref[:1, :1]))
     answer = padded(answer_ref[...], width) * along_ref[...]
@@ -352,6 +364,7 @@
     own_ref,
     other_ref,
     window_ref,
+    turned_ref,
     first_ref,
     second_ref,
     cross_ref,
@@ -371,14 +384,15 @@
     target = cross_ref[...] + ridge_weight * (consensus - dual)
     window = window_ref[...]
     samples = first_ref.shape[0]
-    projected = gathered_lags(nt_dot(target.astype(bf16), window), samples) * (1.0 / CAP)
+    products = nn_dot(target.astype(bf16), turned_ref[...])
+    projected = gathered_lags(products, samples) * (1.0 / CAP)
     weights = times_matrix(projected, first_ref[...], second_ref[...])
     kept = padded(weights.astype(bf16).astype(f32), window.shape[0]) * along_ref[...]
     local = (target - spread_times_window(kept, window)) / ridge_weight
     store_halves(core, local + dual, later_ref, send_ref, keep_ref)
 
 
-def part_kernel(boots, own_ref, other_ref, window_ref, support_ref, *refs):
+def part_kernel(boots, own_ref, other_ref, turned_ref, support_ref, *refs):
     piece_refs, (tally_ref, full_ref, blocks_ref) = refs[:boots], refs[boots:]
     core, _, position = place()
     join_halves(core, own_ref, other_ref, full_ref)
@@ -404,7 +418,7 @@
     share = (weighted / tally).reshape(full_ref.shape).astype(bf16)
     half = RESPONSE_COUNT // 2
     samples = (piece_refs[0].shape[1] - width) // 2
-    forecast = gathered_lags(nt_dot(share, window_ref[...]), samples).astype(bf16)
+    forecast = gathered_lags(nn_dot(share, turned_ref[...]), samples).astype(bf16)
     for d in range(boots):
         opening = lax.bitwise_xor(position, d) * width
         row = lax.div(opening, channels) * RESPONSE_COUNT + core * half
@@ -533,9 +547,9 @@
             if count + 1 < ITERS:
                 break
         if count == 1:
-            cross, first, second = called(
+            cross, first, second, turned = called(
                 side_kernel,
-                (full_shape, square, square),
+                (full_shape, square, square, shaped((channels, width), bf16)),
                 [VMEM] * 6,
                 cost=pl.CostEstimate(
                     flops=14 * samples**3, bytes_accessed=1 << 20, transcendentals=0
@@ -546,9 +560,9 @@
         send, keep, *states = called(
             next_kernel,
             (half_shape, half_shape) + (full_shape,) * going,
-            [VMEM] * 8,
+            [VMEM] * 9,
             [pltpu.VMEM((rows, channels), f32)],
-        )(mean, swapped(mean, "tm", 1), window, first, second, cross, along, state)
+        )(mean, swapped(mean, "tm", 1), window, turned, first, second, cross, along, state)
         state = states[0] if going else None
 
     features = LAGS * channels // boots
@@ -558,7 +572,7 @@
         (piece,) * boots + (shaped((1, features)),),
         [VMEM] * 4,
         [pltpu.VMEM((rows, channels), f32), pltpu.VMEM((boots, boots, features), f32)],
-    )(mean, swapped(mean, "tm", 1), window, support)
+    )(mean, swapped(mean, "tm", 1), turned, support)
     pieces = pieces[:1] + [swapped(pieces[d], "boot", d) for d in range(1, boots)]
     averaged = called(
         average_kernel, shaped((RESPONSE_COUNT // 2, features)), [VMEM] * (boots + 1)

time: 74.2 us -> 73.2 us (0.987)
  Pallas kernels: 14.4 us -> 13.4 us
where the time goes in v3:
time: 73.2 us; the launch traced here: 73 us
  waiting for transfers between devices  32.9 us (45%)
  starting transfers between devices  25.4 us (35%)
  Pallas kernels  13.4 us (18%)
  between operations  0.78 us (1%)
    ppermute x25, waiting for transfers between devices, swapped(): return lax.ppermute(block, axis, [(i, i ^ distance) for i in devices])  32.9 us
    ppermute x25, starting transfers between devices, swapped(): return lax.ppermute(block, axis, [(i, i ^ distance) for i in devices])  25.4 us
    pallas_call x1, Pallas kernels, per_device(): called(functools.partial(first_kernel, samples * shards, len(powers), len...  3.89 us
    pallas_call x2, Pallas kernels, per_device(): called(next_kernel, (half_shape, half_shape) + (full_shape,) * going, [VM...  3.34 us
    pallas_call x1, Pallas kernels, per_device(): called(side_kernel, (full_shape, square, square, shaped((channels, width)...  2.8 us
  transfers between devices with their start and end apart: 25, of which 18 were waited for; matrix products, arithmetic and copies ran while one was open for 0% of the time, Pallas kernels for 5%

profile of v3, /device:TPU:0, one launch (start us, length us, event | category | flops | bytes accessed | tf_op | source)
XLA Modules:
  0.0 73.0 jit_solution(12478406135603465932)
XLA Ops:
  0.6 1.3 %shard_map.59 = (bf16[512,1024]{1,0:T(8,128)(2,1)S(1)}, f32[8,1024]{1,0:T(8,128)S(1)}, f32[1,640]{1,0:T(1,128)S(1)}, f32[512,128]{1,0:T(8,128)S(1)}) custom-call(s32[1,6]{1,0:T(1,128)} %starts_hbm.1, s32[1,6]{1,0:T(1,128)} %lengths_hbm.1, bf16[512,1024]{1,0:T(8,128)(2,1)} %source_ref.1), custom_call_target="tpu_custom_call" | custom-call | tf_op jit(solution)/shard_map/pallas_call | solution.py:484
  2.5 0.9 %collective-permute-done.other_ref.refs_4_ = f32[8,1024]{1,0:T(8,128)S(1)} collective-permute-done((f32[8,1024]{1,0:T(8,128)S(1)}, f32[8,1024]{1,0:T(8,128)S(1)}, u32[]{:S(2)}, u32[]{:S(2)}) %collective-permute-start) | collective-permute-done | bytes 32800 | tf_op jit(solution)/shard_map/ppermute | solution.py:35
  3.4 3.8 %collective-permute-start.3 = (bf16[8,1024]{1,0:T(8,128)(2,1)S(1)}, bf16[8,1024]{1,0:T(8,128)(2,1)S(1)}, u32[]{:S(2)}, u32[]{:S(2)}) collective-permute-start(bf16[8,1024]{1,0:T(8,128)(2,1)S(1)} %shard_map.60.refs_0_), channel_id=1, source_target_pairs={{0,6},{1,7},{2,4},{3,5},{4,2},{5,3},{6,0},{7,1},{8,14},{9,15},{10,... | collective-permute-start | bytes 49160 | tf_op jit(solution)/shard_map/ppermute | solution.py:35
  7.8 1.1 %collective-permute-done.3.refs_3_.refs_7_ = bf16[8,1024]{1,0:T(8,128)(2,1)S(1)} collective-permute-done((bf16[8,1024]{1,0:T(8,128)(2,1)S(1)}, bf16[8,1024]{1,0:T(8,128)(2,1)S(1)}, u32[]{:S(2)}, u32[]{:S(2)}) %collective-permute-start.3) | collective-permute-done | bytes 16416 | tf_op jit(solution)/shard_map/ppermute | solution.py:35
  8.9 2.0 %collective-permute-done.2.refs_2_.refs_6_ = bf16[8,1024]{1,0:T(8,128)(2,1)S(1)} collective-permute-done((bf16[8,1024]{1,0:T(8,128)(2,1)S(1)}, bf16[8,1024]{1,0:T(8,128)(2,1)S(1)}, u32[]{:S(2)}, u32[]{:S(2)}) %collective-permute-start.2) | collective-permute-done | bytes 16416 | tf_op jit(solution)/shard_map/ppermute | solution.py:35
  11.4 3.9 %shard_map.61 = (bf16[640,1024]{1,0:T(8,128)(2,1)S(1)}, bf16[512,512]{1,0:T(8,128)(2,1)S(1)}, bf16[512,512]{1,0:T(8,128)(2,1)S(1)}, f32[8,128]{1,0:T(8,128)S(1)}...) custom-call(bf16[8,1024]{1,0:T(8,128)(2,1)S(1)} %shard_map.60.refs_0_, ...), custom_call_target="tpu_custom_call" | custom-call | tf_op jit(solution)/shard_map/pallas_call | solution.py:513
  15.4 1.5 %collective-permute-done.4 = f32[64,1024]{1,0:T(8,128)S(1)} collective-permute-done((f32[64,1024]{1,0:T(8,128)S(1)}, f32[64,1024]{1,0:T(8,128)S(1)}, u32[]{:S(2)}, u32[]{:S(2)}) %collective-permute-start.4) | collective-permute-done | bytes 262176 | tf_op jit(solution)/shard_map/ppermute | solution.py:35
  17.0 1.6 %collective-permute-start.7 = (bf16[64,1024]{1,0:T(8,128)(2,1)S(1)}, bf16[64,1024]{1,0:T(8,128)(2,1)S(1)}, u32[]{:S(2)}, u32[]{:S(2)}) collective-permute-start(bf16[64,1024]{1,0:T(8,128)(2,1)S(1)} %add_convert_fusion), channel_id=1, source_target_pairs={{0,6},{1,7},{2,4},{3,5},{4,2},{5,3},{6,0},{7,1},{8,14},{9,15},{10,... | collective-permute-start | bytes 393224 | tf_op jit(solution)/shard_map/ppermute | solution.py:35
  18.7 1.9 %collective-permute-start.5 = (bf16[64,1024]{1,0:T(8,128)(2,1)S(1)}, bf16[64,1024]{1,0:T(8,128)(2,1)S(1)}, u32[]{:S(2)}, u32[]{:S(2)}) collective-permute-start(bf16[64,1024]{1,0:T(8,128)(2,1)S(1)} %add_convert_fusion), channel_id=1, source_target_pairs={{0,2},{1,3},{2,0},{3,1},{4,6},{5,7},{6,4},{7,5},{8,10},{9,11},{10,... | collective-permute-start | bytes 393224 | tf_op jit(solution)/shard_map/ppermute | solution.py:35
  20.5 1.6 %collective-permute-start.8 = (f32[4,1024]{1,0:T(4,128)S(1)}, f32[4,1024]{1,0:T(4,128)S(1)}, u32[]{:S(2)}, u32[]{:S(2)}) collective-permute-start(f32[4,1024]{1,0:T(4,128)S(1)} %convert_element_type.51), channel_id=1, source_target_pairs={{0,8},{8,0},{16,24},{24,16},{1,9},{9,1},{17,25},{25,17},{2,10},{10... | collective-permute-start | bytes 49160 | tf_op jit(solution)/shard_map/ppermute | solution.py:35
  22.1 2.2 %collective-permute-done.8 = f32[4,1024]{1,0:T(4,128)S(1)} collective-permute-done((f32[4,1024]{1,0:T(4,128)S(1)}, f32[4,1024]{1,0:T(4,128)S(1)}, u32[]{:S(2)}, u32[]{:S(2)}) %collective-permute-start.8) | collective-permute-done | bytes 16416 | tf_op jit(solution)/shard_map/ppermute | solution.py:35
  24.3 2.0 %collective-permute-done.6 = bf16[64,1024]{1,0:T(8,128)(2,1)S(1)} collective-permute-done((bf16[64,1024]{1,0:T(8,128)(2,1)S(1)}, bf16[64,1024]{1,0:T(8,128)(2,1)S(1)}, u32[]{:S(2)}, u32[]{:S(2)}) %collective-permute-start.6) | collective-permute-done | bytes 131104 | tf_op jit(solution)/shard_map/ppermute | solution.py:35
  26.6 2.8 %shard_map.62 = (f32[128,1024]{1,0:T(8,128)S(1)}, bf16[512,512]{1,0:T(8,128)(2,1)S(1)}, bf16[512,512]{1,0:T(8,128)(2,1)S(1)}, bf16[1024,640]{1,0:T(8,128)(2,1)S(1)}) custom-call(bf16[640,1024]{1,0:T(8,128)(2,1)S(1)} %get-tuple-element.66.window_ref, bf16[512,512]{1,0:T(8,128)(2,1)S(1)} %get-tuple-element.51.high_ref, ...), custom_call_target="tpu_custom_call" | custom-call | flops 1879048192 | bytes 1048576 | tf_op jit(solution)/shard_map/pallas_call | solution.py:550
  29.4 1.7 %shard_map.63 = (f32[64,1024]{1,0:T(8,128)S(1)}, f32[64,1024]{1,0:T(8,128)S(1)}, f32[128,1024]{1,0:T(8,128)S(1)}) custom-call(f32[64,1024]{1,0:T(8,128)S(1)} %broadcast_multiply_fusion.1.own_ref, f32[64,1024]{1,0:T(8,128)S(1)} %collective-permute-done.9.other_ref, bf16[640,1024]{1,0:T(8,128)(2,1)S(1)} %get-tuple-element.66.window_ref, ...), custom_call_target="tpu_custom_call" | custom-call | tf_op jit(solution)/shard_map/pallas_call | solution.py:560
  31.6 1.2 %collective-permute-done.10 = f32[64,1024]{1,0:T(8,128)S(1)} collective-permute-done((f32[64,1024]{1,0:T(8,128)S(1)}, f32[64,1024]{1,0:T(8,128)S(1)}, u32[]{:S(2)}, u32[]{:S(2)}) %collective-permute-start.10) | collective-permute-done | bytes 262176 | tf_op jit(solution)/shard_map/ppermute | solution.py:35
  32.8 2.6 %collective-permute-start.14 = (f32[8,1024]{1,0:T(8,128)S(1)}, f32[8,1024]{1,0:T(8,128)S(1)}, u32[]{:S(2)}, u32[]{:S(2)}) collective-permute-start(f32[8,1024]{1,0:T(8,128)S(1)} %pad_maximum_fusion.1), channel_id=1, source_target_pairs={{0,16},{8,24},{16,0},{24,8},{1,17},{9,25},{17,1},{25,9},{2,18},{10... | collective-permute-start | bytes 98312 | tf_op jit(solution)/shard_map/ppermute | solution.py:35
  35.5 1.4 %collective-permute-start.13 = (bf16[64,1024]{1,0:T(8,128)(2,1)S(1)}, bf16[64,1024]{1,0:T(8,128)(2,1)S(1)}, u32[]{:S(2)}, u32[]{:S(2)}) collective-permute-start(bf16[64,1024]{1,0:T(8,128)(2,1)S(1)} %fusion.3), channel_id=1, source_target_pairs={{0,6},{1,7},{2,4},{3,5},{4,2},{5,3},{6,0},{7,1},{8,14},{9,15},{10,... | collective-permute-start | bytes 393224 | tf_op jit(solution)/shard_map/ppermute | solution.py:35
  37.5 1.5 %collective-permute-start.11 = (bf16[64,1024]{1,0:T(8,128)(2,1)S(1)}, bf16[64,1024]{1,0:T(8,128)(2,1)S(1)}, u32[]{:S(2)}, u32[]{:S(2)}) collective-permute-start(bf16[64,1024]{1,0:T(8,128)(2,1)S(1)} %fusion.3), channel_id=1, source_target_pairs={{0,2},{1,3},{2,0},{3,1},{4,6},{5,7},{6,4},{7,5},{8,10},{9,11},{10,... | collective-permute-start | bytes 393224 | tf_op jit(solution)/shard_map/ppermute | solution.py:35
  39.0 3.8 %collective-permute-done.13 = bf16[64,1024]{1,0:T(8,128)(2,1)S(1)} collective-permute-done((bf16[64,1024]{1,0:T(8,128)(2,1)S(1)}, bf16[64,1024]{1,0:T(8,128)(2,1)S(1)}, u32[]{:S(2)}, u32[]{:S(2)}) %collective-permute-start.13) | collective-permute-done | bytes 131104 | tf_op jit(solution)/shard_map/ppermute | solution.py:35
  42.8 1.9 %collective-permute-done.12 = bf16[64,1024]{1,0:T(8,128)(2,1)S(1)} collective-permute-done((bf16[64,1024]{1,0:T(8,128)(2,1)S(1)}, bf16[64,1024]{1,0:T(8,128)(2,1)S(1)}, u32[]{:S(2)}, u32[]{:S(2)}) %collective-permute-start.12) | collective-permute-done | bytes 131104 | tf_op jit(solution)/shard_map/ppermute | solution.py:35
  44.9 1.5 %collective-permute-done.15.other_ref = f32[64,1024]{1,0:T(8,128)S(1)} collective-permute-done((f32[64,1024]{1,0:T(8,128)S(1)}, f32[64,1024]{1,0:T(8,128)S(1)}, u32[]{:S(2)}, u32[]{:S(2)}) %collective-permute-start.15) | collective-permute-done | bytes 262176 | tf_op jit(solution)/shard_map/ppermute | solution.py:35
  46.4 1.7 %shard_map.64 = (f32[64,1024]{1,0:T(8,128)S(1)}, f32[64,1024]{1,0:T(8,128)S(1)}) custom-call(f32[64,1024]{1,0:T(8,128)S(1)} %get-tuple-element.65.own_ref, f32[64,1024]{1,0:T(8,128)S(1)} %collective-permute-done.15.other_ref, bf16[640,1024]{1,0:T(8,128)(2,1)S(1)} %get-tuple-element.66.window_ref, bf16[1024,640]{1,0:T(8,128)(2,1)S(1)} %get-tuple-element.55.turned_ref, ...), custom_call_target="tpu_custom_call" | custom-call | tf_op jit(solution)/shard_map/pallas_call | solution.py:560
  48.3 1.4 %collective-permute-done.16 = f32[64,1024]{1,0:T(8,128)S(1)} collective-permute-done((f32[64,1024]{1,0:T(8,128)S(1)}, f32[64,1024]{1,0:T(8,128)S(1)}, u32[]{:S(2)}, u32[]{:S(2)}) %collective-permute-start.16) | collective-permute-done | bytes 262176 | tf_op jit(solution)/shard_map/ppermute | solution.py:35
  49.8 1.5 %collective-permute-start.19 = (bf16[64,1024]{1,0:T(8,128)(2,1)S(1)}, bf16[64,1024]{1,0:T(8,128)(2,1)S(1)}, u32[]{:S(2)}, u32[]{:S(2)}) collective-permute-start(bf16[64,1024]{1,0:T(8,128)(2,1)S(1)} %fusion.5), channel_id=1, source_target_pairs={{0,6},{1,7},{2,4},{3,5},{4,2},{5,3},{6,0},{7,1},{8,14},{9,15},{10,... | collective-permute-start | bytes 393224 | tf_op jit(solution)/shard_map/ppermute | solution.py:35
  51.8 1.5 %collective-permute-start.17 = (bf16[64,1024]{1,0:T(8,128)(2,1)S(1)}, bf16[64,1024]{1,0:T(8,128)(2,1)S(1)}, u32[]{:S(2)}, u32[]{:S(2)}) collective-permute-start(bf16[64,1024]{1,0:T(8,128)(2,1)S(1)} %fusion.5), channel_id=1, source_target_pairs={{0,2},{1,3},{2,0},{3,1},{4,6},{5,7},{6,4},{7,5},{8,10},{9,11},{10,... | collective-permute-start | bytes 393224 | tf_op jit(solution)/shard_map/ppermute | solution.py:35
  53.3 3.8 %collective-permute-done.19 = bf16[64,1024]{1,0:T(8,128)(2,1)S(1)} collective-permute-done((bf16[64,1024]{1,0:T(8,128)(2,1)S(1)}, bf16[64,1024]{1,0:T(8,128)(2,1)S(1)}, u32[]{:S(2)}, u32[]{:S(2)}) %collective-permute-start.19) | collective-permute-done | bytes 131104 | tf_op jit(solution)/shard_map/ppermute | solution.py:35
  57.1 1.9 %collective-permute-done.18 = bf16[64,1024]{1,0:T(8,128)(2,1)S(1)} collective-permute-done((bf16[64,1024]{1,0:T(8,128)(2,1)S(1)}, bf16[64,1024]{1,0:T(8,128)(2,1)S(1)}, u32[]{:S(2)}, u32[]{:S(2)}) %collective-permute-start.18) | collective-permute-done | bytes 131104 | tf_op jit(solution)/shard_map/ppermute | solution.py:35
  59.3 1.5 %collective-permute-done.20.other_ref = f32[64,1024]{1,0:T(8,128)S(1)} collective-permute-done((f32[64,1024]{1,0:T(8,128)S(1)}, f32[64,1024]{1,0:T(8,128)S(1)}, u32[]{:S(2)}, u32[]{:S(2)}) %collective-permute-start.20) | collective-permute-done | bytes 262176 | tf_op jit(solution)/shard_map/ppermute | solution.py:35
  60.8 0.7 %shard_map.65 = (bf16[16,2048]{1,0:T(8,128)(2,1)S(1)}, bf16[16,2048]{1,0:T(8,128)(2,1)S(1)}, bf16[16,2048]{1,0:T(8,128)(2,1)S(1)}, bf16[16,2048]{1,0:T(8,128)(2,1)S(1)}, f32[1,1024]{1,0:T(1,128)S(1)}) custom-call(f32[64,1024]{1,0:T(8,128)S(1)} %add_multiply_fusion.own_ref, f32[64,1024]{1,0:T(8,128)S(1)} %collective-permute-done.20.other_ref, ...), custom_call_target="tpu_custom_call" | custom-call | tf_op jit(solution)/shard_map/pallas_call | solution.py:570
  61.5 1.6 %collective-permute-start.21 = (bf16[16,2048]{1,0:T(8,128)(2,1)S(1)}, bf16[16,2048]{1,0:T(8,128)(2,1)S(1)}, u32[]{:S(2)}, u32[]{:S(2)}) collective-permute-start(bf16[16,2048]{1,0:T(8,128)(2,1)S(1)} %get-tuple-element.72), channel_id=1, source_target_pairs={{0,8},{8,0},{16,24},{24,16},{1,9},{9,1},{17,25},{25,17},{2,10},{10... | collective-permute-start | bytes 196616 | tf_op jit(solution)/shard_map/ppermute | solution.py:35
  63.5 2.5 %collective-permute-start.23 = (bf16[16,2048]{1,0:T(8,128)(2,1)S(1)}, bf16[16,2048]{1,0:T(8,128)(2,1)S(1)}, u32[]{:S(2)}, u32[]{:S(2)}) collective-permute-start(bf16[16,2048]{1,0:T(8,128)(2,1)S(1)} %get-tuple-element.74), channel_id=1, source_target_pairs={{0,24},{8,16},{16,8},{24,0},{1,25},{9,17},{17,9},{25,1},{2,26},{10... | collective-permute-start | bytes 196616 | tf_op jit(solution)/shard_map/ppermute | solution.py:35
  66.0 5.0 %collective-permute-done.22.refs_2_ = bf16[16,2048]{1,0:T(8,128)(2,1)S(1)} collective-permute-done((bf16[16,2048]{1,0:T(8,128)(2,1)S(1)}, bf16[16,2048]{1,0:T(8,128)(2,1)S(1)}, u32[]{:S(2)}, u32[]{:S(2)}) %collective-permute-start.22) | collective-permute-done | bytes 65568 | tf_op jit(solution)/shard_map/ppermute | solution.py:35
  (39 shorter events, 7.1 us)
Async XLA Ops:
  0.6 14.8 %copy-start = (s32[4,1024]{1,0:T(4,128)S(1)}, s32[4,1024]{1,0:T(4,128)}, u32[]{:S(2)}) copy-start(s32[4,1024]{1,0:T(4,128)} %param.7) | copy-start | bytes 49156
  1.9 1.4 %collective-permute-start = (f32[8,1024]{1,0:T(8,128)S(1)}, f32[8,1024]{1,0:T(8,128)S(1)}, u32[]{:S(2)}, u32[]{:S(2)}) collective-permute-start(f32[8,1024]{1,0:T(8,128)S(1)} %get-tuple-element.39.own_ref), channel_id=1, source_target_pairs={{0,1},{1,0},{2,3},{3,2},{4,5},{5,4},{6,7},{7,6},{8,9},{9,8},{10,11... | collective-permute-start | bytes 98312 | tf_op jit(solution)/shard_map/ppermute | solution.py:35
  3.4 5.6 %collective-permute-start.3 = (bf16[8,1024]{1,0:T(8,128)(2,1)S(1)}, bf16[8,1024]{1,0:T(8,128)(2,1)S(1)}, u32[]{:S(2)}, u32[]{:S(2)}) collective-permute-start(bf16[8,1024]{1,0:T(8,128)(2,1)S(1)} %shard_map.60.refs_0_), channel_id=1, source_target_pairs={{0,6},{1,7},{2,4},{3,5},{4,2},{5,3},{6,0},{7,1},{8,14},{9,15},{10,... | collective-permute-start | bytes 49160 | tf_op jit(solution)/shard_map/ppermute | solution.py:35
  7.2 3.7 %collective-permute-start.2 = (bf16[8,1024]{1,0:T(8,128)(2,1)S(1)}, bf16[8,1024]{1,0:T(8,128)(2,1)S(1)}, u32[]{:S(2)}, u32[]{:S(2)}) collective-permute-start(bf16[8,1024]{1,0:T(8,128)(2,1)S(1)} %shard_map.60.refs_0_), channel_id=1, source_target_pairs={{0,4},{1,5},{2,6},{3,7},{4,0},{5,1},{6,2},{7,3},{8,12},{9,13},{10,... | collective-permute-start | bytes 49160 | tf_op jit(solution)/shard_map/ppermute | solution.py:35
  7.7 3.7 %collective-permute-start.1 = (bf16[8,1024]{1,0:T(8,128)(2,1)S(1)}, bf16[8,1024]{1,0:T(8,128)(2,1)S(1)}, u32[]{:S(2)}, u32[]{:S(2)}) collective-permute-start(bf16[8,1024]{1,0:T(8,128)(2,1)S(1)} %shard_map.60.refs_0_), channel_id=1, source_target_pairs={{0,2},{1,3},{2,0},{3,1},{4,6},{5,7},{6,4},{7,5},{8,10},{9,11},{10,... | collective-permute-start | bytes 49160 | tf_op jit(solution)/shard_map/ppermute | solution.py:35
  15.3 1.6 %collective-permute-start.4 = (f32[64,1024]{1,0:T(8,128)S(1)}, f32[64,1024]{1,0:T(8,128)S(1)}, u32[]{:S(2)}, u32[]{:S(2)}) collective-permute-start(f32[64,1024]{1,0:T(8,128)S(1)} %get-tuple-element.44), channel_id=1, source_target_pairs={{0,1},{1,0},{2,3},{3,2},{4,5},{5,4},{6,7},{7,6},{8,9},{9,8},{10,11... | collective-permute-start | bytes 786440 | tf_op jit(solution)/shard_map/ppermute | solution.py:35
  17.0 7.4 %collective-permute-start.7 = (bf16[64,1024]{1,0:T(8,128)(2,1)S(1)}, bf16[64,1024]{1,0:T(8,128)(2,1)S(1)}, u32[]{:S(2)}, u32[]{:S(2)}) collective-permute-start(bf16[64,1024]{1,0:T(8,128)(2,1)S(1)} %add_convert_fusion), channel_id=1, source_target_pairs={{0,6},{1,7},{2,4},{3,5},{4,2},{5,3},{6,0},{7,1},{8,14},{9,15},{10,... | collective-permute-start | bytes 393224 | tf_op jit(solution)/shard_map/ppermute | solution.py:35
  18.5 7.8 %collective-permute-start.6 = (bf16[64,1024]{1,0:T(8,128)(2,1)S(1)}, bf16[64,1024]{1,0:T(8,128)(2,1)S(1)}, u32[]{:S(2)}, u32[]{:S(2)}) collective-permute-start(bf16[64,1024]{1,0:T(8,128)(2,1)S(1)} %add_convert_fusion), channel_id=1, source_target_pairs={{0,4},{1,5},{2,6},{3,7},{4,0},{5,1},{6,2},{7,3},{8,12},{9,13},{10,... | collective-permute-start | bytes 393224 | tf_op jit(solution)/shard_map/ppermute | solution.py:35
  18.7 7.7 %collective-permute-start.5 = (bf16[64,1024]{1,0:T(8,128)(2,1)S(1)}, bf16[64,1024]{1,0:T(8,128)(2,1)S(1)}, u32[]{:S(2)}, u32[]{:S(2)}) collective-permute-start(bf16[64,1024]{1,0:T(8,128)(2,1)S(1)} %add_convert_fusion), channel_id=1, source_target_pairs={{0,2},{1,3},{2,0},{3,1},{4,6},{5,7},{6,4},{7,5},{8,10},{9,11},{10,... | collective-permute-start | bytes 393224 | tf_op jit(solution)/shard_map/ppermute | solution.py:35
  20.5 3.7 %collective-permute-start.8 = (f32[4,1024]{1,0:T(4,128)S(1)}, f32[4,1024]{1,0:T(4,128)S(1)}, u32[]{:S(2)}, u32[]{:S(2)}) collective-permute-start(f32[4,1024]{1,0:T(4,128)S(1)} %convert_element_type.51), channel_id=1, source_target_pairs={{0,8},{8,0},{16,24},{24,16},{1,9},{9,1},{17,25},{25,17},{2,10},{10... | collective-permute-start | bytes 49160 | tf_op jit(solution)/shard_map/ppermute | solution.py:35
  26.5 2.9 %collective-permute-start.9 = (f32[64,1024]{1,0:T(8,128)S(1)}, f32[64,1024]{1,0:T(8,128)S(1)}, u32[]{:S(2)}, u32[]{:S(2)}) collective-permute-start(f32[64,1024]{1,0:T(8,128)S(1)} %broadcast_multiply_fusion.1.own_ref), channel_id=1, source_target_pairs={{0,1},{1,0},{2,3},{3,2},{4,5},{5,4},{6,7},{7,6},{8,9},{9,8},{10,11... | collective-permute-start | bytes 786440 | tf_op jit(solution)/shard_map/ppermute | solution.py:35
  31.1 1.7 %collective-permute-start.10 = (f32[64,1024]{1,0:T(8,128)S(1)}, f32[64,1024]{1,0:T(8,128)S(1)}, u32[]{:S(2)}, u32[]{:S(2)}) collective-permute-start(f32[64,1024]{1,0:T(8,128)S(1)} %get-tuple-element.61), channel_id=1, source_target_pairs={{0,1},{1,0},{2,3},{3,2},{4,5},{5,4},{6,7},{7,6},{8,9},{9,8},{10,11... | collective-permute-start | bytes 786440 | tf_op jit(solution)/shard_map/ppermute | solution.py:35
  32.8 6.1 %collective-permute-start.14 = (f32[8,1024]{1,0:T(8,128)S(1)}, f32[8,1024]{1,0:T(8,128)S(1)}, u32[]{:S(2)}, u32[]{:S(2)}) collective-permute-start(f32[8,1024]{1,0:T(8,128)S(1)} %pad_maximum_fusion.1), channel_id=1, source_target_pairs={{0,16},{8,24},{16,0},{24,8},{1,17},{9,25},{17,1},{25,9},{2,18},{10... | collective-permute-start | bytes 98312 | tf_op jit(solution)/shard_map/ppermute | solution.py:35
  35.5 7.3 %collective-permute-start.13 = (bf16[64,1024]{1,0:T(8,128)(2,1)S(1)}, bf16[64,1024]{1,0:T(8,128)(2,1)S(1)}, u32[]{:S(2)}, u32[]{:S(2)}) collective-permute-start(bf16[64,1024]{1,0:T(8,128)(2,1)S(1)} %fusion.3), channel_id=1, source_target_pairs={{0,6},{1,7},{2,4},{3,5},{4,2},{5,3},{6,0},{7,1},{8,14},{9,15},{10,... | collective-permute-start | bytes 393224 | tf_op jit(solution)/shard_map/ppermute | solution.py:35
  36.9 7.8 %collective-permute-start.12 = (bf16[64,1024]{1,0:T(8,128)(2,1)S(1)}, bf16[64,1024]{1,0:T(8,128)(2,1)S(1)}, u32[]{:S(2)}, u32[]{:S(2)}) collective-permute-start(bf16[64,1024]{1,0:T(8,128)(2,1)S(1)} %fusion.3), channel_id=1, source_target_pairs={{0,4},{1,5},{2,6},{3,7},{4,0},{5,1},{6,2},{7,3},{8,12},{9,13},{10,... | collective-permute-start | bytes 393224 | tf_op jit(solution)/shard_map/ppermute | solution.py:35
  37.5 7.2 %collective-permute-start.11 = (bf16[64,1024]{1,0:T(8,128)(2,1)S(1)}, bf16[64,1024]{1,0:T(8,128)(2,1)S(1)}, u32[]{:S(2)}, u32[]{:S(2)}) collective-permute-start(bf16[64,1024]{1,0:T(8,128)(2,1)S(1)} %fusion.3), channel_id=1, source_target_pairs={{0,2},{1,3},{2,0},{3,1},{4,6},{5,7},{6,4},{7,5},{8,10},{9,11},{10,... | collective-permute-start | bytes 393224 | tf_op jit(solution)/shard_map/ppermute | solution.py:35
  44.8 1.6 %collective-permute-start.15 = (f32[64,1024]{1,0:T(8,128)S(1)}, f32[64,1024]{1,0:T(8,128)S(1)}, u32[]{:S(2)}, u32[]{:S(2)}) collective-permute-start(f32[64,1024]{1,0:T(8,128)S(1)} %get-tuple-element.65.own_ref), channel_id=1, source_target_pairs={{0,1},{1,0},{2,3},{3,2},{4,5},{5,4},{6,7},{7,6},{8,9},{9,8},{10,11... | collective-permute-start | bytes 786440 | tf_op jit(solution)/shard_map/ppermute | solution.py:35
  48.1 1.6 %collective-permute-start.16 = (f32[64,1024]{1,0:T(8,128)S(1)}, f32[64,1024]{1,0:T(8,128)S(1)}, u32[]{:S(2)}, u32[]{:S(2)}) collective-permute-start(f32[64,1024]{1,0:T(8,128)S(1)} %get-tuple-element.69), channel_id=1, source_target_pairs={{0,1},{1,0},{2,3},{3,2},{4,5},{5,4},{6,7},{7,6},{8,9},{9,8},{10,11... | collective-permute-start | bytes 786440 | tf_op jit(solution)/shard_map/ppermute | solution.py:35
  49.8 7.4 %collective-permute-start.19 = (bf16[64,1024]{1,0:T(8,128)(2,1)S(1)}, bf16[64,1024]{1,0:T(8,128)(2,1)S(1)}, u32[]{:S(2)}, u32[]{:S(2)}) collective-permute-start(bf16[64,1024]{1,0:T(8,128)(2,1)S(1)} %fusion.5), channel_id=1, source_target_pairs={{0,6},{1,7},{2,4},{3,5},{4,2},{5,3},{6,0},{7,1},{8,14},{9,15},{10,... | collective-permute-start | bytes 393224 | tf_op jit(solution)/shard_map/ppermute | solution.py:35
  51.2 7.8 %collective-permute-start.18 = (bf16[64,1024]{1,0:T(8,128)(2,1)S(1)}, bf16[64,1024]{1,0:T(8,128)(2,1)S(1)}, u32[]{:S(2)}, u32[]{:S(2)}) collective-permute-start(bf16[64,1024]{1,0:T(8,128)(2,1)S(1)} %fusion.5), channel_id=1, source_target_pairs={{0,4},{1,5},{2,6},{3,7},{4,0},{5,1},{6,2},{7,3},{8,12},{9,13},{10,... | collective-permute-start | bytes 393224 | tf_op jit(solution)/shard_map/ppermute | solution.py:35
  51.8 7.3 %collective-permute-start.17 = (bf16[64,1024]{1,0:T(8,128)(2,1)S(1)}, bf16[64,1024]{1,0:T(8,128)(2,1)S(1)}, u32[]{:S(2)}, u32[]{:S(2)}) collective-permute-start(bf16[64,1024]{1,0:T(8,128)(2,1)S(1)} %fusion.5), channel_id=1, source_target_pairs={{0,2},{1,3},{2,0},{3,1},{4,6},{5,7},{6,4},{7,5},{8,10},{9,11},{10,... | collective-permute-start | bytes 393224 | tf_op jit(solution)/shard_map/ppermute | solution.py:35
  59.2 1.6 %collective-permute-start.20 = (f32[64,1024]{1,0:T(8,128)S(1)}, f32[64,1024]{1,0:T(8,128)S(1)}, u32[]{:S(2)}, u32[]{:S(2)}) collective-permute-start(f32[64,1024]{1,0:T(8,128)S(1)} %add_multiply_fusion.own_ref), channel_id=1, source_target_pairs={{0,1},{1,0},{2,3},{3,2},{4,5},{5,4},{6,7},{7,6},{8,9},{9,8},{10,11... | collective-permute-start | bytes 786440 | tf_op jit(solution)/shard_map/ppermute | solution.py:35
  61.5 4.5 %collective-permute-start.21 = (bf16[16,2048]{1,0:T(8,128)(2,1)S(1)}, bf16[16,2048]{1,0:T(8,128)(2,1)S(1)}, u32[]{:S(2)}, u32[]{:S(2)}) collective-permute-start(bf16[16,2048]{1,0:T(8,128)(2,1)S(1)} %get-tuple-element.72), channel_id=1, source_target_pairs={{0,8},{8,0},{16,24},{24,16},{1,9},{9,1},{17,25},{25,17},{2,10},{10... | collective-permute-start | bytes 196616 | tf_op jit(solution)/shard_map/ppermute | solution.py:35
  63.2 7.8 %collective-permute-start.22 = (bf16[16,2048]{1,0:T(8,128)(2,1)S(1)}, bf16[16,2048]{1,0:T(8,128)(2,1)S(1)}, u32[]{:S(2)}, u32[]{:S(2)}) collective-permute-start(bf16[16,2048]{1,0:T(8,128)(2,1)S(1)} %get-tuple-element.73), channel_id=1, source_target_pairs={{0,16},{8,24},{16,0},{24,8},{1,17},{9,25},{17,1},{25,9},{2,18},{10... | collective-permute-start | bytes 196616 | tf_op jit(solution)/shard_map/ppermute | solution.py:35
  63.5 7.5 %collective-permute-start.23 = (bf16[16,2048]{1,0:T(8,128)(2,1)S(1)}, bf16[16,2048]{1,0:T(8,128)(2,1)S(1)}, u32[]{:S(2)}, u32[]{:S(2)}) collective-permute-start(bf16[16,2048]{1,0:T(8,128)(2,1)S(1)} %get-tuple-element.74), channel_id=1, source_target_pairs={{0,24},{8,16},{16,8},{24,0},{1,25},{9,17},{17,9},{25,1},{2,26},{10... | collective-permute-start | bytes 196616 | tf_op jit(solution)/shard_map/ppermute | solution.py:35
  71.1 1.3 %collective-permute-start.24 = (f32[16,1024]{1,0:T(8,128)S(1)}, f32[16,1024]{1,0:T(8,128)S(1)}, u32[]{:S(2)}, u32[]{:S(2)}) collective-permute-start(f32[16,1024]{1,0:T(8,128)S(1)} %shard_map.66.own_ref), channel_id=1, source_target_pairs={{0,1},{1,0},{2,3},{3,2},{4,5},{5,4},{6,7},{7,6},{8,9},{9,8},{10,11... | collective-permute-start | bytes 196616 | tf_op jit(solution)/shard_map/ppermute | solution.py:35

commit v4 on v3

--- a/solution.py
+++ b/solution.py
@@ -281,6 +281,7 @@
         window_ref,
         high_ref,
         low_ref,
+        cross_ref,
         bound_ref,
         answer_ref,
         state_ref,
@@ -315,33 +316,21 @@
 
     answer = window_ref[:samples, :128].astype(f32).T[:RESPONSE_COUNT]
     answer_ref[...] = answer
-    short = answer.astype(bf16)
-    projected = (nn_dot(short, high) + nn_dot(short, low)) * (1.0 / CAP)
+    cross = spread_times_window(padded(answer, width) * along, window) * (1.0 / CAP)
+    cross_ref[...] = cross
+    products = nt_dot(cross.astype(bf16), window)
+    projected = gathered_lags(products, samples) * (1.0 / CAP)
     weights = chebyshev(high, low, projected, bound).astype(bf16).astype(f32)
-    kept = padded(answer * (1.0 / CAP) - weights, width) * along
-    local = spread_times_window(kept, window) / ridge_weight
+    back = spread_times_window(padded(weights, width) * along, window)
+    local = (cross - back) / ridge_weight
     core, _, _ = place()
     store_halves(core, local, state_ref, send_ref, keep_ref)
 
 
-def side_kernel(
-    window_ref,
-    high_ref,
-    low_ref,
-    bound_ref,
-    answer_ref,
-    along_ref,
-    cross_ref,
-    first_ref,
-    second_ref,
-    turned_ref,
-):
-    width = window_ref.shape[0]
+def side_kernel(window_ref, high_ref, low_ref, bound_ref, first_ref, second_ref, turned_ref):
     turned_ref[...] = window_ref[...].T
     weighted = high_ref[...].astype(f32) + low_ref[...].astype(f32)
     first_ref[...], second_ref[...] = split(solving_matrix(weighted, bound_ref[:1, :1]))
-    answer = padded(answer_ref[...], width) * along_ref[...]
-    cross_ref[...] = spread_times_window(answer, window_ref[...]) * (1.0 / CAP)
 
 
 def column_norms(mean):
@@ -510,12 +499,13 @@
         halos = [lax.ppermute(packet, "tm", [(i, i + 1) for i in range(shards - 1)])]
 
     square = shaped((samples, samples), bf16)
-    window, high, low, bound, answer, state, send, keep = called(
+    window, high, low, cross, bound, answer, state, send, keep = called(
         functools.partial(first_kernel, samples * shards, len(powers), len(halos)),
         (
             shaped((width, channels), bf16),
             square,
             square,
+            full_shape,
             shaped((8, 128)),
             shaped((RESPONSE_COUNT, samples)),
             full_shape,
@@ -547,14 +537,14 @@
             if count + 1 < ITERS:
                 break
         if count == 1:
-            cross, first, second, turned = called(
+            first, second, turned = called(
                 side_kernel,
-                (full_shape, square, square, shaped((channels, width), bf16)),
-                [VMEM] * 6,
+                (square, square, shaped((channels, width), bf16)),
+                [VMEM] * 4,
                 cost=pl.CostEstimate(
                     flops=14 * samples**3, bytes_accessed=1 << 20, transcendentals=0
                 ),
-            )(window, high, low, bound, answer, along)
+            )(window, high, low, bound)
         mean, support = lax.optimization_barrier((mean, support))
         going = count + 1 < ITERS
         send, keep, *states = called(

time: 73.2 us -> 72.6 us (level)
  transfers between devices with their start and end apart: 25 -> 25, of which waited for: 18 -> 18; matrix products, arithmetic and copies ran while one was open for 0% -> 0% of each run, Pallas kernels for 5% -> 4%
where the time goes in v4:
time: 72.6 us; the launch traced here: 72.5 us
  waiting for transfers between devices  32.9 us (45%)
  starting transfers between devices  25.5 us (35%)
  Pallas kernels  12.8 us (18%)
  between operations  0.78 us (1%)
    ppermute x25, waiting for transfers between devices, swapped(): return lax.ppermute(block, axis, [(i, i ^ distance) for i in devices])  32.9 us
    ppermute x25, starting transfers between devices, swapped(): return lax.ppermute(block, axis, [(i, i ^ distance) for i in devices])  25.5 us
    pallas_call x1, Pallas kernels, per_device(): called(functools.partial(first_kernel, samples * shards, len(powers), len...  3.75 us
    pallas_call x2, Pallas kernels, per_device(): called(next_kernel, (half_shape, half_shape) + (full_shape,) * going, [VM...  3.32 us
    pallas_call x1, Pallas kernels, per_device(): called(side_kernel, (square, square, shaped((channels, width), bf16)), [V...  2.37 us
  transfers between devices with their start and end apart: 25, of which 18 were waited for; matrix products, arithmetic and copies ran while one was open for 0% of the time, Pallas kernels for 4%

profile of v4, /device:TPU:0, one launch (start us, length us, event | category | flops | bytes accessed | tf_op | source)
XLA Modules:
  0.0 72.5 jit_solution(12417548167686267969)
XLA Ops:
  0.6 1.3 %shard_map.59 = (bf16[512,1024]{1,0:T(8,128)(2,1)S(1)}, f32[8,1024]{1,0:T(8,128)S(1)}, f32[1,640]{1,0:T(1,128)S(1)}, f32[512,128]{1,0:T(8,128)S(1)}) custom-call(s32[1,6]{1,0:T(1,128)} %starts_hbm.1, s32[1,6]{1,0:T(1,128)} %lengths_hbm.1, bf16[512,1024]{1,0:T(8,128)(2,1)} %source_ref.1), custom_call_target="tpu_custom_call" | custom-call | tf_op jit(solution)/shard_map/pallas_call | solution.py:473
  2.5 0.9 %collective-permute-done.other_ref.refs_4_ = f32[8,1024]{1,0:T(8,128)S(1)} collective-permute-done((f32[8,1024]{1,0:T(8,128)S(1)}, f32[8,1024]{1,0:T(8,128)S(1)}, u32[]{:S(2)}, u32[]{:S(2)}) %collective-permute-start) | collective-permute-done | bytes 32800 | tf_op jit(solution)/shard_map/ppermute | solution.py:35
  3.4 3.8 %collective-permute-start.3 = (bf16[8,1024]{1,0:T(8,128)(2,1)S(1)}, bf16[8,1024]{1,0:T(8,128)(2,1)S(1)}, u32[]{:S(2)}, u32[]{:S(2)}) collective-permute-start(bf16[8,1024]{1,0:T(8,128)(2,1)S(1)} %shard_map.60.refs_0_), channel_id=1, source_target_pairs={{0,6},{1,7},{2,4},{3,5},{4,2},{5,3},{6,0},{7,1},{8,14},{9,15},{10,... | collective-permute-start | bytes 49160 | tf_op jit(solution)/shard_map/ppermute | solution.py:35
  7.8 1.1 %collective-permute-done.3.refs_3_.refs_7_ = bf16[8,1024]{1,0:T(8,128)(2,1)S(1)} collective-permute-done((bf16[8,1024]{1,0:T(8,128)(2,1)S(1)}, bf16[8,1024]{1,0:T(8,128)(2,1)S(1)}, u32[]{:S(2)}, u32[]{:S(2)}) %collective-permute-start.3) | collective-permute-done | bytes 16416 | tf_op jit(solution)/shard_map/ppermute | solution.py:35
  8.9 2.0 %collective-permute-done.2.refs_2_.refs_6_ = bf16[8,1024]{1,0:T(8,128)(2,1)S(1)} collective-permute-done((bf16[8,1024]{1,0:T(8,128)(2,1)S(1)}, bf16[8,1024]{1,0:T(8,128)(2,1)S(1)}, u32[]{:S(2)}, u32[]{:S(2)}) %collective-permute-start.2) | collective-permute-done | bytes 16416 | tf_op jit(solution)/shard_map/ppermute | solution.py:35
  11.4 3.7 %shard_map.61 = (bf16[640,1024]{1,0:T(8,128)(2,1)S(1)}, bf16[512,512]{1,0:T(8,128)(2,1)S(1)}, bf16[512,512]{1,0:T(8,128)(2,1)S(1)}, f32[128,1024]{1,0:T(8,128)S(...) custom-call(bf16[8,1024]{1,0:T(8,128)(2,1)S(1)} %shard_map.60.refs_0, ...), custom_call_target="tpu_custom_call" | custom-call | tf_op jit(solution)/shard_map/pallas_call | solution.py:502
  15.3 1.5 %collective-permute-done.4 = f32[64,1024]{1,0:T(8,128)S(1)} collective-permute-done((f32[64,1024]{1,0:T(8,128)S(1)}, f32[64,1024]{1,0:T(8,128)S(1)}, u32[]{:S(2)}, u32[]{:S(2)}) %collective-permute-start.4) | collective-permute-done | bytes 262176 | tf_op jit(solution)/shard_map/ppermute | solution.py:35
  16.8 1.6 %collective-permute-start.7 = (bf16[64,1024]{1,0:T(8,128)(2,1)S(1)}, bf16[64,1024]{1,0:T(8,128)(2,1)S(1)}, u32[]{:S(2)}, u32[]{:S(2)}) collective-permute-start(bf16[64,1024]{1,0:T(8,128)(2,1)S(1)} %add_convert_fusion), channel_id=1, source_target_pairs={{0,6},{1,7},{2,4},{3,5},{4,2},{5,3},{6,0},{7,1},{8,14},{9,15},{10,... | collective-permute-start | bytes 393224 | tf_op jit(solution)/shard_map/ppermute | solution.py:35
  18.5 1.9 %collective-permute-start.5 = (bf16[64,1024]{1,0:T(8,128)(2,1)S(1)}, bf16[64,1024]{1,0:T(8,128)(2,1)S(1)}, u32[]{:S(2)}, u32[]{:S(2)}) collective-permute-start(bf16[64,1024]{1,0:T(8,128)(2,1)S(1)} %add_convert_fusion), channel_id=1, source_target_pairs={{0,2},{1,3},{2,0},{3,1},{4,6},{5,7},{6,4},{7,5},{8,10},{9,11},{10,... | collective-permute-start | bytes 393224 | tf_op jit(solution)/shard_map/ppermute | solution.py:35
  20.4 1.6 %collective-permute-start.8 = (f32[4,1024]{1,0:T(4,128)S(1)}, f32[4,1024]{1,0:T(4,128)S(1)}, u32[]{:S(2)}, u32[]{:S(2)}) collective-permute-start(f32[4,1024]{1,0:T(4,128)S(1)} %convert_element_type.51), channel_id=1, source_target_pairs={{0,8},{8,0},{16,24},{24,16},{1,9},{9,1},{17,25},{25,17},{2,10},{10... | collective-permute-start | bytes 49160 | tf_op jit(solution)/shard_map/ppermute | solution.py:35
  22.0 2.2 %collective-permute-done.8 = f32[4,1024]{1,0:T(4,128)S(1)} collective-permute-done((f32[4,1024]{1,0:T(4,128)S(1)}, f32[4,1024]{1,0:T(4,128)S(1)}, u32[]{:S(2)}, u32[]{:S(2)}) %collective-permute-start.8) | collective-permute-done | bytes 16416 | tf_op jit(solution)/shard_map/ppermute | solution.py:35
  24.2 2.0 %collective-permute-done.6 = bf16[64,1024]{1,0:T(8,128)(2,1)S(1)} collective-permute-done((bf16[64,1024]{1,0:T(8,128)(2,1)S(1)}, bf16[64,1024]{1,0:T(8,128)(2,1)S(1)}, u32[]{:S(2)}, u32[]{:S(2)}) %collective-permute-start.6) | collective-permute-done | bytes 131104 | tf_op jit(solution)/shard_map/ppermute | solution.py:35
  26.4 2.4 %shard_map.62 = (bf16[512,512]{1,0:T(8,128)(2,1)S(1)}, bf16[512,512]{1,0:T(8,128)(2,1)S(1)}, bf16[1024,640]{1,0:T(8,128)(2,1)S(1)}) custom-call(bf16[640,1024]{1,0:T(8,128)(2,1)S(1)} %get-tuple-element.65.window_ref, bf16[512,512]{1,0:T(8,128)(2,1)S(1)} %get-tuple-element.51.high_ref, bf16[512,512]{1,0:T(8,128)(2,1)S(1)} %get-tuple-element.52.low_ref, ...), custom_call_target="tpu_custom_call" | custom-call | flops 1879048192 | bytes 1048576 | tf_op jit(solution)/shard_map/pallas_call | solution.py:540
  28.8 1.7 %shard_map.63 = (f32[64,1024]{1,0:T(8,128)S(1)}, f32[64,1024]{1,0:T(8,128)S(1)}, f32[128,1024]{1,0:T(8,128)S(1)}) custom-call(f32[64,1024]{1,0:T(8,128)S(1)} %broadcast_multiply_fusion.1.own_ref, f32[64,1024]{1,0:T(8,128)S(1)} %collective-permute-done.9.other_ref, bf16[640,1024]{1,0:T(8,128)(2,1)S(1)} %get-tuple-element.65.window_ref, ...), custom_call_target="tpu_custom_call" | custom-call | tf_op jit(solution)/shard_map/pallas_call | solution.py:550
  31.0 1.2 %collective-permute-done.10 = f32[64,1024]{1,0:T(8,128)S(1)} collective-permute-done((f32[64,1024]{1,0:T(8,128)S(1)}, f32[64,1024]{1,0:T(8,128)S(1)}, u32[]{:S(2)}, u32[]{:S(2)}) %collective-permute-start.10) | collective-permute-done | bytes 262176 | tf_op jit(solution)/shard_map/ppermute | solution.py:35
  32.2 2.7 %collective-permute-start.14 = (f32[8,1024]{1,0:T(8,128)S(1)}, f32[8,1024]{1,0:T(8,128)S(1)}, u32[]{:S(2)}, u32[]{:S(2)}) collective-permute-start(f32[8,1024]{1,0:T(8,128)S(1)} %pad_maximum_fusion.1), channel_id=1, source_target_pairs={{0,16},{8,24},{16,0},{24,8},{1,17},{9,25},{17,1},{25,9},{2,18},{10... | collective-permute-start | bytes 98312 | tf_op jit(solution)/shard_map/ppermute | solution.py:35
  34.9 1.4 %collective-permute-start.13 = (bf16[64,1024]{1,0:T(8,128)(2,1)S(1)}, bf16[64,1024]{1,0:T(8,128)(2,1)S(1)}, u32[]{:S(2)}, u32[]{:S(2)}) collective-permute-start(bf16[64,1024]{1,0:T(8,128)(2,1)S(1)} %fusion.3), channel_id=1, source_target_pairs={{0,6},{1,7},{2,4},{3,5},{4,2},{5,3},{6,0},{7,1},{8,14},{9,15},{10,... | collective-permute-start | bytes 393224 | tf_op jit(solution)/shard_map/ppermute | solution.py:35
  36.9 1.5 %collective-permute-start.11 = (bf16[64,1024]{1,0:T(8,128)(2,1)S(1)}, bf16[64,1024]{1,0:T(8,128)(2,1)S(1)}, u32[]{:S(2)}, u32[]{:S(2)}) collective-permute-start(bf16[64,1024]{1,0:T(8,128)(2,1)S(1)} %fusion.3), channel_id=1, source_target_pairs={{0,2},{1,3},{2,0},{3,1},{4,6},{5,7},{6,4},{7,5},{8,10},{9,11},{10,... | collective-permute-start | bytes 393224 | tf_op jit(solution)/shard_map/ppermute | solution.py:35
  38.4 3.8 %collective-permute-done.13 = bf16[64,1024]{1,0:T(8,128)(2,1)S(1)} collective-permute-done((bf16[64,1024]{1,0:T(8,128)(2,1)S(1)}, bf16[64,1024]{1,0:T(8,128)(2,1)S(1)}, u32[]{:S(2)}, u32[]{:S(2)}) %collective-permute-start.13) | collective-permute-done | bytes 131104 | tf_op jit(solution)/shard_map/ppermute | solution.py:35
  42.2 1.9 %collective-permute-done.12 = bf16[64,1024]{1,0:T(8,128)(2,1)S(1)} collective-permute-done((bf16[64,1024]{1,0:T(8,128)(2,1)S(1)}, bf16[64,1024]{1,0:T(8,128)(2,1)S(1)}, u32[]{:S(2)}, u32[]{:S(2)}) %collective-permute-start.12) | collective-permute-done | bytes 131104 | tf_op jit(solution)/shard_map/ppermute | solution.py:35
  44.4 1.5 %collective-permute-done.15.other_ref = f32[64,1024]{1,0:T(8,128)S(1)} collective-permute-done((f32[64,1024]{1,0:T(8,128)S(1)}, f32[64,1024]{1,0:T(8,128)S(1)}, u32[]{:S(2)}, u32[]{:S(2)}) %collective-permute-start.15) | collective-permute-done | bytes 262176 | tf_op jit(solution)/shard_map/ppermute | solution.py:35
  45.9 1.6 %shard_map.64 = (f32[64,1024]{1,0:T(8,128)S(1)}, f32[64,1024]{1,0:T(8,128)S(1)}) custom-call(f32[64,1024]{1,0:T(8,128)S(1)} %get-tuple-element.64.own_ref, f32[64,1024]{1,0:T(8,128)S(1)} %collective-permute-done.15.other_ref, bf16[640,1024]{1,0:T(8,128)(2,1)S(1)} %get-tuple-element.65.window_ref, bf16[1024,640]{1,0:T(8,128)(2,1)S(1)} %get-tuple-element.54.turned_ref, ...), custom_call_target="tpu_custom_call" | custom-call | tf_op jit(solution)/shard_map/pallas_call | solution.py:550
  47.7 1.4 %collective-permute-done.16 = f32[64,1024]{1,0:T(8,128)S(1)} collective-permute-done((f32[64,1024]{1,0:T(8,128)S(1)}, f32[64,1024]{1,0:T(8,128)S(1)}, u32[]{:S(2)}, u32[]{:S(2)}) %collective-permute-start.16) | collective-permute-done | bytes 262176 | tf_op jit(solution)/shard_map/ppermute | solution.py:35
  49.2 1.5 %collective-permute-start.19 = (bf16[64,1024]{1,0:T(8,128)(2,1)S(1)}, bf16[64,1024]{1,0:T(8,128)(2,1)S(1)}, u32[]{:S(2)}, u32[]{:S(2)}) collective-permute-start(bf16[64,1024]{1,0:T(8,128)(2,1)S(1)} %fusion.5), channel_id=1, source_target_pairs={{0,6},{1,7},{2,4},{3,5},{4,2},{5,3},{6,0},{7,1},{8,14},{9,15},{10,... | collective-permute-start | bytes 393224 | tf_op jit(solution)/shard_map/ppermute | solution.py:35
  51.2 1.5 %collective-permute-start.17 = (bf16[64,1024]{1,0:T(8,128)(2,1)S(1)}, bf16[64,1024]{1,0:T(8,128)(2,1)S(1)}, u32[]{:S(2)}, u32[]{:S(2)}) collective-permute-start(bf16[64,1024]{1,0:T(8,128)(2,1)S(1)} %fusion.5), channel_id=1, source_target_pairs={{0,2},{1,3},{2,0},{3,1},{4,6},{5,7},{6,4},{7,5},{8,10},{9,11},{10,... | collective-permute-start | bytes 393224 | tf_op jit(solution)/shard_map/ppermute | solution.py:35
  52.7 3.8 %collective-permute-done.19 = bf16[64,1024]{1,0:T(8,128)(2,1)S(1)} collective-permute-done((bf16[64,1024]{1,0:T(8,128)(2,1)S(1)}, bf16[64,1024]{1,0:T(8,128)(2,1)S(1)}, u32[]{:S(2)}, u32[]{:S(2)}) %collective-permute-start.19) | collective-permute-done | bytes 131104 | tf_op jit(solution)/shard_map/ppermute | solution.py:35
  56.6 1.9 %collective-permute-done.18 = bf16[64,1024]{1,0:T(8,128)(2,1)S(1)} collective-permute-done((bf16[64,1024]{1,0:T(8,128)(2,1)S(1)}, bf16[64,1024]{1,0:T(8,128)(2,1)S(1)}, u32[]{:S(2)}, u32[]{:S(2)}) %collective-permute-start.18) | collective-permute-done | bytes 131104 | tf_op jit(solution)/shard_map/ppermute | solution.py:35
  58.7 1.5 %collective-permute-done.20.other_ref = f32[64,1024]{1,0:T(8,128)S(1)} collective-permute-done((f32[64,1024]{1,0:T(8,128)S(1)}, f32[64,1024]{1,0:T(8,128)S(1)}, u32[]{:S(2)}, u32[]{:S(2)}) %collective-permute-start.20) | collective-permute-done | bytes 262176 | tf_op jit(solution)/shard_map/ppermute | solution.py:35
  60.2 0.7 %shard_map.65 = (bf16[16,2048]{1,0:T(8,128)(2,1)S(1)}, bf16[16,2048]{1,0:T(8,128)(2,1)S(1)}, bf16[16,2048]{1,0:T(8,128)(2,1)S(1)}, bf16[16,2048]{1,0:T(8,128)(2,1)S(1)}, f32[1,1024]{1,0:T(1,128)S(1)}) custom-call(f32[64,1024]{1,0:T(8,128)S(1)} %add_multiply_fusion.own_ref, f32[64,1024]{1,0:T(8,128)S(1)} %collective-permute-done.20.other_ref, ...), custom_call_target="tpu_custom_call" | custom-call | tf_op jit(solution)/shard_map/pallas_call | solution.py:560
  61.0 1.6 %collective-permute-start.21 = (bf16[16,2048]{1,0:T(8,128)(2,1)S(1)}, bf16[16,2048]{1,0:T(8,128)(2,1)S(1)}, u32[]{:S(2)}, u32[]{:S(2)}) collective-permute-start(bf16[16,2048]{1,0:T(8,128)(2,1)S(1)} %get-tuple-element.71), channel_id=1, source_target_pairs={{0,8},{8,0},{16,24},{24,16},{1,9},{9,1},{17,25},{25,17},{2,10},{10... | collective-permute-start | bytes 196616 | tf_op jit(solution)/shard_map/ppermute | solution.py:35
  62.9 2.5 %collective-permute-start.23 = (bf16[16,2048]{1,0:T(8,128)(2,1)S(1)}, bf16[16,2048]{1,0:T(8,128)(2,1)S(1)}, u32[]{:S(2)}, u32[]{:S(2)}) collective-permute-start(bf16[16,2048]{1,0:T(8,128)(2,1)S(1)} %get-tuple-element.73), channel_id=1, source_target_pairs={{0,24},{8,16},{16,8},{24,0},{1,25},{9,17},{17,9},{25,1},{2,26},{10... | collective-permute-start | bytes 196616 | tf_op jit(solution)/shard_map/ppermute | solution.py:35
  65.4 5.0 %collective-permute-done.22.refs_2_ = bf16[16,2048]{1,0:T(8,128)(2,1)S(1)} collective-permute-done((bf16[16,2048]{1,0:T(8,128)(2,1)S(1)}, bf16[16,2048]{1,0:T(8,128)(2,1)S(1)}, u32[]{:S(2)}, u32[]{:S(2)}) %collective-permute-start.22) | collective-permute-done | bytes 65568 | tf_op jit(solution)/shard_map/ppermute | solution.py:35
  (39 shorter events, 7.1 us)
Async XLA Ops:
  0.6 14.6 %copy-start = (s32[4,1024]{1,0:T(4,128)S(1)}, s32[4,1024]{1,0:T(4,128)}, u32[]{:S(2)}) copy-start(s32[4,1024]{1,0:T(4,128)} %param.7) | copy-start | bytes 49156
  1.9 1.4 %collective-permute-start = (f32[8,1024]{1,0:T(8,128)S(1)}, f32[8,1024]{1,0:T(8,128)S(1)}, u32[]{:S(2)}, u32[]{:S(2)}) collective-permute-start(f32[8,1024]{1,0:T(8,128)S(1)} %get-tuple-element.39.own_ref), channel_id=1, source_target_pairs={{0,1},{1,0},{2,3},{3,2},{4,5},{5,4},{6,7},{7,6},{8,9},{9,8},{10,11... | collective-permute-start | bytes 98312 | tf_op jit(solution)/shard_map/ppermute | solution.py:35
  3.4 5.6 %collective-permute-start.3 = (bf16[8,1024]{1,0:T(8,128)(2,1)S(1)}, bf16[8,1024]{1,0:T(8,128)(2,1)S(1)}, u32[]{:S(2)}, u32[]{:S(2)}) collective-permute-start(bf16[8,1024]{1,0:T(8,128)(2,1)S(1)} %shard_map.60.refs_0_), channel_id=1, source_target_pairs={{0,6},{1,7},{2,4},{3,5},{4,2},{5,3},{6,0},{7,1},{8,14},{9,15},{10,... | collective-permute-start | bytes 49160 | tf_op jit(solution)/shard_map/ppermute | solution.py:35
  7.2 3.7 %collective-permute-start.2 = (bf16[8,1024]{1,0:T(8,128)(2,1)S(1)}, bf16[8,1024]{1,0:T(8,128)(2,1)S(1)}, u32[]{:S(2)}, u32[]{:S(2)}) collective-permute-start(bf16[8,1024]{1,0:T(8,128)(2,1)S(1)} %shard_map.60.refs_0_), channel_id=1, source_target_pairs={{0,4},{1,5},{2,6},{3,7},{4,0},{5,1},{6,2},{7,3},{8,12},{9,13},{10,... | collective-permute-start | bytes 49160 | tf_op jit(solution)/shard_map/ppermute | solution.py:35
  7.7 3.7 %collective-permute-start.1 = (bf16[8,1024]{1,0:T(8,128)(2,1)S(1)}, bf16[8,1024]{1,0:T(8,128)(2,1)S(1)}, u32[]{:S(2)}, u32[]{:S(2)}) collective-permute-start(bf16[8,1024]{1,0:T(8,128)(2,1)S(1)} %shard_map.60.refs_0_), channel_id=1, source_target_pairs={{0,2},{1,3},{2,0},{3,1},{4,6},{5,7},{6,4},{7,5},{8,10},{9,11},{10,... | collective-permute-start | bytes 49160 | tf_op jit(solution)/shard_map/ppermute | solution.py:35
  15.2 1.6 %collective-permute-start.4 = (f32[64,1024]{1,0:T(8,128)S(1)}, f32[64,1024]{1,0:T(8,128)S(1)}, u32[]{:S(2)}, u32[]{:S(2)}) collective-permute-start(f32[64,1024]{1,0:T(8,128)S(1)} %get-tuple-element.44), channel_id=1, source_target_pairs={{0,1},{1,0},{2,3},{3,2},{4,5},{5,4},{6,7},{7,6},{8,9},{9,8},{10,11... | collective-permute-start | bytes 786440 | tf_op jit(solution)/shard_map/ppermute | solution.py:35
  16.8 7.4 %collective-permute-start.7 = (bf16[64,1024]{1,0:T(8,128)(2,1)S(1)}, bf16[64,1024]{1,0:T(8,128)(2,1)S(1)}, u32[]{:S(2)}, u32[]{:S(2)}) collective-permute-start(bf16[64,1024]{1,0:T(8,128)(2,1)S(1)} %add_convert_fusion), channel_id=1, source_target_pairs={{0,6},{1,7},{2,4},{3,5},{4,2},{5,3},{6,0},{7,1},{8,14},{9,15},{10,... | collective-permute-start | bytes 393224 | tf_op jit(solution)/shard_map/ppermute | solution.py:35
  18.4 7.8 %collective-permute-start.6 = (bf16[64,1024]{1,0:T(8,128)(2,1)S(1)}, bf16[64,1024]{1,0:T(8,128)(2,1)S(1)}, u32[]{:S(2)}, u32[]{:S(2)}) collective-permute-start(bf16[64,1024]{1,0:T(8,128)(2,1)S(1)} %add_convert_fusion), channel_id=1, source_target_pairs={{0,4},{1,5},{2,6},{3,7},{4,0},{5,1},{6,2},{7,3},{8,12},{9,13},{10,... | collective-permute-start | bytes 393224 | tf_op jit(solution)/shard_map/ppermute | solution.py:35
  18.5 7.8 %collective-permute-start.5 = (bf16[64,1024]{1,0:T(8,128)(2,1)S(1)}, bf16[64,1024]{1,0:T(8,128)(2,1)S(1)}, u32[]{:S(2)}, u32[]{:S(2)}) collective-permute-start(bf16[64,1024]{1,0:T(8,128)(2,1)S(1)} %add_convert_fusion), channel_id=1, source_target_pairs={{0,2},{1,3},{2,0},{3,1},{4,6},{5,7},{6,4},{7,5},{8,10},{9,11},{10,... | collective-permute-start | bytes 393224 | tf_op jit(solution)/shard_map/ppermute | solution.py:35
  20.4 3.7 %collective-permute-start.8 = (f32[4,1024]{1,0:T(4,128)S(1)}, f32[4,1024]{1,0:T(4,128)S(1)}, u32[]{:S(2)}, u32[]{:S(2)}) collective-permute-start(f32[4,1024]{1,0:T(4,128)S(1)} %convert_element_type.51), channel_id=1, source_target_pairs={{0,8},{8,0},{16,24},{24,16},{1,9},{9,1},{17,25},{25,17},{2,10},{10... | collective-permute-start | bytes 49160 | tf_op jit(solution)/shard_map/ppermute | solution.py:35
  26.3 2.5 %collective-permute-start.9 = (f32[64,1024]{1,0:T(8,128)S(1)}, f32[64,1024]{1,0:T(8,128)S(1)}, u32[]{:S(2)}, u32[]{:S(2)}) collective-permute-start(f32[64,1024]{1,0:T(8,128)S(1)} %broadcast_multiply_fusion.1.own_ref), channel_id=1, source_target_pairs={{0,1},{1,0},{2,3},{3,2},{4,5},{5,4},{6,7},{7,6},{8,9},{9,8},{10,11... | collective-permute-start | bytes 786440 | tf_op jit(solution)/shard_map/ppermute | solution.py:35
  30.5 1.7 %collective-permute-start.10 = (f32[64,1024]{1,0:T(8,128)S(1)}, f32[64,1024]{1,0:T(8,128)S(1)}, u32[]{:S(2)}, u32[]{:S(2)}) collective-permute-start(f32[64,1024]{1,0:T(8,128)S(1)} %get-tuple-element.60), channel_id=1, source_target_pairs={{0,1},{1,0},{2,3},{3,2},{4,5},{5,4},{6,7},{7,6},{8,9},{9,8},{10,11... | collective-permute-start | bytes 786440 | tf_op jit(solution)/shard_map/ppermute | solution.py:35
  32.2 6.1 %collective-permute-start.14 = (f32[8,1024]{1,0:T(8,128)S(1)}, f32[8,1024]{1,0:T(8,128)S(1)}, u32[]{:S(2)}, u32[]{:S(2)}) collective-permute-start(f32[8,1024]{1,0:T(8,128)S(1)} %pad_maximum_fusion.1), channel_id=1, source_target_pairs={{0,16},{8,24},{16,0},{24,8},{1,17},{9,25},{17,1},{25,9},{2,18},{10... | collective-permute-start | bytes 98312 | tf_op jit(solution)/shard_map/ppermute | solution.py:35
  34.9 7.3 %collective-permute-start.13 = (bf16[64,1024]{1,0:T(8,128)(2,1)S(1)}, bf16[64,1024]{1,0:T(8,128)(2,1)S(1)}, u32[]{:S(2)}, u32[]{:S(2)}) collective-permute-start(bf16[64,1024]{1,0:T(8,128)(2,1)S(1)} %fusion.3), channel_id=1, source_target_pairs={{0,6},{1,7},{2,4},{3,5},{4,2},{5,3},{6,0},{7,1},{8,14},{9,15},{10,... | collective-permute-start | bytes 393224 | tf_op jit(solution)/shard_map/ppermute | solution.py:35
  36.3 7.8 %collective-permute-start.12 = (bf16[64,1024]{1,0:T(8,128)(2,1)S(1)}, bf16[64,1024]{1,0:T(8,128)(2,1)S(1)}, u32[]{:S(2)}, u32[]{:S(2)}) collective-permute-start(bf16[64,1024]{1,0:T(8,128)(2,1)S(1)} %fusion.3), channel_id=1, source_target_pairs={{0,4},{1,5},{2,6},{3,7},{4,0},{5,1},{6,2},{7,3},{8,12},{9,13},{10,... | collective-permute-start | bytes 393224 | tf_op jit(solution)/shard_map/ppermute | solution.py:35
  36.9 7.2 %collective-permute-start.11 = (bf16[64,1024]{1,0:T(8,128)(2,1)S(1)}, bf16[64,1024]{1,0:T(8,128)(2,1)S(1)}, u32[]{:S(2)}, u32[]{:S(2)}) collective-permute-start(bf16[64,1024]{1,0:T(8,128)(2,1)S(1)} %fusion.3), channel_id=1, source_target_pairs={{0,2},{1,3},{2,0},{3,1},{4,6},{5,7},{6,4},{7,5},{8,10},{9,11},{10,... | collective-permute-start | bytes 393224 | tf_op jit(solution)/shard_map/ppermute | solution.py:35
  44.3 1.6 %collective-permute-start.15 = (f32[64,1024]{1,0:T(8,128)S(1)}, f32[64,1024]{1,0:T(8,128)S(1)}, u32[]{:S(2)}, u32[]{:S(2)}) collective-permute-start(f32[64,1024]{1,0:T(8,128)S(1)} %get-tuple-element.64.own_ref), channel_id=1, source_target_pairs={{0,1},{1,0},{2,3},{3,2},{4,5},{5,4},{6,7},{7,6},{8,9},{9,8},{10,11... | collective-permute-start | bytes 786440 | tf_op jit(solution)/shard_map/ppermute | solution.py:35
  47.5 1.6 %collective-permute-start.16 = (f32[64,1024]{1,0:T(8,128)S(1)}, f32[64,1024]{1,0:T(8,128)S(1)}, u32[]{:S(2)}, u32[]{:S(2)}) collective-permute-start(f32[64,1024]{1,0:T(8,128)S(1)} %get-tuple-element.68), channel_id=1, source_target_pairs={{0,1},{1,0},{2,3},{3,2},{4,5},{5,4},{6,7},{7,6},{8,9},{9,8},{10,11... | collective-permute-start | bytes 786440 | tf_op jit(solution)/shard_map/ppermute | solution.py:35
  49.2 7.4 %collective-permute-start.19 = (bf16[64,1024]{1,0:T(8,128)(2,1)S(1)}, bf16[64,1024]{1,0:T(8,128)(2,1)S(1)}, u32[]{:S(2)}, u32[]{:S(2)}) collective-permute-start(bf16[64,1024]{1,0:T(8,128)(2,1)S(1)} %fusion.5), channel_id=1, source_target_pairs={{0,6},{1,7},{2,4},{3,5},{4,2},{5,3},{6,0},{7,1},{8,14},{9,15},{10,... | collective-permute-start | bytes 393224 | tf_op jit(solution)/shard_map/ppermute | solution.py:35
  50.6 7.9 %collective-permute-start.18 = (bf16[64,1024]{1,0:T(8,128)(2,1)S(1)}, bf16[64,1024]{1,0:T(8,128)(2,1)S(1)}, u32[]{:S(2)}, u32[]{:S(2)}) collective-permute-start(bf16[64,1024]{1,0:T(8,128)(2,1)S(1)} %fusion.5), channel_id=1, source_target_pairs={{0,4},{1,5},{2,6},{3,7},{4,0},{5,1},{6,2},{7,3},{8,12},{9,13},{10,... | collective-permute-start | bytes 393224 | tf_op jit(solution)/shard_map/ppermute | solution.py:35
  51.2 7.3 %collective-permute-start.17 = (bf16[64,1024]{1,0:T(8,128)(2,1)S(1)}, bf16[64,1024]{1,0:T(8,128)(2,1)S(1)}, u32[]{:S(2)}, u32[]{:S(2)}) collective-permute-start(bf16[64,1024]{1,0:T(8,128)(2,1)S(1)} %fusion.5), channel_id=1, source_target_pairs={{0,2},{1,3},{2,0},{3,1},{4,6},{5,7},{6,4},{7,5},{8,10},{9,11},{10,... | collective-permute-start | bytes 393224 | tf_op jit(solution)/shard_map/ppermute | solution.py:35
  58.6 1.6 %collective-permute-start.20 = (f32[64,1024]{1,0:T(8,128)S(1)}, f32[64,1024]{1,0:T(8,128)S(1)}, u32[]{:S(2)}, u32[]{:S(2)}) collective-permute-start(f32[64,1024]{1,0:T(8,128)S(1)} %add_multiply_fusion.own_ref), channel_id=1, source_target_pairs={{0,1},{1,0},{2,3},{3,2},{4,5},{5,4},{6,7},{7,6},{8,9},{9,8},{10,11... | collective-permute-start | bytes 786440 | tf_op jit(solution)/shard_map/ppermute | solution.py:35
  61.0 4.5 %collective-permute-start.21 = (bf16[16,2048]{1,0:T(8,128)(2,1)S(1)}, bf16[16,2048]{1,0:T(8,128)(2,1)S(1)}, u32[]{:S(2)}, u32[]{:S(2)}) collective-permute-start(bf16[16,2048]{1,0:T(8,128)(2,1)S(1)} %get-tuple-element.71), channel_id=1, source_target_pairs={{0,8},{8,0},{16,24},{24,16},{1,9},{9,1},{17,25},{25,17},{2,10},{10... | collective-permute-start | bytes 196616 | tf_op jit(solution)/shard_map/ppermute | solution.py:35
  62.6 7.8 %collective-permute-start.22 = (bf16[16,2048]{1,0:T(8,128)(2,1)S(1)}, bf16[16,2048]{1,0:T(8,128)(2,1)S(1)}, u32[]{:S(2)}, u32[]{:S(2)}) collective-permute-start(bf16[16,2048]{1,0:T(8,128)(2,1)S(1)} %get-tuple-element.72), channel_id=1, source_target_pairs={{0,16},{8,24},{16,0},{24,8},{1,17},{9,25},{17,1},{25,9},{2,18},{10... | collective-permute-start | bytes 196616 | tf_op jit(solution)/shard_map/ppermute | solution.py:35
  62.9 7.5 %collective-permute-start.23 = (bf16[16,2048]{1,0:T(8,128)(2,1)S(1)}, bf16[16,2048]{1,0:T(8,128)(2,1)S(1)}, u32[]{:S(2)}, u32[]{:S(2)}) collective-permute-start(bf16[16,2048]{1,0:T(8,128)(2,1)S(1)} %get-tuple-element.73), channel_id=1, source_target_pairs={{0,24},{8,16},{16,8},{24,0},{1,25},{9,17},{17,9},{25,1},{2,26},{10... | collective-permute-start | bytes 196616 | tf_op jit(solution)/shard_map/ppermute | solution.py:35
  70.5 1.3 %collective-permute-start.24 = (f32[16,1024]{1,0:T(8,128)S(1)}, f32[16,1024]{1,0:T(8,128)S(1)}, u32[]{:S(2)}, u32[]{:S(2)}) collective-permute-start(f32[16,1024]{1,0:T(8,128)S(1)} %shard_map.66.own_ref), channel_id=1, source_target_pairs={{0,1},{1,0},{2,3},{3,2},{4,5},{5,4},{6,7},{7,6},{8,9},{9,8},{10,11... | collective-permute-start | bytes 196616 | tf_op jit(solution)/shard_map/ppermute | solution.py:35
